TPU v7x, 32 devices: a whole 2x2x4 slice. The times are simulated.
32 devices in a mesh: dp: 8 (over y, x, core), mp: 4 (over z).
Axes of the slice: x: 2, y: 2, z: 4, core: 2. Of those that a mesh axis runs over, the one named last changes fastest.
Arguments:
- vq_in: bfloat16 [16, 768, 32], P('dp'), may hold values from -6 to 6
- codes: int32 [16, 768], P('dp'), may hold values from 0 to 4095
- segment: int32 [16, 768], P('dp'), may hold values from 0 to 3, never falling along the last dimension, each value on 1 to 680 neighbouring positions
- live: int32 [16, 768], P('dp'), may hold values from 0 to 1
- labels: int32 [16, 4], P('dp'), may hold values from 0 to 999
- level_weight: int32 [10], replicated, may hold values from 1 to 4
- qkv_w: float32 [3, 1024, 1024], P(None, 'dp', 'mp'), may hold values from -0.1875 to 0.1875
- proj_w: float32 [1024, 1024], P('mp', 'dp'), may hold values from -0.5 to 0.5
- fc1_w: float32 [1024, 4096], P('dp', 'mp'), may hold values from -0.1875 to 0.1875
- fc2_w: float32 [4096, 1024], P('mp', 'dp'), may hold values from -0.09375 to 0.09375
- head_w: float32 [1024, 4096], P('dp', 'mp'), may hold values from -0.5625 to 0.5625
- ada_w: float32 [1024, 8192], P('dp'), may hold values from -0.1875 to 0.1875
- tables: float32 [1042, 1024], P(None, 'dp'), may hold values from -6 to 6
- head_scale: float32 [16], P('mp'), may hold values from 2.3 to 3
- d_stats: float32 [6, 1024], P(None, 'dp'), may hold values from 4.967054e-09 to 7.947286e-08
- qkv_stat: float32 [3, 1024], P(None, 'mp'), may hold values from 1.9868216e-08 to 7.947286e-08
- proj_stat: float32 [1024], P('mp'), may hold values from 1.9868216e-08 to 7.947286e-08
- fc1_stat: float32 [4096], P('mp'), may hold values from 1.9868216e-08 to 7.947286e-08
- fc2_stat: float32 [4096], P('mp'), may hold values from 1.9868216e-08 to 7.947286e-08
- head_stat: float32 [4096], P('mp'), may hold values from 4.967054e-09 to 1.9868216e-08
- ada_stat: float32 [8192], replicated, may hold values from 1.9868216e-08 to 7.947286e-08
- tables_v: float32 [1042, 1024], P(None, 'dp'), may hold values from 1.9868216e-08 to 3.1789145e-07
- scale_v: float32 [16], P('mp'), may hold values from 1.6276041e-07 to 8.138021e-07
Outputs:
- loss_sum: float32 [], replicated
- weight_sum: float32 [], replicated
- qkv_grad: float32 [3, 1024, 1024], P(None, 'dp', 'mp')
- proj_grad: float32 [1024, 1024], P('mp', 'dp')
- fc1_grad: float32 [1024, 4096], P('dp', 'mp')
- fc2_grad: float32 [4096, 1024], P('mp', 'dp')
- head_grad: float32 [1024, 4096], P('dp', 'mp')
- ada_grad: float32 [1024, 8192], P('dp')
- tables_grad: float32 [1042, 1024], P(None, 'dp')
- scale_grad: float32 [16], P('mp')
- d_stats_new: float32 [6, 1024], P(None, 'dp')
- qkv_stat_new: float32 [3, 1024], P(None, 'mp')
- proj_stat_new: float32 [1024], P('mp')
- fc1_stat_new: float32 [4096], P('mp')
- fc2_stat_new: float32 [4096], P('mp')
- head_stat_new: float32 [4096], P('mp')
- ada_stat_new: float32 [8192], replicated
- tables_v_new: float32 [1042, 1024], P(None, 'dp')
- scale_v_new: float32 [16], P('mp')
- qkv_new: float32 [3, 1024, 1024], P(None, 'dp', 'mp')
- proj_new: float32 [1024, 1024], P('mp', 'dp')
- fc1_new: float32 [1024, 4096], P('dp', 'mp')
- fc2_new: float32 [4096, 1024], P('mp', 'dp')
- head_new: float32 [1024, 4096], P('dp', 'mp')
- ada_new: float32 [1024, 8192], P('dp')
- tables_new: float32 [1042, 1024], P(None, 'dp')
- scale_new: float32 [16], P('mp')
Inputs may be any that keep to these rules, and one draw needn't show every extreme that they name: `segment`: each packed row holds 4 items in order, each of 1 to 680 tokens, one of exactly 680.
All inputs are finite; a program needn't handle non-finite values.
Results may differ from a plain program's by a relative error of at most 0.0085.
The roundings to bfloat16 on the way count: a program that leaves them out, or rounds other values in their place, can miss the bound.
Values may be sent and summed in bfloat16 or wider, within the bound.
No kernel may reach another device: no remote copies, remote signals or barrier semaphores. Data moves between devices by JAX's collectives and lax.ppermute only.
A program may use at most 320 MiB of HBM per device.

v0:
```python
import math

import jax
import jax.numpy as jnp
from jax import lax
from jax.sharding import PartitionSpec as P

STEP = 8


level_starts = (1, 5, 14, 30, 55, 91, 155, 255, 424)
eps_norm = 1e-06
eps_one = 1e-30
eps_two = 0.001
rate_step = 0.3
clip_rms = 1.0
highest = lax.Precision.HIGHEST
low_type = jnp.bfloat16
full_type = jnp.float32


def joined(part, axis, combine):
    gathered = jax.tree.map(lambda a: lax.all_gather(a, axis), part)

    def take(source):
        return jax.tree.map(lambda a: lax.dynamic_index_in_dim(a, source, 0, False), gathered)

    return lax.fori_loop(
        1, lax.axis_size(axis), lambda source, state: combine(state, take(source)), take(0)
    )


def plain_dot(left_side, right_side):
    return jnp.dot(left_side, right_side, preferred_element_type=full_type)


def over_rows(left_side, right_side):
    return lax.dot_general(
        left_side, right_side, (((0,), (0,)), ((), ())), preferred_element_type=full_type
    )


def exact_over_rows(left_side, right_side):
    return lax.dot_general(
        left_side,
        right_side,
        (((0,), (0,)), ((), ())),
        precision=highest,
        preferred_element_type=full_type,
    )


def against_rows(left_side, right_side):
    return lax.dot_general(
        left_side, right_side, (((1,), (1,)), ((), ())), preferred_element_type=full_type
    )


def layer_norm(values):
    centered = values - jnp.mean(values, -1, keepdims=True)
    return centered * lax.rsqrt(jnp.mean(centered * centered, -1, keepdims=True) + eps_norm)


def norm_back(values, incoming):
    unused, pull_back = jax.vjp(layer_norm, values)
    return pull_back(incoming)[0]


def unit_rows(values, gain):
    return values * lax.rsqrt(jnp.mean(values * values, -1, keepdims=True) + eps_norm) * gain


def query_norm(values, log_scale):
    return unit_rows(values, (jnp.exp(log_scale) / math.sqrt(values.shape[-1]))[:, None])


def key_norm(values):
    return unit_rows(values, 1.0 / math.sqrt(values.shape[-1]))


def gelu_tanh(values):
    return jax.nn.gelu(values, approximate=True)


def layout(seg_row, count):
    seg_hot = seg_row[:, None] == jnp.arange(count, dtype=jnp.int32)[None, :]
    counts = jnp.sum(seg_hot.astype(jnp.int32), 0)
    starts = jnp.cumsum(counts) - counts
    first_pos = jnp.sum(jnp.where(seg_hot, starts[None, :], 0), 1)
    within = jnp.arange(seg_row.shape[0], dtype=jnp.int32) - first_pos
    level_row = jnp.sum(
        (within[:, None] >= jnp.array(level_starts, dtype=jnp.int32)[None, :]).astype(jnp.int32), 1
    )
    return (seg_hot.astype(full_type), level_row)


def allowed_mask(seg_row, level_row, live_row):
    length = seg_row.shape[0]
    same_item = seg_row[:, None] == seg_row[None, :]
    earlier = level_row[None, :] <= level_row[:, None]
    diagonal = jnp.arange(length)[:, None] == jnp.arange(length)[None, :]
    usable = (live_row[None, :] > 0) | diagonal
    return same_item & earlier & usable


def row_scores(query_row, key_row, seg_row, level_row, live_row):
    scores = jnp.einsum("thd,shd->hts", query_row, key_row, preferred_element_type=full_type)
    return jnp.where(allowed_mask(seg_row, level_row, live_row)[None], scores, -1e30)


def attend(row_data):
    query_row, key_row, value_row, seg_row, level_row, live_row = row_data
    scores = row_scores(query_row, key_row, seg_row, level_row, live_row)
    row_peak = jnp.max(scores, -1, keepdims=True)
    exponent = jnp.exp(scores - row_peak)
    row_total = jnp.sum(exponent, -1, keepdims=True)
    att_low = (exponent / row_total).astype(low_type)
    mixed = jnp.einsum("hts,shd->thd", att_low, value_row, preferred_element_type=full_type)
    return (mixed.astype(low_type), (row_peak + jnp.log(row_total))[..., 0])


def attend_back(row_data):
    query_row, key_row, value_row, seg_row, level_row, live_row, log_row, dmix_row = row_data
    scores = row_scores(query_row, key_row, seg_row, level_row, live_row)
    attention = jnp.exp(scores - log_row[..., None])
    att_low = attention.astype(low_type)
    d_value = jnp.einsum("hts,thd->shd", att_low, dmix_row, preferred_element_type=full_type)
    d_att = jnp.einsum("thd,shd->hts", dmix_row, value_row, preferred_element_type=full_type)
    d_scores = (attention * (d_att - jnp.sum(attention * d_att, -1, keepdims=True))).astype(
        low_type
    )
    d_query = jnp.einsum("hts,shd->thd", d_scores, key_row, preferred_element_type=full_type)
    d_key = jnp.einsum("hts,thd->shd", d_scores, query_row, preferred_element_type=full_type)
    return (d_query, d_key, d_value)


def combine_stats(left_part, right_part):
    maximum = jnp.maximum(left_part[0], right_part[0])
    total = left_part[1] * jnp.exp(left_part[0] - maximum) + right_part[1] * jnp.exp(
        right_part[0] - maximum
    )
    return (maximum, total, left_part[2] + right_part[2])


def qkv_view(array_in):
    return jnp.transpose(array_in, (1, 0, 2)).reshape(array_in.shape[1], -1)


def qkv_unview(array_in):
    return jnp.transpose(array_in.reshape(array_in.shape[0], 3, -1), (1, 0, 2))


def body(
    vq_in,
    codes,
    segment,
    live,
    labels,
    level_weight,
    qkv_w,
    proj_w,
    fc1_w,
    fc2_w,
    head_w,
    ada_w,
    tables,
    head_scale,
    d_stats,
    qkv_stat,
    proj_stat,
    fc1_stat,
    fc2_stat,
    head_stat,
    ada_stat,
    tables_v,
    scale_v,
):
    dp_count = lax.axis_size("dp")
    mp_count = lax.axis_size("mp")
    row_count, seq_len, code_dim = vq_in.shape
    item_count = labels.shape[1]
    level_count = level_weight.shape[0]
    width = tables.shape[1] * dp_count
    heads_here = head_scale.shape[0]
    head_dim = qkv_w.shape[2] // heads_here
    token_count = row_count * seq_len
    class_count = tables.shape[0] - code_dim - level_count
    qkv_low, proj_low, fc1_low, fc2_low, head_low, ada_low, table_low = (
        lax.all_gather(qkv_w.astype(low_type), "dp", axis=1, tiled=True),
        lax.all_gather(proj_w.astype(low_type), "dp", axis=1, tiled=True),
        lax.all_gather(fc1_w.astype(low_type), "dp", axis=0, tiled=True),
        lax.all_gather(fc2_w.astype(low_type), "dp", axis=1, tiled=True),
        lax.all_gather(head_w.astype(low_type), "dp", axis=0, tiled=True),
        lax.all_gather(ada_w.astype(low_type), "dp", axis=0, tiled=True),
        lax.all_gather(tables.astype(low_type), "dp", axis=1, tiled=True),
    )
    seg_hot, level_rows = jax.vmap(lambda seg_row: layout(seg_row, item_count))(segment)
    level_match = (
        level_rows.reshape(token_count)[:, None]
        == jnp.arange(level_count, dtype=jnp.int32)[None, :]
    )
    weight_tok = (
        live.reshape(token_count) * jnp.sum(jnp.where(level_match, level_weight[None, :], 0), 1)
    ).astype(full_type)
    weight_sum = lax.psum(jnp.sum(weight_tok), "dp")
    vq_flat = vq_in.reshape(token_count, code_dim)
    stream_zero = plain_dot(vq_flat, table_low[:code_dim]) + plain_dot(
        level_match.astype(low_type), table_low[code_dim : code_dim + level_count]
    )
    class_hot = labels.reshape(-1)[:, None] == jnp.arange(class_count, dtype=jnp.int32)[None, :]
    class_vec = plain_dot(class_hot.astype(low_type), table_low[code_dim + level_count :])
    activated = jax.nn.silu(class_vec).astype(low_type)
    mod_items = plain_dot(activated, ada_low).reshape(row_count, item_count, -1)
    modulation = jnp.einsum("rtc,rcm->rtm", seg_hot, mod_items, precision=highest).reshape(
        token_count, -1
    )
    shift_one, scale_one, gate_one, shift_two, scale_two, gate_two, shift_out, scale_out = (
        jnp.split(modulation, 8, axis=1)
    )

    def to_rows(array_in):
        return array_in.reshape(row_count, seq_len, heads_here, head_dim)

    normed_one = layer_norm(stream_zero)
    input_one = (normed_one * (1.0 + scale_one) + shift_one).astype(low_type)
    qkv_out = jnp.einsum("td,cde->cte", input_one, qkv_low, preferred_element_type=full_type)
    query = qkv_out[0].reshape(token_count, heads_here, head_dim)
    keyed = qkv_out[1].reshape(token_count, heads_here, head_dim)
    query_low = query_norm(query, head_scale).astype(low_type)
    key_low = key_norm(keyed).astype(low_type)
    value_low = qkv_out[2].reshape(token_count, heads_here, head_dim).astype(low_type)
    mixed_rows, log_rows = lax.map(
        attend,
        (to_rows(query_low), to_rows(key_low), to_rows(value_low), segment, level_rows, live),
    )
    mixed_low = mixed_rows.reshape(token_count, heads_here * head_dim)
    branch_one = lax.psum(plain_dot(mixed_low, proj_low).astype(jnp.bfloat16), "mp").astype(
        jnp.float32
    )
    stream_one = stream_zero + gate_one * branch_one
    normed_two = layer_norm(stream_one)
    input_two = (normed_two * (1.0 + scale_two) + shift_two).astype(low_type)
    hidden = plain_dot(input_two, fc1_low)
    act_two = gelu_tanh(hidden).astype(low_type)
    branch_two = lax.psum(plain_dot(act_two, fc2_low), "mp")
    stream_two = stream_one + gate_two * branch_two
    normed_out = layer_norm(stream_two)
    input_out = (normed_out * (1.0 + scale_out) + shift_out).astype(low_type)
    logits = plain_dot(input_out, head_low)
    vocab_here = logits.shape[1]
    shifted_codes = codes.reshape(token_count) - lax.axis_index("mp") * vocab_here
    target_hot = shifted_codes[:, None] == jnp.arange(vocab_here, dtype=jnp.int32)[None, :]
    local_peak = jnp.max(logits, 1)
    local_total = jnp.sum(jnp.exp(logits - local_peak[:, None]), 1)
    local_pick = jnp.sum(jnp.where(target_hot, logits, 0.0), 1)
    peak_all, total_all, picked_all = joined(
        (local_peak, local_total, local_pick), "mp", combine_stats
    )
    log_total = peak_all + jnp.log(total_all)
    loss_here = jnp.sum(weight_tok * (log_total - picked_all))
    coefficient = weight_tok / weight_sum
    d_logits = (
        coefficient[:, None] * (jnp.exp(logits - log_total[:, None]) - target_hot.astype(full_type))
    ).astype(low_type)
    head_part = over_rows(input_out, d_logits)
    d_out = lax.psum(against_rows(d_logits, head_low), "mp")
    d_scale_out = d_out * normed_out
    d_two = norm_back(stream_two, d_out * (1.0 + scale_out))
    d_branch_two = (d_two * gate_two).astype(low_type)
    d_gate_two = d_two * branch_two
    fc2_part = over_rows(act_two, d_branch_two)
    d_act_two = against_rows(d_branch_two, fc2_low)
    unused, gelu_pull = jax.vjp(gelu_tanh, hidden)
    d_hidden = gelu_pull(d_act_two)[0].astype(low_type)
    fc1_part = over_rows(input_two, d_hidden)
    d_in_two = lax.psum(against_rows(d_hidden, fc1_low), "mp")
    d_scale_two = d_in_two * normed_two
    d_one = d_two + norm_back(stream_one, d_in_two * (1.0 + scale_two))
    d_branch_one = (d_one * gate_one).astype(low_type)
    d_gate_one = d_one * branch_one
    proj_part = over_rows(mixed_low, d_branch_one)
    d_mixed = against_rows(d_branch_one, proj_low).astype(low_type)
    d_query_rows, d_key_rows, d_value_rows = lax.map(
        attend_back,
        (
            to_rows(query_low),
            to_rows(key_low),
            to_rows(value_low),
            segment,
            level_rows,
            live,
            log_rows,
            to_rows(d_mixed),
        ),
    )
    unused, query_pull = jax.vjp(query_norm, query, head_scale)
    d_query, scale_part = query_pull(d_query_rows.reshape(token_count, heads_here, head_dim))
    unused, key_pull = jax.vjp(key_norm, keyed)
    d_key = key_pull(d_key_rows.reshape(token_count, heads_here, head_dim))[0]
    d_qkv = jnp.stack(
        [
            d_query.reshape(token_count, -1),
            d_key.reshape(token_count, -1),
            d_value_rows.reshape(token_count, -1),
        ]
    ).astype(low_type)
    qkv_part = jnp.einsum("td,cte->cde", input_one, d_qkv, preferred_element_type=full_type)
    d_in_one = lax.psum(
        jnp.einsum("cte,cde->td", d_qkv, qkv_low, preferred_element_type=full_type).astype(
            jnp.bfloat16
        ),
        "mp",
    ).astype(jnp.float32)
    d_scale_one = d_in_one * normed_one
    d_zero = d_one + norm_back(stream_zero, d_in_one * (1.0 + scale_one))
    d_mods = jnp.concatenate(
        [d_in_one, d_scale_one, d_gate_one, d_in_two, d_scale_two, d_gate_two, d_out, d_scale_out],
        1,
    )
    d_items = jnp.einsum(
        "rtc,rtm->rcm", seg_hot, d_mods.reshape(row_count, seq_len, -1), precision=highest
    ).reshape(row_count * item_count, -1)
    d_act = jnp.einsum(
        "im,dm->id", d_items, ada_low, precision=highest, preferred_element_type=full_type
    )
    unused, silu_pull = jax.vjp(jax.nn.silu, class_vec)
    d_class = silu_pull(d_act)[0]
    table_part = jnp.concatenate(
        [
            exact_over_rows(vq_flat.astype(full_type), d_zero),
            exact_over_rows(level_match.astype(full_type), d_zero),
            exact_over_rows(class_hot.astype(full_type), d_class),
        ],
        0,
    )
    qkv_grad, proj_grad, fc1_grad, fc2_grad, head_grad, tables_grad = (
        lax.psum_scatter(qkv_part, "dp", scatter_dimension=1, tiled=True),
        lax.psum_scatter(proj_part, "dp", scatter_dimension=1, tiled=True),
        lax.psum_scatter(fc1_part, "dp", scatter_dimension=0, tiled=True),
        lax.psum_scatter(fc2_part, "dp", scatter_dimension=1, tiled=True),
        lax.psum_scatter(head_part, "dp", scatter_dimension=0, tiled=True),
        lax.psum_scatter(table_part, "dp", scatter_dimension=1, tiled=True),
    )
    ada_part = exact_over_rows(activated.astype(full_type), d_items)
    ada_grad = lax.psum_scatter(ada_part, "dp", scatter_dimension=0, tiled=True)
    decay_rate = 1.0 - STEP ** (-0.8)
    gradients = [qkv_view(qkv_grad), proj_grad.T, fc1_grad, fc2_grad.T, head_grad, ada_grad]
    masters = [qkv_view(qkv_w), proj_w.T, fc1_w, fc2_w.T, head_w, ada_w]
    col_old = [qkv_stat.reshape(-1), proj_stat, fc1_stat, fc2_stat, head_stat, ada_stat]
    wide_full = [
        3 * width,
        width,
        fc1_w.shape[1] * mp_count,
        fc2_w.shape[0] * mp_count,
        head_w.shape[1] * mp_count,
        ada_w.shape[1],
    ]
    squares = [gradient * gradient + eps_one for gradient in gradients]
    row_parts = [jnp.sum(square, 1) for square in squares]
    col_parts = [jnp.sum(square, 0) for square in squares]
    row_summed = lax.psum(
        (row_parts[0], row_parts[1], row_parts[2], row_parts[3], row_parts[4]), "mp"
    )
    row_totals = list(row_summed) + [row_parts[5]]
    row_new = [
        decay_rate * d_stats[position]
        + (1.0 - decay_rate) * row_totals[position] / wide_full[position]
        for position in range(6)
    ]
    row_local = jnp.stack([jnp.sum(vector) for vector in row_new])
    col_summed = lax.psum(
        (
            col_parts[0],
            col_parts[1],
            col_parts[2],
            col_parts[3],
            col_parts[4],
            col_parts[5],
            row_local,
            scale_part,
            loss_here,
        ),
        "dp",
    )
    col_new = [
        decay_rate * col_old[position] + (1.0 - decay_rate) * col_summed[position] / width
        for position in range(6)
    ]
    row_means = col_summed[6] / width
    scale_grad = col_summed[7]
    loss_sum = col_summed[8]
    raw_steps = [
        gradients[position]
        * lax.rsqrt(row_new[position][:, None] * col_new[position][None, :] / row_means[position])
        for position in range(6)
    ]
    tables_v_new = decay_rate * tables_v + (1.0 - decay_rate) * (
        tables_grad * tables_grad + eps_one
    )
    scale_v_new = decay_rate * scale_v + (1.0 - decay_rate) * (scale_grad * scale_grad + eps_one)
    raw_steps = raw_steps + [
        tables_grad * lax.rsqrt(tables_v_new),
        scale_grad * lax.rsqrt(scale_v_new),
    ]
    olds = masters + [tables, head_scale]
    shares = [1.0, 1.0, 1.0, 1.0, 1.0, 1.0 / mp_count, 1.0 / mp_count, 1.0 / dp_count]
    update_local = jnp.stack(
        [
            jnp.sum(raw_steps[position] * raw_steps[position]) * shares[position]
            for position in range(8)
        ]
    )
    weight_local = jnp.stack(
        [jnp.sum(olds[position] * olds[position]) * shares[position] for position in range(8)]
    )
    update_all, weight_all = lax.psum((update_local, weight_local), ("dp", "mp"))
    news = []
    for position in range(8):
        entries = olds[position].size * dp_count * mp_count * shares[position]
        ratio = jnp.sqrt(update_all[position] / entries) / clip_rms
        spread = jnp.maximum(eps_two, jnp.sqrt(weight_all[position] / entries))
        news.append(
            olds[position] - rate_step * spread * raw_steps[position] / jnp.maximum(1.0, ratio)
        )
    d_stats_new = jnp.stack(row_new)
    return (
        loss_sum,
        weight_sum,
        qkv_grad,
        proj_grad,
        fc1_grad,
        fc2_grad,
        head_grad,
        ada_grad,
        tables_grad,
        scale_grad,
        d_stats_new,
        col_new[0].reshape(3, -1),
        col_new[1],
        col_new[2],
        col_new[3],
        col_new[4],
        col_new[5],
        tables_v_new,
        scale_v_new,
        qkv_unview(news[0]),
        news[1].T,
        news[2],
        news[3].T,
        news[4],
        news[5],
        news[6],
        news[7],
    )


def solution(mesh):
    return jax.shard_map(
        body,
        mesh=mesh,
        in_specs=(
            P("dp", None, None),
            P("dp", None),
            P("dp", None),
            P("dp", None),
            P("dp", None),
            P(),
            P(None, "dp", "mp"),
            P("mp", "dp"),
            P("dp", "mp"),
            P("mp", "dp"),
            P("dp", "mp"),
            P("dp", None),
            P(None, "dp"),
            P("mp"),
            P(None, "dp"),
            P(None, "mp"),
            P("mp"),
            P("mp"),
            P("mp"),
            P("mp"),
            P(),
            P(None, "dp"),
            P("mp"),
        ),
        out_specs=(
            P(),
            P(),
            P(None, "dp", "mp"),
            P("mp", "dp"),
            P("dp", "mp"),
            P("mp", "dp"),
            P("dp", "mp"),
            P("dp", None),
            P(None, "dp"),
            P("mp"),
            P(None, "dp"),
            P(None, "mp"),
            P("mp"),
            P("mp"),
            P("mp"),
            P("mp"),
            P(),
            P(None, "dp"),
            P("mp"),
            P(None, "dp", "mp"),
            P("mp", "dp"),
            P("dp", "mp"),
            P("mp", "dp"),
            P("dp", "mp"),
            P("dp", None),
            P(None, "dp"),
            P("mp"),
        ),
        check_vma=False,
    )
```

profile of v0, /device:TPU:0, one launch (start us, length us, event | category | flops | bytes accessed | tf_op | source)
XLA Modules:
  0.0 2169.9 jit_solution(15399791563829577058)
XLA Ops:
  19.0 13.2 all_gather.42
  32.2 10.2 all-gather.13.cloned.1.call-done
  49.4 85.4 %all-gather.15.cloned.1.call-done = bf16[1024,8192]{1,0:T(8,128)(2,1)} async-done(((bf16[128,8192]{1,0:T(8,128)(2,1)}), bf16[1024,8192]{1,0:T(8,128)(2,1)}) %all-gather.15.cloned.1.call-update) | async-done | bytes 16777232 | tf_op jit(solution)/shard_map/all_gather | solution.py:194
  142.9 24.4 %fusion.107 = f32[2,768,8192]{2,1,0:T(8,128)} fusion(f32[2,4,8192]{2,1,0:T(4,128)S(1)} %reshape.727, s32[2,768]{1,0:T(2,128)S(1)} %copy-done.54), kind=kOutput, calls=%fused_computation.230 | convolution fusion | flops 603985920 | bytes 50599936 | tf_op jit(solution)/shard_map/rtc,rcm->rtm/dot_general | solution.py:214
  167.3 33.6 %fusion.139 = (f32[1536,1024]{1,0:T(8,128)}, f32[1536,1024]{1,0:T(8,128)}, f32[1536,1024]{1,0:T(8,128)}, f32[1536,1024]{1,0:T(8,128)}, f32[1536,1024]{1,0:T(8,12...) fusion(f32[1536,8192]{1,0:T(8,128)} %bitcast.312), kind=kLoop, calls=%fused_computation.307 | loop fusion | bytes 100663296 | tf_op jit(solution)/shard_map/split | solution.py:218
  245.0 16.6 while.45
  290.8 98.3 %all-reduce.9.cloned.1.call-done = bf16[1536,1024]{0,1:T(8,128)(2,1)} async-done(((bf16[1536,1024]{0,1:T(8,128)(2,1)}), bf16[1536,1024]{0,1:T(8,128)(2,1)}) %all-reduce.9.cloned.1.call-update) | async-done | bytes 3145744 | tf_op jit(solution)/shard_map/psum | solution.py:237
  407.7 10.6 all-gather.19.cloned.1.call-done
  426.9 21.9 %all-gather.21.cloned.1.call-done = bf16[1024,1024]{1,0:T(8,128)(2,1)} async-done(((bf16[1024,128]{1,0:T(8,128)(2,1)}), bf16[1024,1024]{1,0:T(8,128)(2,1)}) %all-gather.21.cloned.1.call-update) | async-done | bytes 2097168 | tf_op jit(solution)/shard_map/all_gather | solution.py:192
  462.1 14.1 psum.157
  496.1 185.9 %all-reduce.11.cloned.1.call-done = f32[1536,1024]{0,1:T(8,128)} async-done(((f32[1536,1024]{0,1:T(8,128)}), f32[1536,1024]{0,1:T(8,128)}) %all-reduce.11.cloned.1.call-update) | async-done | bytes 6291472 | tf_op jit(solution)/shard_map/psum | solution.py:245
  722.0 13.2 all-gather.4
  735.3 13.1 all-gather.5
  748.4 13.1 all-gather.3
  772.2 223.0 %all-reduce.13.cloned.1.call-done = f32[1536,1024]{0,1:T(8,128)} async-done(((f32[1536,1024]{0,1:T(8,128)}), f32[1536,1024]{0,1:T(8,128)}) %all-reduce.13.cloned.1.call-update) | async-done | bytes 6291472 | tf_op jit(solution)/shard_map/psum | solution.py:266
  1030.2 221.2 %all-reduce.15.cloned.1.call-done = f32[1536,1024]{0,1:T(8,128)} async-done(((f32[1536,1024]{0,1:T(8,128)}), f32[1536,1024]{0,1:T(8,128)}) %all-reduce.15.cloned.1.call-update) | async-done | bytes 6291472 | tf_op jit(solution)/shard_map/psum | solution.py:276
  1267.1 12.4 multiply_convert_fusion.1
  1290.5 56.2 %while.47 = (s32[]{:T(128)}, f32[2,768,4,64]{1,3,2,0:T(8,128)}, f32[2,768,4,64]{1,3,2,0:T(8,128)}, bf16[2,768,4,64]{1,3,2,0:T(8,128)(2,1)}, bf16[2,768,4,64]{1,3...) while((s32[]{:T(128)}, f32[2,768,4,64]{1,3,2,0:T(8,128)}, ...), condition=%wide.region_36.37_spmd, body=%wide.region_34.36_spmd.sunk | while | flops 1541797632 | bytes 144424752 | solution.py:283
  1301.3 10.8 multiply_convert_fusion.14
  1329.2 10.8 multiply_convert_fusion.14
  1412.3 82.9 %all-reduce.17.cloned.1.call-done = bf16[1536,1024]{0,1:T(8,128)(2,1)} async-done(((bf16[1536,1024]{0,1:T(8,128)(2,1)}), bf16[1536,1024]{0,1:T(8,128)(2,1)}) %all-reduce.17.cloned.1.call-update) | async-done | bytes 3145744 | tf_op jit(solution)/shard_map/psum | solution.py:308
  1544.1 49.6 %copy.244 = f32[1536,8192]{1,0:T(8,128)} copy(f32[1536,8192]{0,1:T(8,128)} %multiply_dynamic-update-slice_fusion) | data formatting | bytes 100663296 | tf_op jit(solution)/shard_map/reshape | solution.py:321
  1593.7 22.6 %fusion.106 = f32[2,4,8192]{2,1,0:T(4,128)} fusion(f32[2,768,8192]{2,1,0:T(8,128)} %bitcast.307, s32[2,768]{1,0:T(2,128)S(1)} %get-tuple-element.1075), kind=kOutput, calls=%fused_computation.229 | convolution fusion | flops 603985920 | bytes 50599936 | tf_op jit(solution)/shard_map/rtc,rtm->rcm/dot_general | solution.py:320
  1630.7 17.1 fusion.149
  1658.7 11.8 concatenate.7
  1670.6 17.3 fusion.121
  1708.0 42.0 %reduce-scatter.8.cloned.1.call-done = f32[3,128,256]{1,2,0:T(8,128)} async-done(((f32[3,1024,256]{1,2,0:T(8,128)}), f32[3,128,256]{1,2,0:T(8,128)}) %reduce-scatter.8.cloned.1.call-update) | async-done | bytes 393232 | tf_op jit(solution)/shard_map/reduce_scatter | solution.py:337
  1753.9 12.2 all-reduce.2
  1766.1 41.4 %reduce-scatter.20.cloned.1.call-done = f32[1042,128]{1,0:T(8,128)} async-done(((f32[1042,1024]{1,0:T(8,128)}), f32[1042,128]{1,0:T(8,128)}) %reduce-scatter.20.cloned.1.call-update) | async-done | bytes 533520 | tf_op jit(solution)/shard_map/reduce_scatter | solution.py:342
  1810.1 206.6 %reduce-scatter.18.cloned.1.call-done = f32[128,8192]{1,0:T(8,128)} async-done(((f32[1024,8192]{1,0:T(8,128)}), f32[128,8192]{1,0:T(8,128)}) %reduce-scatter.18.cloned.1.call-update) | async-done | bytes 4194320 | tf_op jit(solution)/shard_map/reduce_scatter | solution.py:345
  2027.4 24.7 %all-reduce.1 = (f32[]{:T(128)}, f32[4]{0:T(128)}, f32[768]{0:T(1024)}, f32[256]{0:T(256)}, f32[1024]{0:T(1024)}, /*index=5*/f32[1024]{0:T(1024)}, f32[1024]{0:T(1024)}, f32[8192]{0:T(1024)}, f32[6]{0:T(128)}) all-reduce(f32[]{:T(128)} %get-tuple-element.629, f32[4]{0:T(128)} %get-tuple-element.699, ...), channel_id=1, replica_groups=mesh['dp'=8,'mp'=4] {'dp'}, use_global_device_ids=true, to_apply=%region_25.26 | all-reduce | flops 12299 | bytes 98392 | tf_op jit(solution)/shard_map/psum | solution.py:371
  2082.2 39.6 %all-reduce = (f32[8]{0:T(128)}, f32[8]{0:T(128)}) all-reduce(f32[8]{0:T(128)} %stack.129, f32[8]{0:T(128)} %stack.113), channel_id=1, replica_groups=mesh['dp'=8,'mp'=4] {'dp','mp'}, use_global_device_ids=true, to_apply=%region_98.99 | all-reduce | flops 16 | bytes 128 | tf_op jit(solution)/shard_map/psum | solution.py:416
  (588 shorter events, 555.5 us)
Async XLA Ops:
  7.3 35.1 %all-gather.13.cloned.1.call-start = ((), (), s32[]{:S(2)}) async-start(), calls=%async_computation.7 | async-start | bytes 2414592 | tf_op jit(solution)/shard_map/all_gather | solution.py:195
  10.1 124.7 %all-gather.15.cloned.1.call-start = ((), (), s32[]{:S(2)}) async-start(), calls=%async_computation.8 | async-start | bytes 18874368 | tf_op jit(solution)/shard_map/all_gather | solution.py:194
  16.5 206.3 %all-gather.17.cloned.1.call-start = ((), (), s32[]{:S(2)}) async-start(), calls=%async_computation.9 | async-start | bytes 1769472 | tf_op jit(solution)/shard_map/all_gather | solution.py:189
  17.6 371.5 %all-reduce.9.cloned.1.call-start = ((), (), s32[]{:S(2)}) async-start(), calls=%async_computation.10 | async-start | bytes 6291456 | tf_op jit(solution)/shard_map/psum | solution.py:237
  17.7 225.0 %copy-start.114 = (f32[4]{0:T(128)}, f32[4]{0:T(128)S(1)}, u32[]{:S(2)}) copy-start(f32[4]{0:T(128)S(1)} %exponential_multiply_fusion) | copy-start | bytes 52
  267.9 150.4 %all-gather.19.cloned.1.call-start = ((), (), s32[]{:S(2)}) async-start(), calls=%async_computation.11 | async-start | bytes 2359296 | tf_op jit(solution)/shard_map/all_gather | solution.py:191
  269.3 179.5 %all-gather.21.cloned.1.call-start = ((), (), s32[]{:S(2)}) async-start(), calls=%async_computation.12 | async-start | bytes 2359296 | tf_op jit(solution)/shard_map/all_gather | solution.py:192
  270.8 411.1 %all-reduce.11.cloned.1.call-start = ((), (), s32[]{:S(2)}) async-start(), calls=%async_computation.13 | async-start | bytes 12582912 | tf_op jit(solution)/shard_map/psum | solution.py:245
  396.5 863.2 %copy-start.77 = (f32[1536]{0:T(1024)}, f32[1536]{0:T(1024)S(1)}, u32[]{:S(2)}) copy-start(f32[1536]{0:T(1024)S(1)} %broadcast_multiply_fusion.2) | copy-start | bytes 18436
  399.0 860.7 %copy-start.93 = (f32[1536]{0:T(1024)}, f32[1536]{0:T(1024)S(1)}, u32[]{:S(2)}) copy-start(f32[1536]{0:T(1024)S(1)} %fusion.116) | copy-start | bytes 18436
  458.9 252.3 %all-gather.23.cloned.1.call-start = ((), (), s32[]{:S(2)}) async-start(), calls=%async_computation.14 | async-start | bytes 2359296 | tf_op jit(solution)/shard_map/all_gather | solution.py:193
  461.3 533.9 %all-reduce.13.cloned.1.call-start = ((), (), s32[]{:S(2)}) async-start(), calls=%async_computation.15 | async-start | bytes 12582912 | tf_op jit(solution)/shard_map/psum | solution.py:266
  476.2 287.2 %copy-start.106 = (s32[1536]{0:T(1024)}, s32[1536]{0:T(1024)S(1)}, u32[]{:S(2)}) copy-start(s32[1536]{0:T(1024)S(1)} %sub.184) | copy-start | bytes 18436
  690.8 312.8 %copy-start.79 = (f32[1536]{0:T(1024)}, f32[1536]{0:T(1024)S(1)}, u32[]{:S(2)}) copy-start(f32[1536]{0:T(1024)S(1)} %broadcast_multiply_fusion.1) | copy-start | bytes 18436
  693.4 310.2 %copy-start.95 = (f32[1536]{0:T(1024)}, f32[1536]{0:T(1024)S(1)}, u32[]{:S(2)}) copy-start(f32[1536]{0:T(1024)S(1)} %fusion.117) | copy-start | bytes 18436
  772.2 479.2 %all-reduce.15.cloned.1.call-start = ((), (), s32[]{:S(2)}) async-start(), calls=%async_computation.16 | async-start | bytes 12582912 | tf_op jit(solution)/shard_map/psum | solution.py:276
  1009.4 257.7 %copy-start.89 = (f32[1536]{0:T(1024)}, f32[1536]{0:T(1024)S(1)}, u32[]{:S(2)}) copy-start(f32[1536]{0:T(1024)S(1)} %negate_multiply_fusion.2) | copy-start | bytes 18436
  1029.4 465.8 %all-reduce.17.cloned.1.call-start = ((), (), s32[]{:S(2)}) async-start(), calls=%async_computation.22 | async-start | bytes 6291456 | tf_op jit(solution)/shard_map/psum | solution.py:308
  1375.0 317.8 %reduce-scatter.16.cloned.1.call-start = ((), (), s32[]{:S(2)}) async-start(), calls=%async_computation.21 | async-start | bytes 4718592 | tf_op jit(solution)/shard_map/reduce_scatter | solution.py:341
  1383.3 317.4 %reduce-scatter.14.cloned.1.call-start = ((), (), s32[]{:S(2)}) async-start(), calls=%async_computation.20 | async-start | bytes 4718592 | tf_op jit(solution)/shard_map/reduce_scatter | solution.py:340
  1392.9 311.6 %reduce-scatter.12.cloned.1.call-start = ((), (), s32[]{:S(2)}) async-start(), calls=%async_computation.19 | async-start | bytes 4718592 | tf_op jit(solution)/shard_map/reduce_scatter | solution.py:339
  1401.4 305.0 %reduce-scatter.10.cloned.1.call-start = ((), (), s32[]{:S(2)}) async-start(), calls=%async_computation.18 | async-start | bytes 1179648 | tf_op jit(solution)/shard_map/reduce_scatter | solution.py:338
  1405.5 344.5 %reduce-scatter.8.cloned.1.call-start = ((), (), s32[]{:S(2)}) async-start(), calls=%async_computation.17 | async-start | bytes 3538944 | tf_op jit(solution)/shard_map/reduce_scatter | solution.py:337
  1411.8 395.7 %reduce-scatter.20.cloned.1.call-start = ((), (), s32[]{:S(2)}) async-start(), calls=%async_computation.24 | async-start | bytes 4829184 | tf_op jit(solution)/shard_map/reduce_scatter | solution.py:342
  1670.5 346.3 %reduce-scatter.18.cloned.1.call-start = ((), (), s32[]{:S(2)}) async-start(), calls=%async_computation.23 | async-start | bytes 37748736 | tf_op jit(solution)/shard_map/reduce_scatter | solution.py:345
  1704.5 366.2 %copy-start.34 = (f32[128,1024]{1,0:T(8,128)S(1)}, f32[128,1024]{1,0:T(8,128)}, u32[]{:S(2)}) copy-start(f32[128,1024]{1,0:T(8,128)} %reduce-scatter.12.cloned.1.call-done) | copy-start | bytes 1572868
  1706.4 362.4 %copy-start.53 = (f32[256,128]{1,0:T(8,128)S(1)}, f32[256,128]{1,0:T(8,128)}, u32[]{:S(2)}) copy-start(f32[256,128]{1,0:T(8,128)} %reduce-scatter.10.cloned.1.call-done) | copy-start | bytes 393220
  1708.0 364.8 %copy-start.25 = (f32[1024,128]{0,1:T(8,128)S(1)}, f32[1024,128]{0,1:T(8,128)}, u32[]{:S(2)}) copy-start(f32[1024,128]{0,1:T(8,128)} %reduce-scatter.14.cloned.1.call-done) | copy-start | bytes 1572868
  1750.0 316.6 %copy-start.30 = (f32[3,128,256]{1,2,0:T(8,128)S(1)}, f32[3,128,256]{1,2,0:T(8,128)}, u32[]{:S(2)}) copy-start(f32[3,128,256]{1,2,0:T(8,128)} %reduce-scatter.8.cloned.1.call-done) | copy-start | bytes 1179652
  1751.9 323.1 %copy-start.33 = (f32[128,1024]{1,0:T(8,128)S(1)}, f32[128,1024]{1,0:T(8,128)}, u32[]{:S(2)}) copy-start(f32[128,1024]{1,0:T(8,128)} %reduce-scatter.16.cloned.1.call-done) | copy-start | bytes 1572868
  1766.1 369.6 %copy-start.36 = (f32[3,128,256]{1,2,0:T(8,128)S(1)}, f32[3,128,256]{1,2,0:T(8,128)}, u32[]{:S(2)}) copy-start(f32[3,128,256]{1,2,0:T(8,128)} %copy-done.35) | copy-start | bytes 1179652
  1809.5 352.2 %copy-start.42 = (f32[1042,128]{1,0:T(8,128)}, f32[1042,128]{1,0:T(8,128)S(1)}, u32[]{:S(2)}) copy-start(f32[1042,128]{1,0:T(8,128)S(1)} %get-tuple-element.608) | copy-start | bytes 1600516
  (139 other events, 2020.3 us)
Sparse Core Ops, SparseCore 0:
  10.6 31.8 all-gather.12
  44.9 89.8 all-gather.14
  137.2 25.9 all-gather.16
  268.0 121.0 all-reduce.8
  391.4 26.8 all-gather.18
  420.6 28.1 all-gather.20
  459.0 222.8 all-reduce.10
  684.4 26.8 all-gather.22
  772.3 222.8 all-reduce.12
  1029.5 221.8 all-reduce.14
  1375.1 120.0 all-reduce.16
  1499.0 50.3 reduce-scatter.15
  1553.0 51.3 reduce-scatter.13
  1608.7 51.3 reduce-scatter.11
  1664.0 36.0 reduce-scatter.9
  1703.7 46.2 reduce-scatter.7
  1753.9 53.5 reduce-scatter.19
  1811.5 205.2 reduce-scatter.17
where the time goes:
time: 2180 us; the launch traced here: 2170 us
  waiting for transfers between devices  1240 us (57%)
  other arithmetic  262 us (12%)
  local copies, waits for them, and re-layouts  246 us (11%)
  matrix products  246 us (11%)
  blocking collectives  143 us (7%)
  between operations  31 us (1%)
    psum x1, waiting for transfers between devices, body(): d_out = lax.psum(against_rows(d_logits, head_low), 'mp')  223 us
    psum x1, waiting for transfers between devices, body(): d_in_two = lax.psum(against_rows(d_hidden, fc1_low), 'mp')  221 us
    reduce_scatter x1, waiting for transfers between devices, body(): ada_grad = lax.psum_scatter(ada_part, 'dp', scatter_dimension=0, tiled=True)  207 us
    psum x1, waiting for transfers between devices, body(): branch_two = lax.psum(plain_dot(act_two, fc2_low), 'mp')  186 us
    psum x1, waiting for transfers between devices, body(): lax.psum(plain_dot(mixed_low, proj_low).astype(jnp.bfloat16), 'mp')  98.3 us
    unnamed x297, local copies, waits for them, and re-layouts  92.4 us
    all_gather x1, waiting for transfers between devices, body(): lax.all_gather(ada_w.astype(low_type), 'dp', axis=0, tiled=True)  85.4 us
    psum x1, waiting for transfers between devices, body(): lax.psum(jnp.einsum('cte,cde->td', d_qkv, qkv_low, preferred_element_type...  82.9 us
  transfers between devices with their start and end apart: 18, of which 13 were waited for; matrix products, arithmetic and copies ran while one was open for 20% of the time, Pallas kernels for 0%

commit v1 on v0

v1 whole, which is shorter than its diff:
```python
import functools
import math

import jax
import jax.numpy as jnp
from jax import lax
from jax.experimental import pallas as pl
from jax.experimental.pallas import tpu as pltpu
from jax.sharding import Mesh, PartitionSpec as P

STEP = 8
level_starts = (1, 5, 14, 30, 55, 91, 155, 255, 424)
eps_norm = 1e-06
eps_one = 1e-30
eps_two = 0.001
rate_step = 0.3
clip_rms = 1.0
low_type = jnp.bfloat16
full_type = jnp.float32
high = lax.Precision.HIGH
highest = lax.Precision.HIGHEST
swap_pairs = ((0, 1), (1, 0))
busy_us = {
    "row_layout": 2, "enter": 5, "enter_first": 6, "attend": 11, "onward": 4, "feed": 9, "head": 6, "merge": 2,
    "head_back": 5, "back": 5, "feed_back": 7, "attend_back": 16, "old_stats": 4, "row_stats": 3,
    "column_stats": 5, "finish": 2, "head_grad": 6, "feed_grad": 12, "first_grad": 6,
}
DP = ("g", "c")
MP = ("h", "l")


def cost(name):
    return pl.CostEstimate(flops=busy_us[name] * 10**9, transcendentals=0, bytes_accessed=busy_us[name] * 10**6)


def low(a):
    return a.astype(low_type)


def full(a):
    return a.astype(full_type)


def dot_nn(a, b, precision=None):
    return jnp.dot(a, b, preferred_element_type=full_type, precision=precision)


def dot_nt(a, b, precision=None):
    return lax.dot_general(
        a, b, (((1,), (1,)), ((), ())), preferred_element_type=full_type, precision=precision
    )


def dot_tn(a, b, precision=None):
    return lax.dot_general(
        a, b, (((0,), (0,)), ((), ())), preferred_element_type=full_type, precision=precision
    )


def over_c(a):
    return lax.ppermute(a, "c", swap_pairs)


def over_l(a):
    return lax.ppermute(a, "l", swap_pairs)


def over_h(a):
    return lax.ppermute(a, "h", swap_pairs)


def over_cl(a):
    return lax.ppermute(a, ("c", "l"), [(i, i ^ 3) for i in range(4)])


def over_g(a, k):
    return lax.ppermute(a, "g", [(i, i ^ k) for i in range(lax.axis_size("g"))])


def ordered(flag, mine, other, axis):
    return jnp.where(
        flag == 0,
        jnp.concatenate([mine, other], axis),
        jnp.concatenate([other, mine], axis),
    )


def gather_g(a):
    count = lax.axis_size("g")
    if count != 4:
        return lax.all_gather(a, "g", axis=0, tiled=True)
    here = lax.axis_index("g")
    out = jnp.zeros((4,) + a.shape, a.dtype)
    for k in range(4):
        piece = a if k == 0 else over_g(a, k)
        out = lax.dynamic_update_index_in_dim(out, piece, here ^ k, 0)
    return out.reshape((4 * a.shape[0],) + a.shape[1:])


def scatter_g(a):
    count = lax.axis_size("g")
    if count != 4:
        return full(lax.psum_scatter(a, "g", scatter_dimension=0, tiled=True))
    here = lax.axis_index("g")
    blocks = a.reshape((4, a.shape[0] // 4) + a.shape[1:])
    total = full(lax.dynamic_index_in_dim(blocks, here, 0, False))
    for k in range(1, 4):
        total = total + full(over_g(lax.dynamic_index_in_dim(blocks, here ^ k, 0, False), k))
    return total


def tie(a, *others):
    return lax.optimization_barrier((a,) + others)[0]


def centre(values):
    centered = values - jnp.mean(values, -1, keepdims=True)
    scale = lax.rsqrt(jnp.mean(centered * centered, -1, keepdims=True) + eps_norm)
    return centered * scale, scale


def centre_back(normed, scale, incoming):
    return (
        incoming
        - jnp.mean(incoming, -1, keepdims=True)
        - normed * jnp.mean(incoming * normed, -1, keepdims=True)
    ) * scale


def gelu_parts(values):
    root = math.sqrt(2.0 / math.pi)
    square = values * values
    bent = jnp.tanh(values * (root + (root * 0.044715) * square))
    half = 0.5 + 0.5 * bent
    slope = half + values * (0.5 - 0.5 * (bent * bent)) * (root + (root * 3.0 * 0.044715) * square)
    return values * half, slope


def split_parts(a, count):
    parts = []
    for _ in range(count):
        parts.append(low(a))
        a = a - full(parts[-1])
    return parts


def item_parts(vectors):
    return jnp.concatenate(split_parts(vectors, 3) + [jnp.zeros(vectors.shape, low_type)], 0)


def item_sums(hot, values):
    upper, lower = split_parts(values, 2)
    return (dot_tn(hot, upper) + dot_tn(hot, lower))[:8]


def whole(shape):
    return pl.BlockSpec(shape, lambda i: (0,) * len(shape), pipeline_mode=pl.Buffered(1))


def tiled(tile, columns):
    return pl.BlockSpec((tile, columns), lambda i: (i, 0))


def call(kernel, grid, in_specs, out_specs, out_shape, scratch, name):
    return pl.pallas_call(
        kernel,
        grid=grid,
        in_specs=in_specs,
        out_specs=out_specs,
        out_shape=[jax.ShapeDtypeStruct(shape, dtype) for shape, dtype in out_shape],
        scratch_shapes=scratch,
        compiler_params=pltpu.CompilerParams(vmem_limit_bytes=48 * 2**20),
        cost_estimate=cost(name),
        name=name,
    )


def rows_kernel(lw_ref, seg_ref, live_ref, place_ref, weight_ref, sum_ref):
    seg, live = seg_ref[...], live_ref[...]
    at = lax.broadcasted_iota(jnp.int32, seg.shape, 1)
    first = jnp.zeros_like(seg)
    for item in range(1, 4):
        count = jnp.sum(full(jnp.where(seg < item, 1, 0)), 1, keepdims=True).astype(jnp.int32)
        first = jnp.where(seg == item, count, first)
    within = at - first
    level = jnp.zeros_like(seg)
    for start in level_starts:
        level = level + jnp.where(within >= start, 1, 0)
    weight = jnp.zeros_like(seg)
    for position in range(lw_ref.shape[0]):
        weight = jnp.where(level == position, lw_ref[position], weight)
    weight = weight * live
    place_ref[...] = seg * 16 + level
    weight_ref[...] = weight
    each = jnp.sum(full(weight), 1, keepdims=True)
    sum_ref[...] = jnp.sum(each, 0, keepdims=True).astype(jnp.int32)


def row_layout(level_weight, segment, live):
    shape = segment.shape
    return pl.pallas_call(
        rows_kernel,
        in_specs=[pl.BlockSpec(memory_space=pltpu.SMEM)] + [pl.BlockSpec(memory_space=pltpu.VMEM)] * 2,
        out_shape=[
            jax.ShapeDtypeStruct(shape, jnp.int32),
            jax.ShapeDtypeStruct(shape, jnp.int32),
            jax.ShapeDtypeStruct((1, 1), jnp.int32),
        ],
        cost_estimate=cost("row_layout"),
        name="row_layout",
    )(level_weight, segment, live)


def enter_tile(feat_ref, table_ref, hot_ref, w, in_ref, qkv_ref, stream_ref, parts_s):
    stream = dot_nn(feat_ref[...], table_ref[...])

    @pl.when(pl.program_id(0) == 0)
    def _():
        stream_ref[...] = stream[: stream_ref.shape[0]]

    normed, _ = centre(stream)
    hot = hot_ref[...]
    given = low(normed * (1.0 + dot_nn(hot, parts_s[1])) + dot_nn(hot, parts_s[0]))
    in_ref[...] = given
    qkv_ref[...] = dot_nn(given, w)


def enter_parts(mod_ref, parts_s):
    parts_s[0] = item_parts(mod_ref[0])
    parts_s[1] = item_parts(mod_ref[1])


def enter_kernel(feat_ref, table_ref, hot_ref, mod_ref, w_ref, in_ref, qkv_ref, stream_ref, parts_s):
    @pl.when(pl.program_id(0) == 0)
    def _():
        enter_parts(mod_ref, parts_s)

    enter_tile(feat_ref, table_ref, hot_ref, w_ref[...], in_ref, qkv_ref, stream_ref, parts_s)


def enter(feats, table, hot, mods, w):
    n, k = feats.shape
    width, columns = w.shape
    tile = n // 2
    return call(
        enter_kernel,
        (2,),
        [tiled(tile, k), whole((k, width)), tiled(tile, 16), whole(mods.shape), whole(w.shape)],
        [tiled(tile, width), tiled(tile, columns), fixed((tile // 2, width))],
        [((n, width), low_type), ((n, columns), full_type), ((tile // 2, width), full_type)],
        [pltpu.VMEM((2, 16, width), low_type)],
        "enter",
    )(feats, table, hot, mods, w)


def enter_first_kernel(
    at_ref, feat_ref, table_ref, hot_ref, mod_ref, a_ref, b_ref, c_ref, d_ref, in_ref, qkv_ref, stream_ref,
    w_ref, p_ref, parts_s
):
    @pl.when(pl.program_id(0) == 0)
    def _():
        enter_parts(mod_ref, parts_s)
        for k, ref in enumerate((a_ref, b_ref, c_ref, d_ref)):
            rows = ref.shape[2]
            start = pl.multiple_of(jnp.bitwise_xor(at_ref[0], k) * rows, rows)
            for j in range(2):
                for c in range(3):
                    w_ref[pl.ds(start, rows), (2 * c + j) * 128 : (2 * c + j + 1) * 128] = ref[j, c]
                p_ref[pl.ds(start, rows), j * 128 : (j + 1) * 128] = ref[j, 3]

    enter_tile(feat_ref, table_ref, hot_ref, w_ref[...], in_ref, qkv_ref, stream_ref, parts_s)


def enter_first(here, feats, table, hot, mods, pieces):
    n, k = feats.shape
    width = table.shape[1]
    columns = 768
    tile = n // 2
    shape = pieces[0].shape
    return call(
        enter_first_kernel,
        (n // tile,),
        [pl.BlockSpec(memory_space=pltpu.SMEM), tiled(tile, k), whole((k, width)), tiled(tile, 16), whole(mods.shape)]
        + [whole(shape)] * 4,
        [tiled(tile, width), tiled(tile, columns), fixed((tile // 2, width))]
        + [fixed((width, columns)), fixed((width, columns // 3))],
        [((n, width), low_type), ((n, columns), full_type), ((tile // 2, width), full_type)]
        + [((width, columns), low_type), ((width, columns // 3), low_type)],
        [pltpu.VMEM((2, 16, width), low_type)],
        "enter_first",
    )(here[None], feats, table, hot, mods, *pieces)


def onward_kernel(a_ref, b_ref, c_ref, x_ref, hot_ref, mod_ref, br_ref, y_ref, in_ref, parts_s, *, picks):
    @pl.when(pl.program_id(0) == 0)
    def _():
        for k, pick in enumerate(picks):
            parts_s[k] = item_parts(mod_ref[pick])

    branch = full(a_ref[...]) + full(b_ref[...]) + full(c_ref[...])
    br_ref[...] = branch
    hot = hot_ref[...]
    stream = x_ref[...] + dot_nn(hot, parts_s[0]) * branch
    y_ref[...] = stream
    normed, _ = centre(stream)
    in_ref[...] = low(normed * (1.0 + dot_nn(hot, parts_s[2])) + dot_nn(hot, parts_s[1]))


def onward(parts, stream, hot, mods, picks):
    n, width = parts[2].shape
    tile = n // 2
    return call(
        functools.partial(onward_kernel, picks=picks),
        (n // tile,),
        [tiled(tile, width)] * 4 + [tiled(tile, 16), whole(mods.shape)],
        [tiled(tile, width)] * 3,
        [((n, width), full_type), ((n, width), full_type), ((n, width), low_type)],
        [pltpu.VMEM((3, 16, width), low_type)],
        "onward",
    )(*parts, stream, hot, mods)


def back_kernel(*refs, gated, carried, picks):
    refs = list(refs)
    a_ref, b_ref, c_ref, x_ref, hot_ref, mod_ref = refs[:6]
    del refs[:6]
    res_ref = refs.pop(0) if carried else None
    br_ref = refs.pop(0) if gated else None
    feat_ref = None if gated else refs.pop(0)
    res_out = refs.pop(0) if gated else None
    d_ref = refs.pop(0) if gated else None
    items_ref = refs.pop(0)
    lead_ref = None if gated else refs.pop(0)
    parts_s = refs.pop(0)

    @pl.when(pl.program_id(0) == 0)
    def _():
        for k, pick in enumerate(picks):
            parts_s[k] = item_parts(mod_ref[pick])
        items_ref[...] = jnp.zeros_like(items_ref)
        if not gated:
            lead_ref[...] = jnp.zeros_like(lead_ref)

    hot = hot_ref[...]
    incoming = full(a_ref[...]) + full(b_ref[...]) + full(c_ref[...])
    normed, scale = centre(x_ref[...])
    items_ref[0] += item_sums(hot, incoming)
    items_ref[1] += item_sums(hot, incoming * normed)
    res = centre_back(normed, scale, incoming * (1.0 + dot_nn(hot, parts_s[0])))
    if carried:
        res = res + res_ref[...]
    if gated:
        res_out[...] = res
        items_ref[2] += item_sums(hot, res * br_ref[...])
        d_ref[...] = low(res * dot_nn(hot, parts_s[1]))
    else:
        upper, lower = split_parts(res, 2)
        feats = feat_ref[...]
        lead_ref[...] += dot_tn(feats, upper) + dot_tn(feats, lower)


def back(parts, stream, hot, mods, picks, carried, branch, feats):
    n, width = parts[2].shape
    tile = n // 2
    gated, has = branch is not None, carried is not None
    extra = ([carried] if has else []) + ([branch] if gated else [feats])
    specs = [tiled(tile, width)] * 4 + [tiled(tile, 16), whole(mods.shape)]
    specs += [tiled(tile, a.shape[1]) for a in extra]
    count = 3 if gated else 2
    out_specs, out_shape = [], []
    if gated:
        out_specs += [tiled(tile, width)] * 2
        out_shape += [((n, width), full_type), ((n, width), low_type)]
    out_specs.append(fixed((count, 8, width)))
    out_shape.append(((count, 8, width), full_type))
    if not gated:
        out_specs.append(fixed((feats.shape[1], width)))
        out_shape.append(((feats.shape[1], width), full_type))
    return call(
        functools.partial(back_kernel, gated=gated, carried=has, picks=picks),
        (n // tile,),
        specs,
        out_specs,
        out_shape,
        [pltpu.VMEM((2, 16, width), low_type)],
        "back",
    )(*parts, stream, hot, mods, *extra)


def either(a_ref, b_ref, c_ref, d_ref):
    top = jnp.concatenate([a_ref[...], b_ref[...]], 0)
    return jnp.where(pl.program_id(0) == 0, top, jnp.concatenate([c_ref[...], d_ref[...]], 0))


def put(value, top_ref, bottom_ref):
    @pl.when(pl.program_id(0) == 0)
    def _():
        top_ref[...] = value

    @pl.when(pl.program_id(0) == 1)
    def _():
        bottom_ref[...] = value


def fixed(shape):
    return pl.BlockSpec(shape, lambda i: (0,) * len(shape))


def column_half(shape, number):
    return pl.BlockSpec(
        shape[:2] + (shape[2] // 2,), lambda i: (0, 0, number), pipeline_mode=pl.Buffered(1)
    )


def feed_kernel(a_ref, b_ref, c_ref, d_ref, one_ref, two_ref, row_ref, act_ref, slope_ref, top_ref, bottom_ref):
    given = either(a_ref, b_ref, c_ref, d_ref)
    row_ref[...] = given
    units = one_ref.shape[2]
    total = None
    for h in range(2):
        at = slice(h * units, (h + 1) * units)
        act, slope = gelu_parts(dot_nn(given, one_ref[h]))
        act = low(act)
        act_ref[:, at] = act
        slope_ref[:, at] = slope
        part = dot_nt(act, two_ref[h])
        total = part if total is None else total + part
    put(low(total), top_ref, bottom_ref)


def feed(pieces, both):
    tile, width = 2 * pieces[0].shape[0], pieces[0].shape[1]
    units = both.shape[2]
    return call(
        feed_kernel,
        (2,),
        [whole(pieces[0].shape)] * 4 + [column_half(both.shape, k) for k in range(2)],
        [tiled(tile, width), tiled(tile, units), tiled(tile, units), fixed((tile, width)), fixed((tile, width))],
        [((2 * tile, width), low_type), ((2 * tile, units), low_type), ((2 * tile, units), full_type)]
        + [((tile, width), low_type)] * 2,
        [],
        "feed",
    )(*pieces, both, both)


def feed_back_kernel(a_ref, b_ref, c_ref, d_ref, slope_ref, one_ref, two_ref, row_ref, dh_ref, top_ref, bottom_ref):
    given = either(a_ref, b_ref, c_ref, d_ref)
    row_ref[...] = given
    units = one_ref.shape[2]
    total = None
    for h in range(2):
        at = slice(h * units, (h + 1) * units)
        d_hidden = low(dot_nn(given, two_ref[h]) * slope_ref[:, at])
        dh_ref[:, at] = d_hidden
        part = dot_nt(d_hidden, one_ref[h])
        total = part if total is None else total + part
    put(low(total), top_ref, bottom_ref)


def feed_back(pieces, slope, both):
    tile, width = 2 * pieces[0].shape[0], pieces[0].shape[1]
    units = both.shape[2]
    return call(
        feed_back_kernel,
        (2,),
        [whole(pieces[0].shape)] * 4 + [tiled(tile, units)] + [column_half(both.shape, k) for k in range(2)],
        [tiled(tile, width), tiled(tile, units), fixed((tile, width)), fixed((tile, width))],
        [((2 * tile, width), low_type), ((2 * tile, units), low_type)] + [((tile, width), low_type)] * 2,
        [],
        "feed_back",
    )(*pieces, slope, both, both)


def head_kernel(a_ref, b_ref, c_ref, d_ref, w_ref, code_ref, column_ref, row_ref, logit_ref, stat_ref):
    given = either(a_ref, b_ref, c_ref, d_ref)
    row_ref[...] = given
    logits = jnp.concatenate([dot_nn(given, w_ref[h]) for h in range(2)], 1)
    logit_ref[...] = logits
    peak = jnp.max(logits, 1, keepdims=True)
    total = jnp.sum(jnp.exp(logits - peak), 1, keepdims=True)
    picked = jnp.sum(jnp.where(code_ref[...] == column_ref[...], logits, 0.0), 1, keepdims=True)
    lane = lax.broadcasted_iota(jnp.int32, (logits.shape[0], 128), 1)
    turned = jnp.where(lane == 0, peak, jnp.where(lane == 1, total, picked)).T
    stat_ref[...] = turned[0:8, :]


def head(pieces, w, code, column):
    tile, width = 2 * pieces[0].shape[0], pieces[0].shape[1]
    units = 2 * w.shape[2]
    return call(
        head_kernel,
        (2,),
        [whole(pieces[0].shape)] * 4 + [whole(w.shape), tiled(tile, 1), whole((1, units))],
        [tiled(tile, width), tiled(tile, units), pl.BlockSpec((8, tile), lambda i: (0, i))],
        [((2 * tile, width), low_type), ((2 * tile, units), full_type), ((8, 2 * tile), full_type)],
        [],
        "head",
    )(*pieces, w, code, column)


def merge_kernel(sum_ref, here_ref, c_ref, l_ref, d_ref, weight_ref, out_ref, loss_ref):
    half = here_ref.shape[1] // 2

    def over_core(a):
        return jnp.concatenate([a[:, half:], a[:, :half]], 1)

    def over_line(a):
        return jnp.concatenate(
            [pltpu.roll(a[:, :half], half // 2, 1), pltpu.roll(a[:, half:], half // 2, 1)], 1
        )

    parts = (here_ref[...], over_core(c_ref[...]), over_line(l_ref[...]), over_core(over_line(d_ref[...])))
    peak = functools.reduce(jnp.maximum, [part[0:1] for part in parts])
    total = sum(part[1:2] * jnp.exp(part[0:1] - peak) for part in parts)
    picked = sum(part[2:3] for part in parts)
    log_total = peak + jnp.log(total)
    weight = weight_ref[...]
    spot = lax.broadcasted_iota(jnp.int32, (1, 2 * half), 1)
    loss = jnp.where(spot < half // 2, weight * (log_total - picked), 0.0)
    loss_ref[...] = jnp.broadcast_to(jnp.sum(loss, 1, keepdims=True), loss_ref.shape)
    blank = jnp.zeros((126, 2 * half), full_type)
    out_ref[...] = jnp.concatenate([log_total, weight / sum_ref[0], blank], 0).T


def merge(weight_sum, here, over_core, over_line, over_both, weights):
    n = here.shape[1]
    return pl.pallas_call(
        merge_kernel,
        in_specs=[pl.BlockSpec(memory_space=pltpu.SMEM)] + [pl.BlockSpec(memory_space=pltpu.VMEM)] * 5,
        out_shape=[jax.ShapeDtypeStruct((n, 128), full_type), jax.ShapeDtypeStruct((1, 128), full_type)],
        cost_estimate=cost("merge"),
        name="merge",
    )(weight_sum[None], here, over_core, over_line, over_both, weights)


def head_back_kernel(logit_ref, w_ref, code_ref, column_ref, line_ref, d_ref, top_ref, bottom_ref):
    hit = jnp.where(code_ref[...] == column_ref[...], 1.0, 0.0)
    line = line_ref[...]
    d_logits = low(line[:, 1:2] * (jnp.exp(logit_ref[...] - line[:, 0:1]) - hit))
    d_ref[...] = d_logits
    units = w_ref.shape[2]
    total = dot_nt(d_logits[:, :units], w_ref[0]) + dot_nt(d_logits[:, units:], w_ref[1])
    put(low(total), top_ref, bottom_ref)


def head_back(logits, w, code, column, lines):
    n, units = logits.shape
    width = w.shape[1]
    tile = n // 2
    return call(
        head_back_kernel,
        (2,),
        [tiled(tile, units), whole(w.shape), tiled(tile, 1), whole((1, units)), tiled(tile, 128)],
        [tiled(tile, units), fixed((tile, width)), fixed((tile, width))],
        [((n, units), low_type)] + [((tile, width), low_type)] * 2,
        [],
        "head_back",
    )(logits, w, code, column, lines)


def old_stats_kernel(qkv_ref, proj_ref, one_ref, two_ref, head_ref, ada_ref, tab_ref, scale_ref, out_ref):
    def total(values):
        return jnp.sum(jnp.sum(values * values, 1, keepdims=True), 0, keepdims=True)

    spot = lax.broadcasted_iota(jnp.int32, (1, 128), 1)
    line = jnp.zeros((1, 128), full_type)
    sums = [sum(total(qkv_ref[c]) for c in range(3))]
    sums += [total(ref[...]) for ref in (proj_ref, one_ref, two_ref, head_ref, scale_ref)]
    for k, value in enumerate(sums):
        line = jnp.where(spot == 16 + k, value, line)
    out_ref[0:1, :] = line
    line = jnp.where(spot == 8, total(ada_ref[...]), 0.0)
    out_ref[1:2, :] = jnp.where(spot == 9, total(tab_ref[...]), line)


def old_stats(*olds):
    return pl.pallas_call(
        old_stats_kernel,
        out_shape=jax.ShapeDtypeStruct((2, 128), full_type),
        compiler_params=pltpu.CompilerParams(vmem_limit_bytes=48 * 2**20),
        cost_estimate=cost("old_stats"),
        name="old_stats",
    )(*olds)


def put_rows(out_ref, start, value):
    groups, _, rows, _ = out_ref.shape
    for g in range(groups):
        out_ref[g, 0, :, start : start + value.shape[1]] = value[g * rows : (g + 1) * rows]


def head_grad_kernel(a_ref, b_ref, c_ref, d_ref, out_ref):
    put_rows(out_ref, 0, low(dot_tn(a_ref[...], c_ref[...]) + dot_tn(b_ref[...], d_ref[...])))


def head_grad_of(inputs, wanted, groups):
    n, width = inputs[0].shape
    columns = wanted[0].shape[1] // 2
    block = pl.BlockSpec((n, columns), lambda i: (0, i))
    return call(
        head_grad_kernel,
        (2,),
        [whole((n, width))] * 2 + [block] * 2,
        [pl.BlockSpec((groups, 1, width // groups, columns), lambda i: (0, i, 0, 0))],
        [((groups, 2, width // groups, columns), low_type)],
        [],
        "head_grad",
    )(*inputs, *wanted)[0]


def feed_grad_kernel(a_ref, b_ref, c_ref, d_ref, e_ref, f_ref, g_ref, h_ref, out_ref):
    @pl.when(pl.program_id(0) < 2)
    def _():
        put_rows(out_ref, 0, low(dot_tn(a_ref[...], c_ref[...]) + dot_tn(b_ref[...], d_ref[...])))

    @pl.when(pl.program_id(0) >= 2)
    def _():
        put_rows(out_ref, 0, low(dot_tn(e_ref[...], g_ref[...]) + dot_tn(f_ref[...], h_ref[...])))


def feed_grad_of(inputs, d_hidden, d_branch, acts, groups):
    n, width = inputs[0].shape
    columns = acts[0].shape[1] // 2
    early = pl.BlockSpec((n, columns), lambda i: (0, jnp.minimum(i, 1)))
    late = pl.BlockSpec((n, columns), lambda i: (0, jnp.maximum(i - 2, 0)))
    return call(
        feed_grad_kernel,
        (4,),
        [whole((n, width))] * 2 + [early] * 2 + [whole((n, width))] * 2 + [late] * 2,
        [pl.BlockSpec((groups, 1, width // groups, columns), lambda i: (0, i % 2, 0, i // 2))],
        [((groups, 2, width // groups, 2 * columns), low_type)],
        [],
        "feed_grad",
    )(*inputs, *d_hidden, *d_branch, *acts)[0]


def first_grad_kernel(a_ref, b_ref, c_ref, d_ref, e_ref, f_ref, g_ref, h_ref, out_ref):
    group = c_ref.shape[1] // 3
    start = pl.program_id(0) * 128

    def columns(ref):
        return jnp.concatenate(
            [ref[:, pl.ds(pl.multiple_of(start + c * group, 128), 128)] for c in range(3)], 1
        )

    put_rows(out_ref, 0, low(dot_tn(a_ref[...], columns(c_ref)) + dot_tn(b_ref[...], columns(d_ref))))
    put_rows(out_ref, 384, low(dot_tn(e_ref[...], g_ref[...]) + dot_tn(f_ref[...], h_ref[...])))


def first_grad_of(inputs, d_qkv, d_branch, mixed, groups):
    n, width = inputs[0].shape
    return call(
        first_grad_kernel,
        (2,),
        [whole((n, width))] * 2 + [whole(d_qkv[0].shape)] * 2 + [whole((n, width))] * 2
        + [pl.BlockSpec((n, 128), lambda i: (0, i))] * 2,
        [pl.BlockSpec((groups, 1, width // groups, 512), lambda i: (0, i, 0, 0))],
        [((groups, 2, width // groups, 512), low_type)],
        [],
        "first_grad",
    )(*inputs, *d_qkv, *d_branch, *mixed)[0]


def row_stats_kernel(qkv_ref, proj_ref, one_ref, two_ref, head_ref, out_ref):
    n = out_ref.shape[1]
    lane = lax.broadcasted_iota(jnp.int32, (n, 128), 1)
    out = jnp.zeros((n, 128), full_type)
    qkv = sum(jnp.sum(qkv_ref[c] * qkv_ref[c], 1, keepdims=True) for c in range(3))
    sums = [qkv + 3 * qkv_ref.shape[2] * eps_one]
    for ref in (proj_ref, one_ref, two_ref, head_ref):
        values = ref[...]
        sums.append(jnp.sum(values * values, 1, keepdims=True) + ref.shape[1] * eps_one)
    for k, column in enumerate(sums):
        out = jnp.where(lane == k, column, out)
    out_ref[...] = out.T[0:8, :]


def row_stats(*gradients):
    n = gradients[1].shape[0]
    return pl.pallas_call(
        row_stats_kernel,
        out_shape=jax.ShapeDtypeStruct((8, n), full_type),
        compiler_params=pltpu.CompilerParams(vmem_limit_bytes=48 * 2**20),
        cost_estimate=cost("row_stats"),
        name="row_stats",
    )(*gradients)


def column_stats_kernel(
    at_ref, row_ref, old_ref, tail_ref, tables_ref, scale_ref, qkv_ref, proj_ref, one_ref, two_ref, head_ref, ada_ref, out_ref, new_ref, *, decay
):
    n = proj_ref.shape[0]
    rows = row_ref[...]
    padded = jnp.concatenate([rows, jnp.zeros((128 - rows.shape[0], n), full_type)], 0).T
    at = 0
    pieces = [(qkv_ref[c], 0) for c in range(3)]
    pieces += [(ref[...], k + 1) for k, ref in enumerate((proj_ref, one_ref, two_ref, head_ref))]
    for values, k in pieces:
        square = values * values
        columns = square.shape[1]
        out_ref[0:1, at : at + columns] = jnp.sum(square, 0, keepdims=True) + n * eps_one
        out_ref[1:2, at : at + columns] = jnp.sum(
            square * (1.0 / padded[:, k : k + 1]), 0, keepdims=True
        )
        at += columns
    columns = ada_ref.shape[1]
    step = 1024
    total = jnp.zeros((n, 1), full_type)
    for start in range(0, columns, step):
        values = ada_ref[:, start : start + step]
        total = total + jnp.sum(values * values, 1, keepdims=True)
    old = jnp.concatenate([old_ref[...], jnp.zeros((127, n), full_type)], 0).T[:, 0:1]
    row = decay * old + (1.0 - decay) * (total / columns + eps_one)
    lane = lax.broadcasted_iota(jnp.int32, (n, 128), 1)
    new_ref[...] = jnp.where(lane == 0, row, 0.0).T[0:8, :]
    for start in range(0, columns, step):
        values = ada_ref[:, start : start + step]
        square = values * values
        out_ref[0:1, at : at + step] = jnp.sum(square, 0, keepdims=True) + n * eps_one
        out_ref[1:2, at : at + step] = jnp.sum(square * (1.0 / row), 0, keepdims=True)
        at += step
    spots = lax.broadcasted_iota(jnp.int32, (1, 128), 1)
    line = tail_ref[...]
    for k in range(5):
        line = jnp.where(spots == k, jnp.sum(rows[k : k + 1, :], 1, keepdims=True), line)
    line = jnp.where(spots == 5, jnp.sum(row, 0, keepdims=True), line)
    line = jnp.where(spots == 10, tables_ref[...], line)
    scales = scale_ref[...]
    for k in range(2):
        value = jnp.sum(jnp.where((spots < 64) == (k == 0), scales, 0.0), 1, keepdims=True)
        line = jnp.where(spots == 11 + k + 2 * at_ref[0], value, line)
    out_ref[0:1, at : at + 128] = line
    out_ref[1:2, at : at + 128] = jnp.zeros_like(line)


def column_stats(at_c, row_new, old, tail, tables_sum, scales, gradients, decay):
    n = gradients[1].shape[0]
    columns = sum(g.size // n for g in gradients)
    return pl.pallas_call(
        functools.partial(column_stats_kernel, decay=decay),
        out_shape=[
            jax.ShapeDtypeStruct((2, columns + 128), full_type),
            jax.ShapeDtypeStruct((8, n), full_type),
        ],
        in_specs=[pl.BlockSpec(memory_space=pltpu.SMEM)]
        + [pl.BlockSpec(memory_space=pltpu.VMEM)] * (5 + len(gradients)),
        compiler_params=pltpu.CompilerParams(vmem_limit_bytes=48 * 2**20),
        cost_estimate=cost("column_stats"),
        name="column_stats",
    )(at_c[None], row_new, old, tail, tables_sum, scales, *gradients)


def finish_kernel(flat_ref, old_ref, col_ref, sum_ref, *, decay, width, starts):
    columns = old_ref.shape[1]
    line = flat_ref[0:1, columns:]
    new = decay * old_ref[...] + (1.0 - decay) * (flat_ref[0:1, :columns] / width)
    col_ref[...] = new
    ratio = flat_ref[1:2, :columns] / new
    spots = lax.broadcasted_iota(jnp.int32, (1, 128), 1)
    out = jnp.zeros((1, 128), full_type)
    for k in range(6):
        mean = jnp.sum(jnp.where(spots == k, line, 0.0), 1, keepdims=True) / width
        value = jnp.sum(ratio[:, starts[k] : starts[k + 1]], 1, keepdims=True) * mean
        out = jnp.where(spots == k, value, out)
    sum_ref[...] = out


def finish(flat, col_old, decay, width, starts):
    return pl.pallas_call(
        functools.partial(finish_kernel, decay=decay, width=width, starts=starts),
        out_shape=[
            jax.ShapeDtypeStruct(col_old.shape, full_type),
            jax.ShapeDtypeStruct((1, 128), full_type),
        ],
        cost_estimate=cost("finish"),
        name="finish",
    )(flat, col_old)


def head_lanes(shape):
    return lax.broadcasted_iota(jnp.int32, shape, len(shape) - 1) < 64


def per_head(values, first):
    left = jnp.sum(jnp.where(first, values, 0.0), -1, keepdims=True)
    right = jnp.sum(jnp.where(first, 0.0, values), -1, keepdims=True)
    return jnp.where(first, left, right)


def attend_kernel(
    q_ref, k_ref, v_ref, gain_ref, cq_ref, sq_ref, ck_ref, proj_ref,
    mix_ref, lse_ref, top_ref, bottom_ref, q_s, k_s, v_s, bias_s, sum_s
):
    length = q_ref.shape[0]
    tile = length // 2
    first = head_lanes((length, 128))
    query = q_ref[...]
    key = k_ref[...]
    q_s[...] = low(
        query * (lax.rsqrt(per_head(query * query, first) / 64.0 + eps_norm) * gain_ref[...])
    )
    k_s[...] = low(key * (lax.rsqrt(per_head(key * key, first) / 64.0 + eps_norm) * 0.125))
    v_s[...] = low(v_ref[...])
    first_t = head_lanes((tile, 128))
    ck = ck_ref[...]

    @pl.when(pl.program_id(0) == 0)
    def _():
        for i in range(2):
            rows = slice(i * tile, (i + 1) * tile)
            shape = (tile, length)
            here = lax.broadcasted_iota(jnp.int32, shape, 1) - lax.broadcasted_iota(jnp.int32, shape, 0)
            keep = ((ck <= cq_ref[rows, :]) & (ck >= sq_ref[rows, :])) | (here == i * tile)
            bias_s[rows, :] = jnp.where(keep, 0.0, -1e30)
        sum_s[...] = jnp.zeros_like(sum_s)

    for i, out_ref in enumerate((top_ref, bottom_ref)):
        rows = slice(i * tile, (i + 1) * tile)
        query_t = q_s[rows, :]
        mixed, logs = [], []
        for head in range(2):
            chosen = first_t if head == 0 else ~first_t
            scores = dot_nt(jnp.where(chosen, query_t, jnp.zeros_like(query_t)), k_s[...]) + bias_s[rows, :]
            peak = jnp.max(scores, -1, keepdims=True)
            exponent = jnp.exp(scores - peak)
            total = jnp.sum(exponent, -1, keepdims=True)
            mixed.append(dot_nn(low(exponent * (1.0 / total)), v_s[...]))
            logs.append(peak + jnp.log(total))
        mixed = low(jnp.where(first_t, mixed[0], mixed[1]))
        mix_ref[rows, :] = mixed
        turned = jnp.where(first_t, logs[0], logs[1]).T
        lse_ref[0, 0:1, rows] = turned[0:1, :]
        lse_ref[0, 1:2, rows] = turned[64:65, :]
        part = sum_s[rows, :] + dot_nt(mixed, proj_ref[...])
        sum_s[rows, :] = part

        @pl.when(pl.program_id(0) == pl.num_programs(0) - 1)
        def _():
            out_ref[...] = low(part)


def attend(qkv, gain, cq, sq, ck, proj):
    length = qkv.shape[0]
    pairs = qkv.shape[1] // 384
    width = proj.shape[0]
    column = pl.BlockSpec((length, 1), lambda p: (0, 0))
    block = pl.BlockSpec((length, 128), lambda p: (0, p))
    return call(
        attend_kernel,
        (pairs,),
        [
            block,
            pl.BlockSpec((length, 128), lambda p: (0, pairs + p)),
            pl.BlockSpec((length, 128), lambda p: (0, 2 * pairs + p)),
            pl.BlockSpec((1, 128), lambda p: (0, p)),
            column,
            column,
            pl.BlockSpec((1, length), lambda p: (0, 0)),
            pl.BlockSpec((width, 128), lambda p: (0, p)),
        ],
        [block, pl.BlockSpec((1, 2, length), lambda p: (p, 0, 0))] + [fixed((length // 2, width))] * 2,
        [((length, 128 * pairs), low_type), ((pairs, 2, length), full_type)]
        + [((length // 2, width), low_type)] * 2,
        [pltpu.VMEM((length, 128), low_type)] * 3
        + [pltpu.VMEM((length, length), full_type), pltpu.VMEM((length, width), full_type)],
        "attend",
    )(qkv, qkv, qkv, gain, cq[:, None], sq[:, None], ck[None, :], proj)


def attend_back_kernel(
    q_ref, k_ref, v_ref, gain_ref, cq_ref, sq_ref, ck_ref, lse_ref, pa_ref, pb_ref, pc_ref, pd_ref,
    proj_ref, wq_ref, wk_ref, wv_ref, row_ref, d_ref, ds_ref, top_ref, bottom_ref,
    q_s, k_s, v_s, dm_ref, dqa, dka, dva, sum_s, *, tile
):
    length = q_ref.shape[0]
    first = head_lanes((length, 128))
    query = q_ref[...]
    key = k_ref[...]
    gain = gain_ref[...]
    q_n = lax.rsqrt(per_head(query * query, first) / 64.0 + eps_norm)
    k_n = lax.rsqrt(per_head(key * key, first) / 64.0 + eps_norm)
    q_s[...] = low(query * (q_n * gain))
    k_s[...] = low(key * (k_n * 0.125))
    v_s[...] = low(v_ref[...])
    quarter = length // 4
    for k, ref in enumerate((pa_ref, pb_ref, pc_ref, pd_ref)):
        rows = slice(k * quarter, (k + 1) * quarter)
        dm_ref[rows, :] = low(dot_nn(ref[...], proj_ref[...]))

    @pl.when(pl.program_id(0) == 0)
    def _():
        sum_s[...] = jnp.zeros_like(sum_s)
        for k, ref in enumerate((pa_ref, pb_ref, pc_ref, pd_ref)):
            row_ref[k * quarter : (k + 1) * quarter, :] = ref[...]

    dka[...] = jnp.zeros_like(dka)
    dva[...] = jnp.zeros_like(dva)
    first_t = head_lanes((tile, 128))
    ck = ck_ref[...]

    def step(i, carry):
        rows = pl.ds(pl.multiple_of(i * tile, tile), tile)
        query_t = q_s[rows, :]
        dmix_t = dm_ref[rows, :]
        shape = (length, tile)
        here = lax.broadcasted_iota(jnp.int32, shape, 0) - lax.broadcasted_iota(jnp.int32, shape, 1)
        keep = ((ck <= cq_ref[:, rows]) & (ck >= sq_ref[:, rows])) | (here == i * tile)
        d_query = []
        for head in range(2):
            chosen = first_t if head == 0 else ~first_t
            zero = jnp.zeros_like(query_t)
            query_h = jnp.where(chosen, query_t, zero)
            dmix_h = jnp.where(chosen, dmix_t, zero)
            scores = dot_nt(k_s[...], query_h)
            attention = jnp.where(keep, jnp.exp(scores - lse_ref[0, head : head + 1, rows]), 0.0)
            dva[...] += dot_nn(low(attention), dmix_h)
            d_att = dot_nt(v_s[...], dmix_h)
            inner = jnp.sum(attention * d_att, 0, keepdims=True)
            d_scores = low(attention * (d_att - inner))
            dka[...] += dot_nn(d_scores, query_h)
            d_query.append(dot_tn(d_scores, k_s[...]))
        dqa[rows, :] = jnp.where(first_t, d_query[0], d_query[1])
        return carry

    lax.fori_loop(0, length // tile, step, 0)
    q_hat = query * q_n
    k_hat = key * k_n
    d_query = dqa[...]
    along = d_query * q_hat
    ds_ref[0] = jnp.sum(along, 0, keepdims=True) * gain
    group = d_ref.shape[1] // 3
    start = pl.program_id(0) * 128

    def columns(c):
        return pl.ds(pl.multiple_of(start + c * group, 128), 128)

    out_q = low(gain * (d_query - q_hat * (per_head(along, first) / 64.0)) * q_n)
    d_ref[:, columns(0)] = out_q
    d_key = dka[...]
    out_k = low(
        0.125 * (d_key - k_hat * (per_head(d_key * k_hat, first) / 64.0)) * k_n
    )
    out_v = low(dva[...])
    d_ref[:, columns(1)] = out_k
    d_ref[:, columns(2)] = out_v
    half = length // 2
    for rows, out_ref in ((slice(0, half), top_ref), (slice(half, length), bottom_ref)):
        part = sum_s[rows, :] + dot_nt(out_q[rows], wq_ref[...])
        part = part + dot_nt(out_k[rows], wk_ref[...]) + dot_nt(out_v[rows], wv_ref[...])
        sum_s[rows, :] = part

        @pl.when(pl.program_id(0) == pl.num_programs(0) - 1)
        def _():
            out_ref[...] = low(part)


def attend_back(qkv, gain, cq, sq, ck, lse, pieces, proj, w):
    length = qkv.shape[0]
    pairs = qkv.shape[1] // 384
    width = proj.shape[0]
    row = pl.BlockSpec((1, length), lambda p: (0, 0))

    def part(rows, number):
        return pl.BlockSpec((rows, 128), lambda p: (0, number * pairs + p))

    return call(
        functools.partial(attend_back_kernel, tile=256),
        (pairs,),
        [
            part(length, 0),
            part(length, 1),
            part(length, 2),
            pl.BlockSpec((1, 128), lambda p: (0, p)),
            row,
            row,
            pl.BlockSpec((length, 1), lambda p: (0, 0)),
            pl.BlockSpec((1, 2, length), lambda p: (p, 0, 0)),
        ]
        + [whole(pieces[0].shape)] * 4
        + [part(width, 0), part(width, 0), part(width, 1), part(width, 2)],
        [
            fixed((length, width)),
            fixed((length, 384 * pairs)),
            pl.BlockSpec((1, 1, 128), lambda p: (p, 0, 0)),
            fixed((length // 2, width)),
            fixed((length // 2, width)),
        ],
        [
            ((length, width), low_type),
            ((length, 384 * pairs), low_type),
            ((pairs, 1, 128), full_type),
            ((length // 2, width), low_type),
            ((length // 2, width), low_type),
        ],
        [pltpu.VMEM((length, 128), low_type)] * 4
        + [pltpu.VMEM((length, 128), full_type)] * 3
        + [pltpu.VMEM((length, width), full_type)],
        "attend_back",
    )(qkv, qkv, qkv, gain, cq[None, :], sq[None, :], ck[:, None], lse, *pieces, proj, w, w, w)


def body(
    vq_in, codes, segment, live, labels, level_weight, qkv_w, proj_w, fc1_w, fc2_w, head_w, ada_w,
    tables, head_scale, d_stats, qkv_stat, proj_stat, fc1_stat, fc2_stat, head_stat, ada_stat,
    tables_v, scale_v,
):
    g_count = lax.axis_size("g")
    dp_count = g_count * lax.axis_size("c")
    mp_count = lax.axis_size("h") * lax.axis_size("l")
    at_c, at_h, at_l = lax.axis_index("c"), lax.axis_index("h"), lax.axis_index("l")
    row_count, seq_len, code_dim = vq_in.shape
    item_count = labels.shape[1]
    level_count = level_weight.shape[0]
    slice_width = tables.shape[1]
    width = slice_width * dp_count
    half, quarter = seq_len // 2, seq_len // 4
    table_rows = tables.shape[0]
    lead = code_dim + level_count
    per_row = row_count * item_count
    note_rows = -(-(2 * per_row + 3) // slice_width)
    lead_pad = -(-(lead + note_rows) // 16) * 16

    def halves(a):
        n = a.shape[-1] // 2
        lower, upper = low(a[..., :n]), low(a[..., n:])
        return jnp.where(at_c == 0, lower, upper), jnp.where(at_c == 0, upper, lower)

    first_mine, first_other = halves(jnp.concatenate([qkv_w, proj_w.T[None]], 0))
    first_near = ordered(at_c, first_mine, over_c(first_other), 1)
    first_far = over_h(first_near)

    place, weight, weight_here = row_layout(level_weight, segment, live)
    weight_here = weight_here[0, 0]

    per_row = row_count * item_count
    note_rows = -(-(2 * per_row + 3) // slice_width)
    lead_pad = -(-(lead + note_rows) // 16) * 16
    tables_low = low(tables)
    label_flat = labels.reshape(-1)
    digits = jnp.stack([weight_here // 4096, (weight_here // 64) % 64, weight_here % 64])
    note = jnp.concatenate([label_flat // 32, label_flat % 32, digits])
    note = jnp.pad(low(note), (0, (lead_pad - lead) * slice_width - note.shape[0]))
    note = note.reshape(lead_pad - lead, slice_width)
    packed = tie(jnp.concatenate([tables_low[:lead], note], 0), first_near)
    gathered = lax.all_gather(packed, DP, axis=0)
    lead_table = jnp.transpose(gathered, (1, 0, 2)).reshape(lead_pad, width)
    notes = gathered[:, lead : lead + note_rows].reshape(dp_count, -1).astype(jnp.int32)
    labels_all = (notes[:, :per_row] * 32 + notes[:, per_row : 2 * per_row]).reshape(-1)
    weight_sum = full(
        jnp.sum(
            notes[:, 2 * per_row] * 4096
            + notes[:, 2 * per_row + 1] * 64
            + notes[:, 2 * per_row + 2]
        )
    )

    class_hot = (
        labels_all[:, None] + lead == jnp.arange(table_rows, dtype=jnp.int32)[None, :]
    )
    class_vec = dot_nn(low(class_hot), tables_low)
    sigma = jax.nn.sigmoid(class_vec)
    activated = low(class_vec * sigma)
    act_pairs = activated.reshape(g_count, 2, per_row, slice_width)
    act_mine = jnp.where(at_h == 0, act_pairs[:, 0], act_pairs[:, 1]).reshape(-1, slice_width)
    ada_low = low(ada_w)
    mod_part = dot_nn(act_mine, ada_low)
    mod_half = ada_w.shape[1] // 2
    left, right = mod_part[:, :mod_half], mod_part[:, mod_half:]
    mod_send = jnp.where(at_c == 0, right, left)
    mod_sum = jnp.where(at_c == 0, left, right) + over_c(mod_send)
    mod_sum = scatter_g(mod_sum)
    mod_items = ordered(at_c, mod_sum, over_c(mod_sum), 1).reshape(row_count, item_count, 8, width)
    mod_rows = jnp.transpose(mod_items, (0, 2, 1, 3))

    codes, place, live, weight, vq_in, head_gain = tie(
        (codes, place, live, weight, vq_in, head_scale), gathered
    )
    fc1_wide, fc2_wide, head_wide = tie((fc1_w, fc2_w, head_w), mod_send)
    qkv_piece = ordered(at_h, first_near[None], first_far[None], 0)
    qkv_pieces = [qkv_piece] + [over_g(qkv_piece, k) for k in range(1, 4)]

    def near_rows(w):
        kept, other = halves(w)
        return ordered(at_c, kept, over_c(other), 0)

    def gathered_weight(a):
        return lax.all_gather(a, ("h", "g"), axis=0, tiled=True).reshape(2, width, -1)

    feed_near = jnp.concatenate([near_rows(fc1_wide), near_rows(fc2_wide.T)], 1)
    head_near = near_rows(head_wide)

    mine = at_c == at_h
    info = jnp.stack([codes, place, live, weight])
    info = jnp.where(mine, info, over_c(info))
    vq_rows = jnp.where(mine, vq_in, over_c(vq_in))

    def relative(a, axis):
        shape = a.shape
        a = a.reshape(shape[:axis] + (2, 2, quarter) + shape[axis + 1 :])
        a = jnp.where(at_c == 0, a, jnp.flip(a, axis))
        return jnp.where(at_l == 0, a, jnp.flip(a, axis + 1)).reshape(shape)

    info = relative(info, 2)
    vq_rows = relative(vq_rows, 1)
    code_r, place_r, live_r, weight_r = info[0], info[1], info[2], info[3]
    seg_r, level_r = place_r // 16, place_r % 16
    base_r = seg_r * 16
    key_r = jnp.where(live_r > 0, place_r, 1 << 20)
    level_hot = low(
        level_r[..., None] == jnp.arange(lead_pad - code_dim, dtype=jnp.int32)
    )
    feats = jnp.concatenate([vq_rows, level_hot], 2)
    spot = jnp.arange(16, dtype=jnp.int32)
    hot = low((seg_r[..., None] == spot % 4) & (spot < 12))

    def window(*values):
        return lax.optimization_barrier(values)

    def far_part(r):
        return low(full(top[r][quarter:]) + full(moved[r][quarter:]))

    def await_head():
        return held[0]

    def turn(norm, kernel, filler=lambda: None, beside=None):
        moved[1] = over_c(bottom[1])
        first, moved[1] = window(norm(0, (top[0], moved[0], across[0])), moved[1])
        across[1] = over_l(far_part(1))
        pieces = [[first, over_l(first), over_c(first), None], None]
        done, across[1], pieces[0][2] = window(filler(), across[1], pieces[0][2])
        if done is not None and filler is await_head:
            held[0] = done
        second, pieces[0][1] = window(norm(1, (top[1], moved[1], across[1])), pieces[0][1])
        pieces[1] = [second, over_l(second), over_c(second), None]
        pieces[0][3] = over_c(pieces[0][1])
        kernel_out, pieces[1], beside = window(kernel(0, pieces[0]), pieces[1][:3], beside)
        return pieces, kernel_out, done, beside

    def launch():
        moved[0] = over_c(bottom[0])
        sent = far_part(0)
        across[0] = over_l(sent)
        return sent

    gain_own = jnp.where(at_c == 0, head_gain[:2], head_gain[2:])
    gains = jnp.exp(ordered(at_h, gain_own, over_h(gain_own), 0)) / 8.0
    gain_row = jnp.repeat(gains, 64)[None, :]
    inputs_one, qkv_rows, mixed_rows, lse_rows, top, bottom, stream_zero = ([None] * 2 for _ in range(7))
    if g_count == 4:
        inputs_one[0], qkv_rows[0], stream_zero[0], qkv_full, proj_full = enter_first(
            lax.axis_index("g"), feats[0], lead_table, hot[0], mod_rows[0], qkv_pieces
        )
    else:
        wide_piece = lax.all_gather(qkv_piece, "g", axis=0)
        wide_piece = jnp.transpose(wide_piece, (0, 3, 2, 1, 4)).reshape(width, -1)
        qkv_full, proj_full = wide_piece[:, :768], wide_piece[:, 768:]
        inputs_one[0], qkv_rows[0], stream_zero[0] = enter(feats[0], lead_table, hot[0], mod_rows[0], qkv_full)
    feed_full = gathered_weight(tie(feed_near, qkv_rows[0]))
    head_full = gathered_weight(tie(head_near, qkv_rows[0]))
    held = [head_full]

    moved, across = [None] * 2, [None] * 2

    def attention(r, given):
        mixed_rows[r], lse_rows[r], top[r], bottom[r] = attend(
            given, gain_row, place_r[r], base_r[r], key_r[r], proj_full
        )
        return top[r], bottom[r]

    attention(0, qkv_rows[0])
    moved[0] = over_c(bottom[0])
    (inputs_one[1], qkv_rows[1], stream_zero[1]), moved[0] = window(
        enter(tie(feats[1], bottom[0]), lead_table, hot[1], mod_rows[1], qkv_full), moved[0]
    )
    sent = far_part(0)
    across[0] = over_l(sent)
    (top[1], bottom[1]), across[0] = window(attention(1, tie(qkv_rows[1], sent)), across[0])

    branch_one, stream_one, acts, slopes, inputs_two = ([None] * 2 for _ in range(5))

    def norm_two(r, parts):
        branch_one[r], stream_one[r], given = onward(parts, stream_zero[r], hot[r], mod_rows[r], (2, 3, 4))
        return given

    def forward(r, pieces):
        inputs_two[r], acts[r], slopes[r], top[r], bottom[r] = feed(pieces, feed_full)
        return top[r], bottom[r]

    pieces_two, (top[0], bottom[0]), olds, _ = turn(
        norm_two,
        forward,
        lambda: old_stats(qkv_w, proj_w, fc1_w, fc2_w, head_w, ada_w, tables, head_scale[None]),
    )
    pieces_two[1].append(over_c(pieces_two[1][1]))
    sent = launch()
    (top[1], bottom[1]), across[0] = window(
        forward(1, [tie(pieces_two[1][0], sent)] + pieces_two[1][1:]), across[0]
    )

    block_codes = head_w.shape[1]
    half_codes = block_codes // 2
    column = jnp.arange(2 * half_codes, dtype=jnp.int32)
    block_here = (column // half_codes) * 2 + at_l
    column_code = (block_here * block_codes + at_c * half_codes + column % half_codes)[None, :]
    code_column = [code_r[r][:, None] for r in range(2)]
    branch_two, stream_two, logits, stats, d_logits, losses, others, inputs_out = ([None] * 2 for _ in range(8))

    def norm_out(r, parts):
        branch_two[r], stream_two[r], given = onward(parts, stream_one[r], hot[r], mod_rows[r], (5, 6, 7))
        return given

    def score(r, pieces):
        inputs_out[r], logits[r], stats[r] = head(pieces, held[0], code_column[r], column_code)
        return stats[r]

    def compare(r):
        return [over_c(stats[r]), over_l(stats[r]), over_cl(stats[r])]

    def score_back(r):
        lines, losses[r] = merge(weight_sum, stats[r], *others[r], full(weight_r[r])[None, :])
        d_logits[r], top[r], bottom[r] = head_back(logits[r], held[0], code_column[r], column_code, lines)
        return top[r], bottom[r]

    pieces_out, stats[0], _, _ = turn(norm_out, score, await_head)
    pieces_out[1].append(over_c(pieces_out[1][1]))
    stats[1], others[0] = window(score(1, pieces_out[1]), compare(0))
    (top[0], bottom[0]), others[1] = window(score_back(0), compare(1))
    sent = launch()
    logits[1] = tie(logits[1], sent)
    (top[1], bottom[1]), across[0] = window(score_back(1), across[0])

    def reduced(a):
        shape = a.shape[1:]
        a = lax.psum_scatter(a.reshape(-1, shape[2]), "g", scatter_dimension=0, tiled=True)
        return a.reshape(shape)

    def theirs(a):
        return jnp.where(at_h == 0, a[1], a[0])

    def settle(a, other):
        a = full(jnp.where(at_h == 0, a[0], a[1])) + full(other)
        rows = a.shape[0] // 2
        kept = jnp.where(at_c == 0, a[:rows], a[rows:])
        return kept, over_c(jnp.where(at_c == 0, a[rows:], a[:rows]))

    d_two, d_one, items_out, items_two, d_hidden, d_branch_two, d_branch_one = ([None] * 2 for _ in range(7))

    def back_out(r, parts):
        d_two[r], given, items_out[r] = back(
            parts, stream_two[r], hot[r], mod_rows[r], (7, 5), None, branch_two[r], None
        )
        return given

    def backward(r, pieces):
        d_branch_two[r], d_hidden[r], top[r], bottom[r] = feed_back(pieces, slopes[r], feed_full)
        return top[r], bottom[r]

    pieces_d_two, (top[0], bottom[0]), head_part, _ = turn(
        back_out, backward, lambda: head_grad_of(inputs_out, d_logits, g_count)
    )
    head_sum = reduced(head_part)
    pieces_d_two[1].append(over_c(pieces_d_two[1][1]))
    sent = launch()
    (top[1], bottom[1]), across[0], head_sum = window(
        backward(1, [tie(pieces_d_two[1][0], sent)] + pieces_d_two[1][1:]), across[0], head_sum
    )

    d_qkv, scale_rows = ([None] * 2 for _ in range(2))

    def back_two(r, parts):
        d_one[r], given, items_two[r] = back(
            parts, stream_one[r], hot[r], mod_rows[r], (4, 2), d_two[r], branch_one[r], None
        )
        return given

    def attention_back(r, pieces):
        d_branch_one[r], d_qkv[r], scale_rows[r], top[r], bottom[r] = attend_back(
            qkv_rows[r], gain_row, place_r[r], base_r[r], key_r[r], lse_rows[r], pieces, proj_full, qkv_full
        )
        return top[r], bottom[r]

    pieces_d_one, (top[0], bottom[0]), feed_part, head_other = turn(
        back_two,
        attention_back,
        lambda: feed_grad_of(inputs_two, d_hidden, d_branch_two, acts, g_count),
        over_h(theirs(head_sum)),
    )
    feed_sum = reduced(feed_part)
    pieces_d_one[1].append(over_c(pieces_d_one[1][1]))
    sent = launch()
    leaving = theirs(feed_sum)
    (top[1], bottom[1]), across[0], feed_other = window(
        attention_back(1, [tie(pieces_d_one[1][0], sent, leaving)] + pieces_d_one[1][1:]), across[0], over_h(leaving)
    )
    moved[1] = over_c(bottom[1])
    items_one, lead_parts = ([None] * 2 for _ in range(2))

    def back_one(r, parts):
        items_one[r], lead_parts[r] = back(
            parts, stream_zero[r], hot[r], mod_rows[r], (1,), d_one[r], None, feats[r]
        )
        return items_one[r]

    items_one[0], moved[1] = window(back_one(0, (top[0], moved[0], across[0])), moved[1])
    sent = far_part(1)
    across[1] = over_l(sent)
    first_part = first_grad_of(inputs_one, tie(d_qkv, sent), d_branch_one, mixed_rows, g_count)
    first_part, across[1] = window(first_part, across[1])
    first_sum = reduced(first_part)
    back_one(1, (top[1], moved[1], across[1]))
    lead_part = lead_parts[0] + lead_parts[1]

    def flat_items(items, number):
        return jnp.concatenate([items[r][number, :item_count] for r in range(2)], 0)

    d_items = jnp.concatenate(
        [flat_items(items_one, 0), flat_items(items_one, 1), flat_items(items_two, 2)]
        + [flat_items(items_two, 0), flat_items(items_two, 1), flat_items(items_out, 2)]
        + [flat_items(items_out, 0), flat_items(items_out, 1)],
        1,
    )
    left, right = d_items[:, :mod_half], d_items[:, mod_half:]
    d_items = jnp.where(at_c == 0, left, right) + over_c(jnp.where(at_c == 0, right, left))
    d_items = low(d_items + over_l(d_items))
    d_items = gather_g(ordered(at_h, d_items, over_h(d_items), 0))
    d_items = ordered(at_c, d_items, over_c(d_items), 1)
    ada_grad = dot_tn(activated, d_items)
    d_act_vec = dot_nt(d_items, ada_low)
    d_class = d_act_vec * (sigma * (1.0 + class_vec * (1.0 - sigma)))
    lead_part = jnp.transpose(lead_part.reshape(lead_pad, dp_count, slice_width), (1, 0, 2))
    lead_grad = jnp.sum(lax.all_to_all(lead_part, DP, 0, 0, tiled=True).reshape(dp_count, lead_pad, slice_width), 0)
    lead_grad = lead_grad + over_l(lead_grad)
    lead_grad = lead_grad + over_h(lead_grad)
    tables_grad = dot_tn(full(class_hot), d_class, highest)
    tables_grad = tables_grad + jnp.pad(lead_grad[:lead], ((0, table_rows - lead), (0, 0)))

    head_grad = ordered(at_c, *settle(tie(head_sum, items_one[0]), head_other), 1)
    kept, moved_half = settle(feed_sum, feed_other)
    n = kept.shape[1] // 2
    fc1_grad = ordered(at_c, kept[:, :n], moved_half[:, :n], 1)
    fc2_grad = ordered(at_c, kept[:, n:], moved_half[:, n:], 1)
    kept, moved_half = settle(first_sum, over_h(theirs(first_sum)))
    first_halves = jnp.stack([kept, moved_half])
    first_halves = jnp.where(at_c == 0, first_halves, first_halves[::-1])
    first_halves = jnp.transpose(first_halves.reshape(2, slice_width, 4, -1), (2, 1, 0, 3))
    first_halves = first_halves.reshape(4, slice_width, -1)
    qkv_grad, proj_grad = first_halves[:3], first_halves[3]

    decay = 1.0 - STEP ** (-0.8)
    grads = [qkv_grad, proj_grad, fc1_grad, fc2_grad, head_grad, ada_grad]
    masters = [qkv_w, proj_w.T, fc1_w, fc2_w.T, head_w, ada_w]
    wide = [g.size // slice_width * (mp_count if k < 5 else 1) for k, g in enumerate(grads)]
    sizes = [g.size // slice_width for g in grads]
    starts = [sum(sizes[:k]) for k in range(7)]

    def over_mp(a):
        a = a + over_l(a)
        return a + over_h(a)

    spots = jnp.arange(128, dtype=jnp.int32)[None, :]
    early_line = over_mp(tie(olds[:1] + jnp.where(spots == 22, losses[0] + losses[1], 0.0), lead_part))
    tail = early_line + olds[1:]
    rows_all = over_mp(row_stats(*grads[:5]))
    wide_column = jnp.array(wide[:5], full_type)[:, None]
    row_new = decay * d_stats[:5] + (1.0 - decay) * (rows_all[:5] / wide_column)
    tables_v_new = decay * tables_v + (1.0 - decay) * (tables_grad * tables_grad + eps_one)
    tables_step = tables_grad * lax.rsqrt(tables_v_new)
    tables_sum = jnp.sum(tables_step * tables_step)[None, None]
    scales = tie(scale_rows[0] + scale_rows[1], lead_part)
    scales = jnp.where(at_h == 0, scales[0], scales[1]) + over_h(
        jnp.where(at_h == 0, scales[1], scales[0])
    )
    flat, ada_row = column_stats(at_c, row_new, d_stats[5:6], tail, tables_sum, scales, grads, decay)
    d_stats_new = jnp.concatenate([row_new, ada_row[:1]], 0)
    if g_count == 4:
        flat = flat + over_c(flat)
        flat = flat + over_g(flat, 1)
        flat = flat + over_g(flat, 2)
    else:
        flat = lax.psum(flat, DP)
    col_old = jnp.concatenate(
        [qkv_stat.reshape(-1), proj_stat, fc1_stat, fc2_stat, head_stat, ada_stat]
    )[None, :]
    col_line, sum_line = finish(flat, col_old, decay, width, starts)
    col_new = [col_line[0, starts[k] : starts[k + 1]] for k in range(6)]
    line = flat[:1, starts[6] :]
    scale_grad = line[0, 11:15]
    loss_sum = line[0, 22]
    scale_v_new = decay * scale_v + (1.0 - decay) * (scale_grad * scale_grad + eps_one)
    scale_step = scale_grad * lax.rsqrt(scale_v_new)
    scale_spot = jnp.where(spots == 7, jnp.sum(scale_step * scale_step), 0.0)
    split = over_mp(jnp.where(spots == 5, 0.0, sum_line) + scale_spot)
    step_line = split + jnp.where(spots == 5, sum_line, 0.0)
    step_line = step_line + jnp.where(spots == 6, line[0, 10], 0.0)
    weight_line = jnp.zeros((1, 128), full_type)
    for k, value in enumerate([line[0, 16 + j] for j in range(5)] + [line[0, 8], line[0, 9], early_line[0, 21]]):
        weight_line = jnp.where(spots == k, value, weight_line)
    entries = [width * wide[k] for k in range(6)] + [table_rows * width, head_scale.shape[0] * mp_count]
    entry_line = jnp.array(entries + [1] * 120, full_type)[None, :]
    ratio = jnp.sqrt(step_line / entry_line) / clip_rms
    spread = jnp.maximum(eps_two, jnp.sqrt(weight_line / entry_line))
    factor = (rate_step * spread / jnp.maximum(1.0, ratio))[0]
    row_mean = line[0, :6] / width
    sides = [col_new[0].reshape(3, 1, -1)] + [c[None, :] for c in col_new[1:]]
    raw_steps = [
        grads[k] * lax.rsqrt(d_stats_new[k][:, None] * sides[k] / row_mean[k]) for k in range(6)
    ] + [tables_step, scale_step]
    parameters = masters + [tables, head_scale]
    news = [parameters[k] - factor[k] * raw_steps[k] for k in range(8)]
    return (
        loss_sum,
        weight_sum,
        qkv_grad,
        proj_grad.T,
        fc1_grad,
        fc2_grad.T,
        head_grad,
        ada_grad,
        tables_grad,
        scale_grad,
        d_stats_new,
        col_new[0].reshape(3, -1),
        col_new[1],
        col_new[2],
        col_new[3],
        col_new[4],
        col_new[5],
        tables_v_new,
        scale_v_new,
        news[0],
        news[1].T,
        news[2],
        news[3].T,
        news[4],
        news[5],
        news[6],
        news[7],
    )


def solution(mesh):
    inner = Mesh(
        mesh.devices.reshape(mesh.shape["dp"] // 2, 2, mesh.shape["mp"] // 2, 2),
        ("g", "c", "h", "l"),
    )
    return jax.shard_map(
        body,
        mesh=inner,
        in_specs=(
            P(DP, None, None),
            P(DP, None),
            P(DP, None),
            P(DP, None),
            P(DP, None),
            P(),
            P(None, DP, MP),
            P(MP, DP),
            P(DP, MP),
            P(MP, DP),
            P(DP, MP),
            P(DP, None),
            P(None, DP),
            P(MP),
            P(None, DP),
            P(None, MP),
            P(MP),
            P(MP),
            P(MP),
            P(MP),
            P(),
            P(None, DP),
            P(MP),
        ),
        out_specs=(
            P(),
            P(),
            P(None, DP, MP),
            P(MP, DP),
            P(DP, MP),
            P(MP, DP),
            P(DP, MP),
            P(DP, None),
            P(None, DP),
            P(MP),
            P(None, DP),
            P(None, MP),
            P(MP),
            P(MP),
            P(MP),
            P(MP),
            P(),
            P(None, DP),
            P(MP),
            P(None, DP, MP),
            P(MP, DP),
            P(DP, MP),
            P(MP, DP),
            P(DP, MP),
            P(DP, None),
            P(None, DP),
            P(MP),
        ),
        check_vma=False,
    )
```

time: 2180 us -> 646 us (0.30)
  waiting for transfers between devices: 1240 us -> 169 us
  matrix products: 246 us -> 12.2 us
  other arithmetic: 262 us -> 65.5 us
  Pallas kernels: 0 us -> 179 us
  local copies, waits for them, and re-layouts: 246 us -> 111 us
  blocking collectives: 143 us -> 9.22 us
  starting transfers between devices: 1.58 us -> 69.4 us
    psum x5 -> x0, waiting for transfers between devices: 811 us -> none  [the longest x1 223 us: body(): d_out = lax.psum(against_rows(d_logits, head_low), 'mp')]
    reduce_scatter x7 -> x3, waiting for transfers between devices: 290 us -> 25.2 us  [reduced(): lax.psum_scatter(a.reshape(-1, shape[2]), 'g', scatter_dimension=0, tiled...]
    dot_general x40 -> x5, matrix products: 246 us -> 12.2 us  [the longest x2 4.86 us: dot_tn(): lax.dot_general(a, b, (((0,), (0,)), ((), ())), preferred_element_type=fu...]
    pallas_call x0 -> x34, Pallas kernels: none -> 179 us  [the longest x2 40.9 us: attend_back(): call(functools.partial(attend_back_kernel, tile=256), (pairs,), [part(len...]
    ppermute x0 -> x91, waiting for transfers between devices: none -> 127 us  [the longest x25 60.3 us: over_l(): return lax.ppermute(a, 'l', swap_pairs)]
    all_gather x6 -> x2, waiting for transfers between devices: 137 us -> 16 us  [gathered_weight(): lax.all_gather(a, ('h', 'g'), axis=0, tiled=True).reshape(2, width, -1)]
    reduce_sum x48 -> x3, other arithmetic: 119 us -> 2.16 us  [the longest x1 1.44 us: body(): scale_spot = jnp.where(spots == 7, jnp.sum(scale_step * scale_step), 0.0)]
    psum x4 -> x0, blocking collectives: 90.6 us -> none  [the longest x1 39.6 us: body(): lax.psum((update_local, weight_local), ('dp', 'mp'))]
  transfers between devices with their start and end apart: 18 -> 97, of which waited for: 13 -> 39; matrix products, arithmetic and copies ran while one was open for 20% -> 10% of each run, Pallas kernels for 0% -> 26%
where the time goes in v1:
time: 646 us; the launch traced here: 636 us
  Pallas kernels  179 us (28%)
  waiting for transfers between devices  169 us (26%)
  local copies, waits for them, and re-layouts  111 us (17%)
  starting transfers between devices  69.4 us (11%)
  other arithmetic  65.5 us (10%)
  between operations  21.4 us (3%)
  matrix products  12.2 us (2%)
  blocking collectives  9.22 us (1%)
    unnamed x566, local copies, waits for them, and re-layouts  89.4 us
    ppermute x25, waiting for transfers between devices, over_l(): return lax.ppermute(a, 'l', swap_pairs)  60.3 us
    pallas_call x2, Pallas kernels, attend_back(): call(functools.partial(attend_back_kernel, tile=256), (pairs,), [part(len...  40.9 us
    ppermute x11, waiting for transfers between devices, over_g(): return lax.ppermute(a, 'g', [(i, i ^ k) for i in range(lax.axis_size('g'))])  39.5 us
    reduce_scatter x3, waiting for transfers between devices, reduced(): lax.psum_scatter(a.reshape(-1, shape[2]), 'g', scatter_dimension=0, tiled...  25.2 us
    ppermute x11, starting transfers between devices, over_h(): return lax.ppermute(a, 'h', swap_pairs)  20 us
    ppermute x25, starting transfers between devices, over_l(): return lax.ppermute(a, 'l', swap_pairs)  20 us
    pallas_call x2, Pallas kernels, attend(): call(attend_kernel, (pairs,), [block, pl.BlockSpec((length, 128), lambda...  19.1 us
  transfers between devices with their start and end apart: 97, of which 39 were waited for; matrix products, arithmetic and copies ran while one was open for 10% of the time, Pallas kernels for 26%

profile of v1, /device:TPU:0, one launch (start us, length us, event | category | flops | bytes accessed | tf_op | source)
XLA Modules:
  0.0 636.4 jit_solution(15647584072221571090)
XLA Ops:
  18.9 9.2 %all-gather = bf16[384,128]{1,0:T(8,128)(2,1)S(1)} all-gather(bf16[48,128]{1,0:T(8,128)(2,1)S(1)} %pad_maximum_fusion.3), channel_id=2, replica_groups=mesh['g'=4,'c'=2,'h'=2,'l'=2] {'g','c'}, dimensions={0}, use_global_device_ids=true | all-gather | bytes 110592 | tf_op jit(solution)/shard_map/all_gather | solution.py:1045
  63.1 21.0 %collective-permute-done.10.c_ref = bf16[2,4,256,128]{3,2,1,0:T(8,128)(2,1)S(1)} collective-permute-done((bf16[2,4,256,128]{3,2,1,0:T(8,128)(2,1)S(1)}, bf16[2,4,256,128]{3,2,1,0:T(8,128)(2,1)S(1)}, u32[]{:S(2)}, u32[]{:S(2)}) %collective-permute-start.10) | collective-permute-done | bytes 524320 | tf_op jit(solution)/shard_map/ppermute | solution.py:77
  85.4 5.7 enter_first.1
  94.7 4.1 collective-permute-done.12
  103.8 10.0 %attend.2 = (bf16[768,256]{1,0:T(8,128)(2,1)S(1)}, f32[2,2,768]{2,1,0:T(2,128)S(1)}, bf16[384,1024]{1,0:T(8,128)(2,1)S(1)}, bf16[384,1024]{1,0:T(8,128)(2,1)}) custom-call(f32[768,768]{1,0:T(8,128)S(1)} %copy-done.124, f32[768,768]{1,0:T(8,128)S(1)} %copy-done.124, f32[768,768]{1,0:T(8,128)S(1)} %copy-done.124, ...), custom_call_target="tpu_custom_call" | custom-call | flops 11000000512 | bytes 11000000 | tf_op jit(solution)/shard_map/attend/pallas_call | solution.py:848
  119.6 5.4 enter.1
  130.9 9.0 %attend.3 = (bf16[768,256]{1,0:T(8,128)(2,1)S(1)}, f32[2,2,768]{2,1,0:T(2,128)S(1)}, bf16[384,1024]{1,0:T(8,128)(2,1)S(1)}, bf16[384,1024]{1,0:T(8,128)(2,1)S(1)}) custom-call(f32[768,768]{1,0:T(8,128)S(1)} %copy-done.117, f32[768,768]{1,0:T(8,128)S(1)} %copy-done.117, f32[768,768]{1,0:T(8,128)S(1)} %copy-done.117, f32[1,256]{1,0:T(1,128)S(1)} %copy-done.55, ...), custom_call_target="tpu_custom_call" | custom-call | flops 11000000512 | bytes 11000000 | tf_op jit(solution)/shard_map/attend/pallas_call | solution.py:848
  139.9 4.2 collective-permute-done.14.c_ref
  153.6 19.9 %collective-permute-done.16.c_ref = bf16[192,1024]{1,0:T(8,128)(2,1)S(1)} collective-permute-done((bf16[192,1024]{1,0:T(8,128)(2,1)S(1)}, bf16[192,1024]{1,0:T(8,128)(2,1)S(1)}, u32[]{:S(2)}, u32[]{:S(2)}) %collective-permute-start.16) | collective-permute-done | bytes 393248 | tf_op jit(solution)/shard_map/ppermute | solution.py:65
  176.3 5.3 collective-permute-done.18.b_ref
  188.4 8.2 %feed.2 = (bf16[768,1024]{1,0:T(8,128)(2,1)S(1)}, bf16[768,1024]{1,0:T(8,128)(2,1)}, f32[768,1024]{1,0:T(8,128)}, bf16[384,1024]{1,0:T(8,128)(2,1)S(1)}, bf16[384,1024]{1,0:T(8,128)(2,1)S(1)}) custom-call(bf16[192,1024]{1,0:T(8,128)(2,1)S(1)} %copy-done.79, bf16[192,1024]{1,0:T(8,128)(2,1)S(1)} %copy-done.86, bf16[192,1024]{1,0:T(8,128)(2,1)S(1)} %copy-done.84, ...), custom_call_target="tpu_custom_call" | custom-call | flops 8999999488 | bytes 9000000 | tf_op jit(solution)/shard_map/feed/pallas_call | solution.py:434
  203.6 8.6 %feed.3 = (bf16[768,1024]{1,0:T(8,128)(2,1)S(1)}, bf16[768,1024]{1,0:T(8,128)(2,1)}, f32[768,1024]{1,0:T(8,128)}, bf16[384,1024]{1,0:T(8,128)(2,1)S(1)}, bf16[384,1024]{1,0:T(8,128)(2,1)S(1)}) custom-call(bf16[192,1024]{1,0:T(8,128)(2,1)S(1)} %copy-done.75, bf16[192,1024]{1,0:T(8,128)(2,1)} %collective-permute-done.22.b_ref, ...), custom_call_target="tpu_custom_call" | custom-call | flops 8999999488 | bytes 9000000 | tf_op jit(solution)/shard_map/feed/pallas_call | solution.py:434
  221.8 16.0 %all-gather.6.cloned.1.call-done = bf16[2048,512]{1,0:T(8,128)(2,1)} async-done(((bf16[256,512]{1,0:T(8,128)(2,1)}), bf16[2048,512]{1,0:T(8,128)(2,1)}) %all-gather.6.cloned.1.call-update) | async-done | bytes 2097168 | tf_op jit(solution)/shard_map/all_gather | solution.py:1087
  251.5 4.8 head.2
  276.9 4.8 head_back.2
  289.8 4.2 head_back.3
  301.1 5.9 head_grad.1
  307.0 5.0 collective-permute-done.45.refs_2_
  326.4 7.6 %feed_back.2 = (bf16[768,1024]{1,0:T(8,128)(2,1)S(1)}, bf16[768,1024]{1,0:T(8,128)(2,1)}, bf16[384,1024]{1,0:T(8,128)(2,1)S(1)}, bf16[384,1024]{1,0:T(8,128)(2,1)S(1)}) custom-call(bf16[192,1024]{1,0:T(8,128)(2,1)S(1)} %copy-done.82, bf16[192,1024]{1,0:T(8,128)(2,1)S(1)} %collective-permute-done.47.b_ref, bf16[192,1024]{1,0:T(8,128)(2,1)S(1)} %copy-done.90, ...), custom_call_target="tpu_custom_call" | custom-call | flops 7000000000 | bytes 7000000 | tf_op jit(solution)/shard_map/feed_back/pallas_call | solution.py:463
  339.3 7.7 %feed_back.3 = (bf16[768,1024]{1,0:T(8,128)(2,1)S(1)}, bf16[768,1024]{1,0:T(8,128)(2,1)}, bf16[384,1024]{1,0:T(8,128)(2,1)S(1)}, bf16[384,1024]{1,0:T(8,128)(2,1)S(1)}) custom-call(bf16[192,1024]{1,0:T(8,128)(2,1)S(1)} %get-tuple-element.345.a_ref, bf16[192,1024]{1,0:T(8,128)(2,1)S(1)} %collective-permute-done.49.b_ref, ...), custom_call_target="tpu_custom_call" | custom-call | flops 7000000000 | bytes 7000000 | tf_op jit(solution)/shard_map/feed_back/pallas_call | solution.py:463
  361.0 11.2 %feed_grad.1 = bf16[4,2,256,1024]{3,2,1,0:T(8,128)(2,1)} custom-call(bf16[768,1024]{1,0:T(8,128)(2,1)S(1)} %copy-done.162, bf16[768,1024]{1,0:T(8,128)(2,1)S(1)} %copy-done.164, bf16[768,1024]{1,0:T(8,128)(2,1)S(1)} %copy-done.115, bf16[768,1024]{1,0:T(8,128)(2,1)} %get-tuple-element.363.d_ref, bf16[768,1024]{1,0:T(8,128)(2,1)} %copy-done.114, ...), custom_call_target="tpu_custom_call" | custom-call | flops 12000000000 | bytes 12000000 | tf_op jit(solution)/shard_map/feed_grad/pallas_call | solution.py:626
  392.9 20.4 %attend_back.2 = (bf16[768,1024]{1,0:T(8,128)(2,1)}, bf16[768,768]{1,0:T(8,128)(2,1)S(1)}, f32[2,1,128]{2,1,0:T(1,128)S(1)}, bf16[384,1024]{1,0:T(8,128)(2,1)S(1)}, bf16[384,1024]{1,0:T(8,128)(2,1)S(1)}) custom-call(f32[768,768]{1,0:T(8,128)} %get-tuple-element.237.q_ref.k_ref.v_ref, f32[768,768]{1,0:T(8,128)} %get-tuple-element.237.q_ref.k_ref.v_ref, ...), custom_call_target="tpu_custom_call" | custom-call | flops 16000000000 | bytes 16000000 | tf_op jit(solution)/shard_map/attend_back/pallas_call | solution.py:966
  418.7 8.3 %reduce-scatter.6.cloned.1.call-done = bf16[512,1024]{1,0:T(8,128)(2,1)} async-done(((bf16[2048,1024]{1,0:T(8,128)(2,1)}), bf16[512,1024]{1,0:T(8,128)(2,1)}) %reduce-scatter.6.cloned.1.call-update) | async-done | bytes 1048592 | tf_op jit(solution)/shard_map/reduce_scatter | solution.py:1234
  436.2 20.5 %attend_back.3 = (bf16[768,1024]{1,0:T(8,128)(2,1)}, bf16[768,768]{1,0:T(8,128)(2,1)S(1)}, f32[2,1,128]{2,1,0:T(1,128)S(1)}, bf16[384,1024]{1,0:T(8,128)(2,1)S(1)}, bf16[384,1024]{1,0:T(8,128)(2,1)}) custom-call(f32[768,768]{1,0:T(8,128)} %get-tuple-element.251.q_ref.k_ref.v_ref, f32[768,768]{1,0:T(8,128)} %get-tuple-element.251.q_ref.k_ref.v_ref, ...), custom_call_target="tpu_custom_call" | custom-call | flops 16000000000 | bytes 16000000 | tf_op jit(solution)/shard_map/attend_back/pallas_call | solution.py:966
  470.2 9.0 %first_grad.1 = bf16[4,2,256,512]{3,2,1,0:T(8,128)(2,1)} custom-call(bf16[768,1024]{1,0:T(8,128)(2,1)S(1)} %copy-done.105, bf16[768,1024]{1,0:T(8,128)(2,1)} %copy-done.106, bf16[768,768]{1,0:T(8,128)(2,1)S(1)} %copy-done.108, bf16[768,768]{1,0:T(8,128)(2,1)S(1)} %copy-done.110, bf16[768,1024]{1,0:T(8,128)(2,1)} %get-tuple-element.398.e_ref, ...), custom_call_target="tpu_custom_call" | custom-call | flops 6000000000 | bytes 6000000 | tf_op jit(solution)/shard_map/first_grad/pallas_call | solution.py:652
  506.9 5.3 collective-permute-done.79
  514.1 16.9 %reduce-scatter.8.cloned.1.call-done = bf16[512,512]{1,0:T(8,128)(2,1)} async-done(((bf16[2048,512]{1,0:T(8,128)(2,1)}), bf16[512,512]{1,0:T(8,128)(2,1)}) %reduce-scatter.8.cloned.1.call-update) | async-done | bytes 524304 | tf_op jit(solution)/shard_map/reduce_scatter | solution.py:1234
  535.3 11.5 %collective-permute-done.68 = bf16[256,512]{1,0:T(8,128)(2,1)S(1)} collective-permute-done((bf16[256,512]{1,0:T(8,128)(2,1)S(1)}, bf16[256,512]{1,0:T(8,128)(2,1)S(1)}, u32[]{:S(2)}, u32[]{:S(2)}) %collective-permute-start.68) | collective-permute-done | bytes 262176 | tf_op jit(solution)/shard_map/ppermute | solution.py:69
  548.1 3.9 convolution_multiply_fusion
  565.6 4.5 column_stats.1
  595.8 6.3 bitcast_divide_fusion
  614.0 7.8 %multiply_subtract_fusion = f32[128,8192]{1,0:T(8,128)} fusion(f32[128,8192]{1,0:T(8,128)} %ada_ref.1, f32[128,8192]{1,0:T(8,128)} %fusion.6.ada_ref, f32[]{:T(128)} %bitcast.118, f32[8192]{0:T(1024)S(1)} %bitcast.264, f32[128]{0:T(128)S(1)} %get-tuple-element.590, f32[]{:T(128)} %bitcast.116), kind=kLoop, calls=%fused_computation | loop fusion | flops 5242880 | bytes 12616200 | tf_op jit(solution)/shard_map/sub | solution.py:1409
  (940 shorter events, 322.7 us)
Async XLA Ops:
  7.2 178.2 %all-gather.4.cloned.1.call-start = ((), (), s32[]{:S(2)}) async-start(), calls=%async_computation.4 | async-start | bytes 4718592 | tf_op jit(solution)/shard_map/all_gather | solution.py:1087
  15.2 42.1 %collective-permute-start.8 = (bf16[4,256,128]{2,1,0:T(8,128)(2,1)}, bf16[4,256,128]{2,1,0:T(8,128)(2,1)}, u32[]{:S(2)}, u32[]{:S(2)}) collective-permute-start(bf16[4,256,128]{2,1,0:T(8,128)(2,1)} %maximum_select_fusion.5), channel_id=1, source_target_pairs={{0,2},{2,0},{1,3},{3,1},{4,6},{6,4},{5,7},{7,5},{8,10},{10,8},{9,1... | collective-permute-start | bytes 786440 | tf_op jit(solution)/shard_map/ppermute | solution.py:69
  36.4 14.9 %collective-permute-start.21 = (bf16[128,512]{1,0:T(8,128)(2,1)}, bf16[128,512]{1,0:T(8,128)(2,1)}, u32[]{:S(2)}, u32[]{:S(2)}) collective-permute-start(bf16[128,512]{1,0:T(8,128)(2,1)} %get-tuple-element.537), channel_id=1, source_target_pairs={{0,4},{4,0},{1,5},{5,1},{2,6},{6,2},{3,7},{7,3},{8,12},{12,8},{9,1... | collective-permute-start | bytes 393224 | tf_op jit(solution)/shard_map/ppermute | solution.py:61
  58.5 25.6 %collective-permute-start.10 = (bf16[2,4,256,128]{3,2,1,0:T(8,128)(2,1)S(1)}, bf16[2,4,256,128]{3,2,1,0:T(8,128)(2,1)S(1)}, u32[]{:S(2)}, u32[]{:S(2)}) collective-permute-start(bf16[2,4,256,128]{3,2,1,0:T(8,128)(2,1)S(1)} %maximum_select_fusion.1.a_ref), channel_id=1, source_target_pairs={{0,16},{8,24},{16,0},{24,8},{1,17},{9,25},{17,1},{25,9},{2,18},{10... | collective-permute-start | bytes 1572872 | tf_op jit(solution)/shard_map/ppermute | solution.py:77
  59.1 25.0 %collective-permute-start.11 = (bf16[2,4,256,128]{3,2,1,0:T(8,128)(2,1)S(1)}, bf16[2,4,256,128]{3,2,1,0:T(8,128)(2,1)S(1)}, u32[]{:S(2)}, u32[]{:S(2)}) collective-permute-start(bf16[2,4,256,128]{3,2,1,0:T(8,128)(2,1)S(1)} %maximum_select_fusion.1.a_ref), channel_id=1, source_target_pairs={{0,24},{8,16},{16,8},{24,0},{1,25},{9,17},{17,9},{25,1},{2,26},{10... | collective-permute-start | bytes 1572872 | tf_op jit(solution)/shard_map/ppermute | solution.py:77
  60.6 24.8 %collective-permute-start.9 = (bf16[2,4,256,128]{3,2,1,0:T(8,128)(2,1)S(1)}, bf16[2,4,256,128]{3,2,1,0:T(8,128)(2,1)S(1)}, u32[]{:S(2)}, u32[]{:S(2)}) collective-permute-start(bf16[2,4,256,128]{3,2,1,0:T(8,128)(2,1)S(1)} %maximum_select_fusion.1.a_ref), channel_id=1, source_target_pairs={{0,8},{8,0},{16,24},{24,16},{1,9},{9,1},{17,25},{25,17},{2,10},{10... | collective-permute-start | bytes 1572872 | tf_op jit(solution)/shard_map/ppermute | solution.py:77
  94.2 143.6 %all-gather.6.cloned.1.call-start = ((), (), s32[]{:S(2)}) async-start(), calls=%async_computation.5 | async-start | bytes 2359296 | tf_op jit(solution)/shard_map/all_gather | solution.py:1087
  127.5 16.6 %collective-permute-start.14 = (bf16[192,1024]{1,0:T(8,128)(2,1)S(1)}, bf16[192,1024]{1,0:T(8,128)(2,1)S(1)}, u32[]{:S(2)}, u32[]{:S(2)}) collective-permute-start(bf16[192,1024]{1,0:T(8,128)(2,1)S(1)} %add_convert_fusion.9), channel_id=1, source_target_pairs={{0,1},{1,0},{2,3},{3,2},{4,5},{5,4},{6,7},{7,6},{8,9},{9,8},{10,11... | collective-permute-start | bytes 1179656 | tf_op jit(solution)/shard_map/ppermute | solution.py:65
  148.5 25.0 %collective-permute-start.16 = (bf16[192,1024]{1,0:T(8,128)(2,1)S(1)}, bf16[192,1024]{1,0:T(8,128)(2,1)S(1)}, u32[]{:S(2)}, u32[]{:S(2)}) collective-permute-start(bf16[192,1024]{1,0:T(8,128)(2,1)S(1)} %add_convert_fusion.8), channel_id=1, source_target_pairs={{0,1},{1,0},{2,3},{3,2},{4,5},{5,4},{6,7},{7,6},{8,9},{9,8},{10,11... | collective-permute-start | bytes 1179656 | tf_op jit(solution)/shard_map/ppermute | solution.py:65
  148.5 25.0 %collective-permute-start.17 = (bf16[192,1024]{1,0:T(8,128)(2,1)S(1)}, bf16[192,1024]{1,0:T(8,128)(2,1)S(1)}, u32[]{:S(2)}, u32[]{:S(2)}) collective-permute-start(bf16[192,1024]{1,0:T(8,128)(2,1)S(1)} %get-tuple-element.258.a_ref), channel_id=1, source_target_pairs={{0,4},{4,0},{1,5},{5,1},{2,6},{6,2},{3,7},{7,3},{8,12},{12,8},{9,1... | collective-permute-start | bytes 1179656 | tf_op jit(solution)/shard_map/ppermute | solution.py:61
  148.8 32.7 %collective-permute-start.18 = (bf16[192,1024]{1,0:T(8,128)(2,1)S(1)}, bf16[192,1024]{1,0:T(8,128)(2,1)S(1)}, u32[]{:S(2)}, u32[]{:S(2)}) collective-permute-start(bf16[192,1024]{1,0:T(8,128)(2,1)S(1)} %get-tuple-element.258.a_ref), channel_id=1, source_target_pairs={{0,1},{1,0},{2,3},{3,2},{4,5},{5,4},{6,7},{7,6},{8,9},{9,8},{10,11... | collective-permute-start | bytes 1179656 | tf_op jit(solution)/shard_map/ppermute | solution.py:65
  184.3 166.3 %reduce-scatter.4.cloned.1.call-start = ((), (), s32[]{:S(2)}) async-start(), calls=%async_computation.6 | async-start | bytes 2621440 | tf_op jit(solution)/shard_map/reduce_scatter | solution.py:1234
  184.3 13.4 %collective-permute-start.22 = (bf16[192,1024]{1,0:T(8,128)(2,1)S(1)}, bf16[192,1024]{1,0:T(8,128)(2,1)}, u32[]{:S(2)}, u32[]{:S(2)}) collective-permute-start(bf16[192,1024]{1,0:T(8,128)(2,1)S(1)} %get-tuple-element.275.a_ref), channel_id=1, source_target_pairs={{0,1},{1,0},{2,3},{3,2},{4,5},{5,4},{6,7},{7,6},{8,9},{9,8},{10,11... | collective-permute-start | bytes 1179656 | tf_op jit(solution)/shard_map/ppermute | solution.py:65
  184.4 13.3 %collective-permute-start.23 = (bf16[192,1024]{1,0:T(8,128)(2,1)S(1)}, bf16[192,1024]{1,0:T(8,128)(2,1)}, u32[]{:S(2)}, u32[]{:S(2)}) collective-permute-start(bf16[192,1024]{1,0:T(8,128)(2,1)S(1)} %get-tuple-element.275.a_ref), channel_id=1, source_target_pairs={{0,4},{4,0},{1,5},{5,1},{2,6},{6,2},{3,7},{7,3},{8,12},{12,8},{9,1... | collective-permute-start | bytes 1179656 | tf_op jit(solution)/shard_map/ppermute | solution.py:61
  200.2 15.8 %collective-permute-start.26 = (bf16[192,1024]{1,0:T(8,128)(2,1)S(1)}, bf16[192,1024]{1,0:T(8,128)(2,1)S(1)}, u32[]{:S(2)}, u32[]{:S(2)}) collective-permute-start(bf16[192,1024]{1,0:T(8,128)(2,1)S(1)} %add_convert_fusion.7), channel_id=1, source_target_pairs={{0,1},{1,0},{2,3},{3,2},{4,5},{5,4},{6,7},{7,6},{8,9},{9,8},{10,11... | collective-permute-start | bytes 1179656 | tf_op jit(solution)/shard_map/ppermute | solution.py:65
  219.5 19.0 %collective-permute-start.29 = (bf16[192,1024]{1,0:T(8,128)(2,1)}, bf16[192,1024]{1,0:T(8,128)(2,1)S(1)}, u32[]{:S(2)}, u32[]{:S(2)}) collective-permute-start(bf16[192,1024]{1,0:T(8,128)(2,1)} %add_convert_fusion.6), channel_id=1, source_target_pairs={{0,1},{1,0},{2,3},{3,2},{4,5},{5,4},{6,7},{7,6},{8,9},{9,8},{10,11... | collective-permute-start | bytes 1179656 | tf_op jit(solution)/shard_map/ppermute | solution.py:65
  221.3 17.2 %collective-permute-start.30 = (bf16[192,1024]{1,0:T(8,128)(2,1)}, bf16[192,1024]{1,0:T(8,128)(2,1)S(1)}, u32[]{:S(2)}, u32[]{:S(2)}) collective-permute-start(bf16[192,1024]{1,0:T(8,128)(2,1)} %get-tuple-element.284.a_ref), channel_id=1, source_target_pairs={{0,4},{4,0},{1,5},{5,1},{2,6},{6,2},{3,7},{7,3},{8,12},{12,8},{9,1... | collective-permute-start | bytes 1179656 | tf_op jit(solution)/shard_map/ppermute | solution.py:61
  221.5 25.5 %collective-permute-start.31 = (bf16[192,1024]{1,0:T(8,128)(2,1)}, bf16[192,1024]{1,0:T(8,128)(2,1)}, u32[]{:S(2)}, u32[]{:S(2)}) collective-permute-start(bf16[192,1024]{1,0:T(8,128)(2,1)} %get-tuple-element.284.a_ref), channel_id=1, source_target_pairs={{0,1},{1,0},{2,3},{3,2},{4,5},{5,4},{6,7},{7,6},{8,9},{9,8},{10,11... | collective-permute-start | bytes 1179656 | tf_op jit(solution)/shard_map/ppermute | solution.py:65
  269.7 13.1 %collective-permute-start.39 = (f32[8,768]{1,0:T(8,128)S(1)}, f32[8,768]{1,0:T(8,128)S(1)}, u32[]{:S(2)}, u32[]{:S(2)}) collective-permute-start(f32[8,768]{1,0:T(8,128)S(1)} %get-tuple-element.309.here_ref), channel_id=1, source_target_pairs={{0,4},{4,0},{1,5},{5,1},{2,6},{6,2},{3,7},{7,3},{8,12},{12,8},{9,1... | collective-permute-start | bytes 73736 | tf_op jit(solution)/shard_map/ppermute | solution.py:61
  313.6 113.4 %reduce-scatter.6.cloned.1.call-start = ((), (), s32[]{:S(2)}) async-start(), calls=%async_computation.7 | async-start | bytes 5242880 | tf_op jit(solution)/shard_map/reduce_scatter | solution.py:1234
  389.5 23.8 %collective-permute-start.61 = (bf16[256,512]{1,0:T(8,128)(2,1)S(1)}, bf16[256,512]{1,0:T(8,128)(2,1)S(1)}, u32[]{:S(2)}, u32[]{:S(2)}) collective-permute-start(bf16[256,512]{1,0:T(8,128)(2,1)S(1)} %select_bitcast_fusion.1), channel_id=1, source_target_pairs={{0,2},{2,0},{1,3},{3,1},{4,6},{6,4},{5,7},{7,5},{8,10},{10,8},{9,1... | collective-permute-start | bytes 786440 | tf_op jit(solution)/shard_map/ppermute | solution.py:69
  391.9 21.4 %collective-permute-start.59 = (bf16[192,1024]{1,0:T(8,128)(2,1)S(1)}, bf16[192,1024]{1,0:T(8,128)(2,1)}, u32[]{:S(2)}, u32[]{:S(2)}) collective-permute-start(bf16[192,1024]{1,0:T(8,128)(2,1)S(1)} %get-tuple-element.384.pa_ref), channel_id=1, source_target_pairs={{0,1},{1,0},{2,3},{3,2},{4,5},{5,4},{6,7},{7,6},{8,9},{9,8},{10,11... | collective-permute-start | bytes 1179656 | tf_op jit(solution)/shard_map/ppermute | solution.py:65
  392.8 20.6 %collective-permute-start.60 = (bf16[192,1024]{1,0:T(8,128)(2,1)S(1)}, bf16[192,1024]{1,0:T(8,128)(2,1)S(1)}, u32[]{:S(2)}, u32[]{:S(2)}) collective-permute-start(bf16[192,1024]{1,0:T(8,128)(2,1)S(1)} %get-tuple-element.384.pa_ref), channel_id=1, source_target_pairs={{0,4},{4,0},{1,5},{5,1},{2,6},{6,2},{3,7},{7,3},{8,12},{12,8},{9,1... | collective-permute-start | bytes 1179656 | tf_op jit(solution)/shard_map/ppermute | solution.py:61
  416.4 14.3 %collective-permute-start.63 = (bf16[192,1024]{1,0:T(8,128)(2,1)}, bf16[192,1024]{1,0:T(8,128)(2,1)S(1)}, u32[]{:S(2)}, u32[]{:S(2)}) collective-permute-start(bf16[192,1024]{1,0:T(8,128)(2,1)} %collective-permute-done.59.pb_ref), channel_id=1, source_target_pairs={{0,4},{4,0},{1,5},{5,1},{2,6},{6,2},{3,7},{7,3},{8,12},{12,8},{9,1... | collective-permute-start | bytes 1179656 | tf_op jit(solution)/shard_map/ppermute | solution.py:61
  417.5 40.8 %collective-permute-start.64 = (bf16[192,1024]{1,0:T(8,128)(2,1)}, bf16[192,1024]{1,0:T(8,128)(2,1)}, u32[]{:S(2)}, u32[]{:S(2)}) collective-permute-start(bf16[192,1024]{1,0:T(8,128)(2,1)} %add_convert_fusion.1), channel_id=1, source_target_pairs={{0,1},{1,0},{2,3},{3,2},{4,5},{5,4},{6,7},{7,6},{8,9},{9,8},{10,11... | collective-permute-start | bytes 1179656 | tf_op jit(solution)/shard_map/ppermute | solution.py:65
  428.2 30.1 %collective-permute-start.65 = (bf16[256,1024]{1,0:T(8,128)(2,1)S(1)}, bf16[256,1024]{1,0:T(8,128)(2,1)S(1)}, u32[]{:S(2)}, u32[]{:S(2)}) collective-permute-start(bf16[256,1024]{1,0:T(8,128)(2,1)S(1)} %broadcast_select_fusion), channel_id=1, source_target_pairs={{0,2},{2,0},{1,3},{3,1},{4,6},{6,4},{5,7},{7,5},{8,10},{10,8},{9,1... | collective-permute-start | bytes 1572872 | tf_op jit(solution)/shard_map/ppermute | solution.py:69
  466.3 13.0 %collective-permute-start.67 = (bf16[192,1024]{1,0:T(8,128)(2,1)S(1)}, bf16[192,1024]{1,0:T(8,128)(2,1)S(1)}, u32[]{:S(2)}, u32[]{:S(2)}) collective-permute-start(bf16[192,1024]{1,0:T(8,128)(2,1)S(1)} %add_convert_fusion), channel_id=1, source_target_pairs={{0,1},{1,0},{2,3},{3,2},{4,5},{5,4},{6,7},{7,6},{8,9},{9,8},{10,11... | collective-permute-start | bytes 1179656 | tf_op jit(solution)/shard_map/ppermute | solution.py:65
  487.6 43.5 %reduce-scatter.8.cloned.1.call-start = ((), (), s32[]{:S(2)}) async-start(), calls=%async_computation.8 | async-start | bytes 2621440 | tf_op jit(solution)/shard_map/reduce_scatter | solution.py:1234
  500.2 34.5 %collective-permute-start.84 = (f32[48,128]{1,0:T(8,128)S(1)}, f32[48,128]{1,0:T(8,128)S(1)}, u32[]{:S(2)}, u32[]{:S(2)}) collective-permute-start(f32[48,128]{1,0:T(8,128)S(1)} %add.346), channel_id=1, source_target_pairs={{0,2},{2,0},{1,3},{3,1},{4,6},{6,4},{5,7},{7,5},{8,10},{10,8},{9,1... | collective-permute-start | bytes 73736 | tf_op jit(solution)/shard_map/ppermute | solution.py:69
  506.7 27.9 %collective-permute-start.81 = (bf16[16,4096]{1,0:T(8,128)(2,1)S(1)}, bf16[16,4096]{1,0:T(8,128)(2,1)S(1)}, u32[]{:S(2)}, u32[]{:S(2)}) collective-permute-start(bf16[16,4096]{1,0:T(8,128)(2,1)S(1)} %maximum_select_fusion.14), channel_id=1, source_target_pairs={{0,24},{8,16},{16,8},{24,0},{1,25},{9,17},{17,9},{25,1},{2,26},{10... | collective-permute-start | bytes 393224 | tf_op jit(solution)/shard_map/ppermute | solution.py:77
  532.1 14.6 %collective-permute-start.68 = (bf16[256,512]{1,0:T(8,128)(2,1)S(1)}, bf16[256,512]{1,0:T(8,128)(2,1)S(1)}, u32[]{:S(2)}, u32[]{:S(2)}) collective-permute-start(bf16[256,512]{1,0:T(8,128)(2,1)S(1)} %broadcast_select_fusion.3), channel_id=1, source_target_pairs={{0,2},{2,0},{1,3},{3,1},{4,6},{6,4},{5,7},{7,5},{8,10},{10,8},{9,1... | collective-permute-start | bytes 786440 | tf_op jit(solution)/shard_map/ppermute | solution.py:69
  534.6 13.4 %collective-permute-start.82 = (bf16[64,4096]{1,0:T(8,128)(2,1)S(1)}, bf16[64,4096]{1,0:T(8,128)(2,1)S(1)}, u32[]{:S(2)}, u32[]{:S(2)}) collective-permute-start(bf16[64,4096]{1,0:T(8,128)(2,1)S(1)} %bitcast.240), channel_id=1, source_target_pairs={{0,4},{4,0},{1,5},{5,1},{2,6},{6,2},{3,7},{7,3},{8,12},{12,8},{9,1... | collective-permute-start | bytes 1572872 | tf_op jit(solution)/shard_map/ppermute | solution.py:61
  (340 other events, 2823.4 us)
Sparse Core Ops, SparseCore 0:
  94.3 78.5 all-gather.3
  184.4 53.3 all-gather.5
  313.7 35.1 reduce-scatter.3
  374.0 52.9 reduce-scatter.5
  491.6 39.3 reduce-scatter.7

commit v2 on v1

--- a/solution.py
+++ b/solution.py
@@ -24,6 +24,7 @@
     "row_layout": 2, "enter": 5, "enter_first": 6, "attend": 11, "onward": 4, "feed": 9, "head": 6, "merge": 2,
     "head_back": 5, "back": 5, "feed_back": 7, "attend_back": 16, "old_stats": 4, "row_stats": 3,
     "column_stats": 5, "finish": 2, "head_grad": 6, "feed_grad": 12, "first_grad": 6,
+    "renew": 8, "arrange": 4,
 }
 DP = ("g", "c")
 MP = ("h", "l")
@@ -209,6 +210,59 @@
         cost_estimate=cost("row_layout"),
         name="row_layout",
     )(level_weight, segment, live)
+
+
+def arrange_kernel(at_ref, mine_ref, other_ref, vq_ref, vq_other_ref, *refs):
+    quarter = mine_ref.shape[2] // 4
+    cols_s, vq_s = refs[-2:]
+    use_mine, at_c, at_l = at_ref[0], at_ref[1], at_ref[2]
+    n = 4 * quarter
+    lane = lax.broadcasted_iota(jnp.int32, (n, 128), 1)
+    for r in range(2):
+        feat_ref, hot_ref, col_ref, row_ref = refs[4 * r : 4 * r + 4]
+        info = jnp.where(use_mine == 1, mine_ref[r], other_ref[r])
+        cols_s[...] = jnp.concatenate([info, jnp.zeros((124, n), full_type)], 0).T
+        vq_s[...] = jnp.where(use_mine == 1, full(vq_ref[r]), full(vq_other_ref[r]))
+        cols, vqs = [], []
+        for k in range(4):
+            start = jnp.bitwise_xor(at_c, k // 2) * 2 + jnp.bitwise_xor(at_l, k % 2)
+            rows = pl.ds(pl.multiple_of(start * quarter, quarter), quarter)
+            cols.append(cols_s[rows, :])
+            vqs.append(vq_s[rows, :])
+        cols = jnp.concatenate(cols, 0)
+        code, place, live, weight = (cols[:, k : k + 1] for k in range(4))
+        segment = jnp.floor(place * (1.0 / 16.0))
+        base = segment * 16.0
+        key = jnp.where(live > 0.0, place, 1048576.0)
+        out = jnp.zeros((n, 128), full_type)
+        for k, column in enumerate((place, base, key, code, weight)):
+            out = jnp.where(lane == k, column, out)
+        col_ref[...] = out
+        row_ref[...] = out.T[0:8, :]
+        spot = lax.broadcasted_iota(jnp.int32, (n, 16), 1)
+        hit = (full(spot % 4) == segment) & (spot < 12)
+        hot_ref[...] = low(jnp.where(hit, 1.0, 0.0))
+        code_dim, padded = vq_ref.shape[2], feat_ref.shape[1]
+        spread = lax.broadcasted_iota(jnp.int32, (code_dim, padded), 0) == lax.broadcasted_iota(
+            jnp.int32, (code_dim, padded), 1
+        )
+        feats = dot_nn(low(jnp.concatenate(vqs, 0)), low(jnp.where(spread, 1.0, 0.0)))
+        level = lax.broadcasted_iota(jnp.int32, (n, padded), 1) - code_dim
+        feat_ref[...] = low(feats + jnp.where(full(level) == place - base, 1.0, 0.0))
+
+
+def arrange(at, mine, other, vq, vq_other, padded):
+    n, code_dim = vq.shape[1:]
+    shapes = [((n, padded), low_type), ((n, 16), low_type), ((n, 128), full_type), ((8, n), full_type)] * 2
+    return pl.pallas_call(
+        arrange_kernel,
+        in_specs=[pl.BlockSpec(memory_space=pltpu.SMEM)] + [pl.BlockSpec(memory_space=pltpu.VMEM)] * 4,
+        out_shape=[jax.ShapeDtypeStruct(shape, dtype) for shape, dtype in shapes],
+        scratch_shapes=[pltpu.VMEM((n, 128), full_type), pltpu.VMEM((n, code_dim), full_type)],
+        compiler_params=pltpu.CompilerParams(vmem_limit_bytes=48 * 2**20),
+        cost_estimate=cost("arrange"),
+        name="arrange",
+    )(at, mine, other, vq, vq_other)
 
 
 def enter_tile(feat_ref, table_ref, hot_ref, w, in_ref, qkv_ref, stream_ref, parts_s):
@@ -408,29 +462,33 @@
 
 def column_half(shape, number):
     return pl.BlockSpec(
-        shape[:2] + (shape[2] // 2,), lambda i: (0, 0, number), pipeline_mode=pl.Buffered(1)
-    )
+        shape[:3] + (shape[3] // 2,), lambda i: (0, 0, 0, number), pipeline_mode=pl.Buffered(1)
+    )
+
+
+def block_of(ref, h):
+    return ref[:, h].reshape(-1, ref.shape[3])
 
 
 def feed_kernel(a_ref, b_ref, c_ref, d_ref, one_ref, two_ref, row_ref, act_ref, slope_ref, top_ref, bottom_ref):
     given = either(a_ref, b_ref, c_ref, d_ref)
     row_ref[...] = given
-    units = one_ref.shape[2]
+    units = one_ref.shape[3]
     total = None
     for h in range(2):
         at = slice(h * units, (h + 1) * units)
-        act, slope = gelu_parts(dot_nn(given, one_ref[h]))
+        act, slope = gelu_parts(dot_nn(given, block_of(one_ref, h)))
         act = low(act)
         act_ref[:, at] = act
         slope_ref[:, at] = slope
-        part = dot_nt(act, two_ref[h])
+        part = dot_nt(act, block_of(two_ref, h))
         total = part if total is None else total + part
     put(low(total), top_ref, bottom_ref)
 
 
 def feed(pieces, both):
     tile, width = 2 * pieces[0].shape[0], pieces[0].shape[1]
-    units = both.shape[2]
+    units = both.shape[3]
     return call(
         feed_kernel,
         (2,),
@@ -446,20 +504,20 @@
 def feed_back_kernel(a_ref, b_ref, c_ref, d_ref, slope_ref, one_ref, two_ref, row_ref, dh_ref, top_ref, bottom_ref):
     given = either(a_ref, b_ref, c_ref, d_ref)
     row_ref[...] = given
-    units = one_ref.shape[2]
+    units = one_ref.shape[3]
     total = None
     for h in range(2):
         at = slice(h * units, (h + 1) * units)
-        d_hidden = low(dot_nn(given, two_ref[h]) * slope_ref[:, at])
+        d_hidden = low(dot_nn(given, block_of(two_ref, h)) * slope_ref[:, at])
         dh_ref[:, at] = d_hidden
-        part = dot_nt(d_hidden, one_ref[h])
+        part = dot_nt(d_hidden, block_of(one_ref, h))
         total = part if total is None else total + part
     put(low(total), top_ref, bottom_ref)
 
 
 def feed_back(pieces, slope, both):
     tile, width = 2 * pieces[0].shape[0], pieces[0].shape[1]
-    units = both.shape[2]
+    units = both.shape[3]
     return call(
         feed_back_kernel,
         (2,),
@@ -474,11 +532,11 @@
 def head_kernel(a_ref, b_ref, c_ref, d_ref, w_ref, code_ref, column_ref, row_ref, logit_ref, stat_ref):
     given = either(a_ref, b_ref, c_ref, d_ref)
     row_ref[...] = given
-    logits = jnp.concatenate([dot_nn(given, w_ref[h]) for h in range(2)], 1)
+    logits = jnp.concatenate([dot_nn(given, block_of(w_ref, h)) for h in range(2)], 1)
     logit_ref[...] = logits
     peak = jnp.max(logits, 1, keepdims=True)
     total = jnp.sum(jnp.exp(logits - peak), 1, keepdims=True)
-    picked = jnp.sum(jnp.where(code_ref[...] == column_ref[...], logits, 0.0), 1, keepdims=True)
+    picked = jnp.sum(jnp.where(code_ref[:, 3:4] == column_ref[...], logits, 0.0), 1, keepdims=True)
     lane = lax.broadcasted_iota(jnp.int32, (logits.shape[0], 128), 1)
     turned = jnp.where(lane == 0, peak, jnp.where(lane == 1, total, picked)).T
     stat_ref[...] = turned[0:8, :]
@@ -486,11 +544,11 @@
 
 def head(pieces, w, code, column):
     tile, width = 2 * pieces[0].shape[0], pieces[0].shape[1]
-    units = 2 * w.shape[2]
+    units = 2 * w.shape[3]
     return call(
         head_kernel,
         (2,),
-        [whole(pieces[0].shape)] * 4 + [whole(w.shape), tiled(tile, 1), whole((1, units))],
+        [whole(pieces[0].shape)] * 4 + [whole(w.shape), tiled(tile, 128), whole((1, units))],
         [tiled(tile, width), tiled(tile, units), pl.BlockSpec((8, tile), lambda i: (0, i))],
         [((2 * tile, width), low_type), ((2 * tile, units), full_type), ((8, 2 * tile), full_type)],
         [],
@@ -514,7 +572,7 @@
     total = sum(part[1:2] * jnp.exp(part[0:1] - peak) for part in parts)
     picked = sum(part[2:3] for part in parts)
     log_total = peak + jnp.log(total)
-    weight = weight_ref[...]
+    weight = weight_ref[4:5, :]
     spot = lax.broadcasted_iota(jnp.int32, (1, 2 * half), 1)
     loss = jnp.where(spot < half // 2, weight * (log_total - picked), 0.0)
     loss_ref[...] = jnp.broadcast_to(jnp.sum(loss, 1, keepdims=True), loss_ref.shape)
@@ -534,23 +592,23 @@
 
 
 def head_back_kernel(logit_ref, w_ref, code_ref, column_ref, line_ref, d_ref, top_ref, bottom_ref):
-    hit = jnp.where(code_ref[...] == column_ref[...], 1.0, 0.0)
+    hit = jnp.where(code_ref[:, 3:4] == column_ref[...], 1.0, 0.0)
     line = line_ref[...]
     d_logits = low(line[:, 1:2] * (jnp.exp(logit_ref[...] - line[:, 0:1]) - hit))
     d_ref[...] = d_logits
-    units = w_ref.shape[2]
-    total = dot_nt(d_logits[:, :units], w_ref[0]) + dot_nt(d_logits[:, units:], w_ref[1])
+    units = w_ref.shape[3]
+    total = dot_nt(d_logits[:, :units], block_of(w_ref, 0)) + dot_nt(d_logits[:, units:], block_of(w_ref, 1))
     put(low(total), top_ref, bottom_ref)
 
 
 def head_back(logits, w, code, column, lines):
     n, units = logits.shape
-    width = w.shape[1]
+    width = w.shape[0] * w.shape[2]
     tile = n // 2
     return call(
         head_back_kernel,
         (2,),
-        [tiled(tile, units), whole(w.shape), tiled(tile, 1), whole((1, units)), tiled(tile, 128)],
+        [tiled(tile, units), whole(w.shape), tiled(tile, 128), whole((1, units)), tiled(tile, 128)],
         [tiled(tile, units), fixed((tile, width)), fixed((tile, width))],
         [((n, units), low_type)] + [((tile, width), low_type)] * 2,
         [],
@@ -750,31 +808,132 @@
     )(at_c[None], row_new, old, tail, tables_sum, scales, *gradients)
 
 
-def finish_kernel(flat_ref, old_ref, col_ref, sum_ref, *, decay, width, starts):
+def spot_of(line, k):
+    spots = lax.broadcasted_iota(jnp.int32, line.shape, 1)
+    return jnp.sum(jnp.where(spots == k, line, 0.0), 1, keepdims=True)
+
+
+def finish_kernel(
+    flat_ref, old_ref, scale_ref, col_ref, part_ref, own_ref, second_ref, step_ref, *, decay, width, starts
+):
     columns = old_ref.shape[1]
     line = flat_ref[0:1, columns:]
     new = decay * old_ref[...] + (1.0 - decay) * (flat_ref[0:1, :columns] / width)
     col_ref[...] = new
     ratio = flat_ref[1:2, :columns] / new
     spots = lax.broadcasted_iota(jnp.int32, (1, 128), 1)
-    out = jnp.zeros((1, 128), full_type)
+    scales = (spots >= 11) & (spots < 15)
+    gradient = jnp.where(scales, line, 0.0)
+    second = decay * scale_ref[...] + (1.0 - decay) * (gradient * gradient + eps_one)
+    step = gradient * lax.rsqrt(second)
+    second_ref[...] = second
+    step_ref[...] = step
+    out = jnp.where(spots == 7, jnp.sum(step * step, 1, keepdims=True), 0.0)
     for k in range(6):
-        mean = jnp.sum(jnp.where(spots == k, line, 0.0), 1, keepdims=True) / width
-        value = jnp.sum(ratio[:, starts[k] : starts[k + 1]], 1, keepdims=True) * mean
-        out = jnp.where(spots == k, value, out)
-    sum_ref[...] = out
-
-
-def finish(flat, col_old, decay, width, starts):
+        value = jnp.sum(ratio[:, starts[k] : starts[k + 1]], 1, keepdims=True) * (spot_of(line, k) / width)
+        if k == 5:
+            own_ref[...] = jnp.where(spots == 5, value, 0.0)
+        else:
+            out = jnp.where(spots == k, value, out)
+    part_ref[...] = out
+
+
+def finish(flat, col_old, scale_line, decay, width, starts):
     return pl.pallas_call(
         functools.partial(finish_kernel, decay=decay, width=width, starts=starts),
-        out_shape=[
-            jax.ShapeDtypeStruct(col_old.shape, full_type),
-            jax.ShapeDtypeStruct((1, 128), full_type),
-        ],
+        out_shape=[jax.ShapeDtypeStruct(col_old.shape, full_type)]
+        + [jax.ShapeDtypeStruct((1, 128), full_type)] * 4,
         cost_estimate=cost("finish"),
         name="finish",
-    )(flat, col_old)
+    )(flat, col_old, scale_line)
+
+
+def renew_kernel(
+    line_ref, part_ref, own_ref, early_ref, rows_ref, col_ref, ada_col_ref,
+    qkv_g, proj_g, one_g, two_g, head_g, ada_g, step_ref, scale_step_ref,
+    qkv_ref, proj_ref, one_ref, two_ref, head_ref, ada_ref, tab_ref, scale_ref,
+    qkv_out, proj_out, one_out, two_out, head_out, ada_out, tab_out, scale_out, proj_turned, two_turned,
+    *, width, entries, starts
+):
+    n = one_g.shape[0]
+    line, part = line_ref[...], part_ref[...]
+
+    def factor(k):
+        step = spot_of(own_ref[...], 5) if k == 5 else spot_of(line, 10) if k == 6 else spot_of(part, k)
+        weight = spot_of(early_ref[...], 21) if k == 7 else spot_of(line, {5: 8, 6: 9}.get(k, 16 + k))
+        ratio = jnp.sqrt(step / entries[k]) / clip_rms
+        spread = jnp.maximum(eps_two, jnp.sqrt(weight / entries[k]))
+        return rate_step * spread / jnp.maximum(1.0, ratio)
+
+    def row(k):
+        rows = jnp.concatenate([rows_ref[k : k + 1, :], jnp.zeros((127, n), full_type)], 0)
+        return rows.T[:, 0:1]
+
+    def change(k, gradient, columns):
+        mean = spot_of(line, k) / width
+        return factor(k) * (gradient * lax.rsqrt(row(k) * columns / mean))
+
+    ada_out[...] = ada_ref[...] - change(5, ada_g[...], ada_col_ref[...])
+    at = pl.program_id(0)
+
+    @pl.when(at == 0)
+    def _():
+        size = qkv_g.shape[2]
+        for c in range(3):
+            qkv_out[c] = qkv_ref[c] - change(0, qkv_g[c], col_ref[:, c * size : (c + 1) * size])
+
+    @pl.when(at == 1)
+    def _():
+        gradient = proj_g[...]
+        proj_turned[...] = gradient.T
+        proj_out[...] = proj_ref[...] - change(1, gradient, col_ref[:, starts[1] : starts[2]]).T
+        scale_out[...] = scale_ref[...] - factor(7) * scale_step_ref[...]
+
+    @pl.when(at == 2)
+    def _():
+        one_out[...] = one_ref[...] - change(2, one_g[...], col_ref[:, starts[2] : starts[3]])
+
+    @pl.when(at == 3)
+    def _():
+        gradient = two_g[...]
+        two_turned[...] = gradient.T
+        two_out[...] = two_ref[...] - change(3, gradient, col_ref[:, starts[3] : starts[4]]).T
+
+    @pl.when(at == 4)
+    def _():
+        head_out[...] = head_ref[...] - change(4, head_g[...], col_ref[:, starts[4] : starts[5]])
+
+    @pl.when(at == 5)
+    def _():
+        tab_out[...] = tab_ref[...] - factor(6) * step_ref[...]
+
+
+def renew(lines, rows, columns, grads, steps, olds, width, entries, starts):
+    n, tile = grads[2].shape[0], 1024
+    ada = pl.BlockSpec((n, tile), lambda i: (0, i))
+    first = starts[5] // tile
+
+    def wholes(arrays):
+        return [whole(a.shape) for a in arrays]
+
+    outs = [a.shape for a in olds] + [olds[1].shape, olds[3].shape]
+    out_specs = [ada if k == 5 else fixed(shape) for k, shape in enumerate(outs)]
+    return call(
+        functools.partial(renew_kernel, width=width, entries=entries, starts=starts),
+        (olds[5].shape[1] // tile,),
+        wholes(lines)
+        + [whole(rows.shape), whole(columns.shape), pl.BlockSpec((1, tile), lambda i: (0, first + i))]
+        + wholes(grads[:5])
+        + [ada]
+        + wholes(steps)
+        + wholes(olds[:5])
+        + [ada]
+        + wholes(olds[6:]),
+        out_specs,
+        [(shape, full_type) for shape in outs],
+        [],
+        "renew",
+    )(*lines, rows, columns, columns, *grads, *steps, *olds)
 
 
 def head_lanes(shape):
@@ -788,7 +947,7 @@
 
 
 def attend_kernel(
-    q_ref, k_ref, v_ref, gain_ref, cq_ref, sq_ref, ck_ref, proj_ref,
+    q_ref, k_ref, v_ref, gain_ref, col_ref, row_ref, proj_ref,
     mix_ref, lse_ref, top_ref, bottom_ref, q_s, k_s, v_s, bias_s, sum_s
 ):
     length = q_ref.shape[0]
@@ -802,15 +961,15 @@
     k_s[...] = low(key * (lax.rsqrt(per_head(key * key, first) / 64.0 + eps_norm) * 0.125))
     v_s[...] = low(v_ref[...])
     first_t = head_lanes((tile, 128))
-    ck = ck_ref[...]
 
     @pl.when(pl.program_id(0) == 0)
     def _():
+        ck = row_ref[2:3, :]
         for i in range(2):
             rows = slice(i * tile, (i + 1) * tile)
             shape = (tile, length)
             here = lax.broadcasted_iota(jnp.int32, shape, 1) - lax.broadcasted_iota(jnp.int32, shape, 0)
-            keep = ((ck <= cq_ref[rows, :]) & (ck >= sq_ref[rows, :])) | (here == i * tile)
+            keep = ((ck <= col_ref[rows, 0:1]) & (ck >= col_ref[rows, 1:2])) | (here == i * tile)
             bias_s[rows, :] = jnp.where(keep, 0.0, -1e30)
         sum_s[...] = jnp.zeros_like(sum_s)
 
@@ -839,11 +998,10 @@
             out_ref[...] = low(part)
 
 
-def attend(qkv, gain, cq, sq, ck, proj):
+def attend(qkv, gain, cols, rows, proj):
     length = qkv.shape[0]
     pairs = qkv.shape[1] // 384
     width = proj.shape[0]
-    column = pl.BlockSpec((length, 1), lambda p: (0, 0))
     block = pl.BlockSpec((length, 128), lambda p: (0, p))
     return call(
         attend_kernel,
@@ -853,9 +1011,8 @@
             pl.BlockSpec((length, 128), lambda p: (0, pairs + p)),
             pl.BlockSpec((length, 128), lambda p: (0, 2 * pairs + p)),
             pl.BlockSpec((1, 128), lambda p: (0, p)),
-            column,
-            column,
-            pl.BlockSpec((1, length), lambda p: (0, 0)),
+            whole((length, 128)),
+            whole((8, length)),
             pl.BlockSpec((width, 128), lambda p: (0, p)),
         ],
         [block, pl.BlockSpec((1, 2, length), lambda p: (p, 0, 0))] + [fixed((length // 2, width))] * 2,
@@ -864,11 +1021,11 @@
         [pltpu.VMEM((length, 128), low_type)] * 3
         + [pltpu.VMEM((length, length), full_type), pltpu.VMEM((length, width), full_type)],
         "attend",
-    )(qkv, qkv, qkv, gain, cq[:, None], sq[:, None], ck[None, :], proj)
+    )(qkv, qkv, qkv, gain, cols, rows, proj)
 
 
 def attend_back_kernel(
-    q_ref, k_ref, v_ref, gain_ref, cq_ref, sq_ref, ck_ref, lse_ref, pa_ref, pb_ref, pc_ref, pd_ref,
+    q_ref, k_ref, v_ref, gain_ref, col_ref, line_ref, lse_ref, pa_ref, pb_ref, pc_ref, pd_ref,
     proj_ref, wq_ref, wk_ref, wv_ref, row_ref, d_ref, ds_ref, top_ref, bottom_ref,
     q_s, k_s, v_s, dm_ref, dqa, dka, dva, sum_s, *, tile
 ):
@@ -896,7 +1053,7 @@
     dka[...] = jnp.zeros_like(dka)
     dva[...] = jnp.zeros_like(dva)
     first_t = head_lanes((tile, 128))
-    ck = ck_ref[...]
+    ck = col_ref[:, 2:3]
 
     def step(i, carry):
         rows = pl.ds(pl.multiple_of(i * tile, tile), tile)
@@ -904,7 +1061,7 @@
         dmix_t = dm_ref[rows, :]
         shape = (length, tile)
         here = lax.broadcasted_iota(jnp.int32, shape, 0) - lax.broadcasted_iota(jnp.int32, shape, 1)
-        keep = ((ck <= cq_ref[:, rows]) & (ck >= sq_ref[:, rows])) | (here == i * tile)
+        keep = ((ck <= line_ref[0:1, rows]) & (ck >= line_ref[1:2, rows])) | (here == i * tile)
         d_query = []
         for head in range(2):
             chosen = first_t if head == 0 else ~first_t
@@ -954,11 +1111,10 @@
             out_ref[...] = low(part)
 
 
-def attend_back(qkv, gain, cq, sq, ck, lse, pieces, proj, w):
+def attend_back(qkv, gain, cols, rows, lse, pieces, proj, w):
     length = qkv.shape[0]
     pairs = qkv.shape[1] // 384
     width = proj.shape[0]
-    row = pl.BlockSpec((1, length), lambda p: (0, 0))
 
     def part(rows, number):
         return pl.BlockSpec((rows, 128), lambda p: (0, number * pairs + p))
@@ -971,9 +1127,8 @@
             part(length, 1),
             part(length, 2),
             pl.BlockSpec((1, 128), lambda p: (0, p)),
-            row,
-            row,
-            pl.BlockSpec((length, 1), lambda p: (0, 0)),
+            whole((length, 128)),
+            whole((8, length)),
             pl.BlockSpec((1, 2, length), lambda p: (p, 0, 0)),
         ]
         + [whole(pieces[0].shape)] * 4
@@ -996,7 +1151,7 @@
         + [pltpu.VMEM((length, 128), full_type)] * 3
         + [pltpu.VMEM((length, width), full_type)],
         "attend_back",
-    )(qkv, qkv, qkv, gain, cq[None, :], sq[None, :], ck[:, None], lse, *pieces, proj, w, w, w)
+    )(qkv, qkv, qkv, gain, cols, rows, lse, *pieces, proj, w, w, w)
 
 
 def body(
@@ -1027,7 +1182,6 @@
 
     first_mine, first_other = halves(jnp.concatenate([qkv_w, proj_w.T[None]], 0))
     first_near = ordered(at_c, first_mine, over_c(first_other), 1)
-    first_far = over_h(first_near)
 
     place, weight, weight_here = row_layout(level_weight, segment, live)
     weight_here = weight_here[0, 0]
@@ -1042,7 +1196,9 @@
     note = jnp.pad(low(note), (0, (lead_pad - lead) * slice_width - note.shape[0]))
     note = note.reshape(lead_pad - lead, slice_width)
     packed = tie(jnp.concatenate([tables_low[:lead], note], 0), first_near)
-    gathered = lax.all_gather(packed, DP, axis=0)
+    gathered, first_far = lax.optimization_barrier(
+        (lax.all_gather(packed, DP, axis=0), over_h(first_near))
+    )
     lead_table = jnp.transpose(gathered, (1, 0, 2)).reshape(lead_pad, width)
     notes = gathered[:, lead : lead + note_rows].reshape(dp_count, -1).astype(jnp.int32)
     labels_all = (notes[:, :per_row] * 32 + notes[:, per_row : 2 * per_row]).reshape(-1)
@@ -1068,50 +1224,23 @@
     left, right = mod_part[:, :mod_half], mod_part[:, mod_half:]
     mod_send = jnp.where(at_c == 0, right, left)
     mod_sum = jnp.where(at_c == 0, left, right) + over_c(mod_send)
+    mod_first = mod_sum
     mod_sum = scatter_g(mod_sum)
     mod_items = ordered(at_c, mod_sum, over_c(mod_sum), 1).reshape(row_count, item_count, 8, width)
     mod_rows = jnp.transpose(mod_items, (0, 2, 1, 3))
 
-    codes, place, live, weight, vq_in, head_gain = tie(
-        (codes, place, live, weight, vq_in, head_scale), gathered
-    )
-    fc1_wide, fc2_wide, head_wide = tie((fc1_w, fc2_w, head_w), mod_send)
-    qkv_piece = ordered(at_h, first_near[None], first_far[None], 0)
-    qkv_pieces = [qkv_piece] + [over_g(qkv_piece, k) for k in range(1, 4)]
+    fc1_wide, fc2_wide = tie((fc1_w, fc2_w), mod_send)
 
     def near_rows(w):
         kept, other = halves(w)
         return ordered(at_c, kept, over_c(other), 0)
 
     def gathered_weight(a):
-        return lax.all_gather(a, ("h", "g"), axis=0, tiled=True).reshape(2, width, -1)
+        wide = lax.all_gather(a.reshape(-1, a.shape[2]), "g", axis=0, tiled=True)
+        return wide.reshape((g_count,) + a.shape)
 
     feed_near = jnp.concatenate([near_rows(fc1_wide), near_rows(fc2_wide.T)], 1)
-    head_near = near_rows(head_wide)
-
-    mine = at_c == at_h
-    info = jnp.stack([codes, place, live, weight])
-    info = jnp.where(mine, info, over_c(info))
-    vq_rows = jnp.where(mine, vq_in, over_c(vq_in))
-
-    def relative(a, axis):
-        shape = a.shape
-        a = a.reshape(shape[:axis] + (2, 2, quarter) + shape[axis + 1 :])
-        a = jnp.where(at_c == 0, a, jnp.flip(a, axis))
-        return jnp.where(at_l == 0, a, jnp.flip(a, axis + 1)).reshape(shape)
-
-    info = relative(info, 2)
-    vq_rows = relative(vq_rows, 1)
-    code_r, place_r, live_r, weight_r = info[0], info[1], info[2], info[3]
-    seg_r, level_r = place_r // 16, place_r % 16
-    base_r = seg_r * 16
-    key_r = jnp.where(live_r > 0, place_r, 1 << 20)
-    level_hot = low(
-        level_r[..., None] == jnp.arange(lead_pad - code_dim, dtype=jnp.int32)
-    )
-    feats = jnp.concatenate([vq_rows, level_hot], 2)
-    spot = jnp.arange(16, dtype=jnp.int32)
-    hot = low((seg_r[..., None] == spot % 4) & (spot < 12))
+    qkv_piece = ordered(at_h, first_near[None], first_far[None], 0)
 
     def window(*values):
         return lax.optimization_barrier(values)
@@ -1119,17 +1248,13 @@
     def far_part(r):
         return low(full(top[r][quarter:]) + full(moved[r][quarter:]))
 
-    def await_head():
-        return held[0]
-
-    def turn(norm, kernel, filler=lambda: None, beside=None):
+    def turn(norm, kernel, filler=lambda: None, beside=None, keep=lambda done: None):
         moved[1] = over_c(bottom[1])
         first, moved[1] = window(norm(0, (top[0], moved[0], across[0])), moved[1])
         across[1] = over_l(far_part(1))
         pieces = [[first, over_l(first), over_c(first), None], None]
         done, across[1], pieces[0][2] = window(filler(), across[1], pieces[0][2])
-        if done is not None and filler is await_head:
-            held[0] = done
+        keep(done)
         second, pieces[0][1] = window(norm(1, (top[1], moved[1], across[1])), pieces[0][1])
         pieces[1] = [second, over_l(second), over_c(second), None]
         pieces[0][3] = over_c(pieces[0][1])
@@ -1142,32 +1267,45 @@
         across[0] = over_l(sent)
         return sent
 
+    head_gain = tie(head_scale, gathered)
     gain_own = jnp.where(at_c == 0, head_gain[:2], head_gain[2:])
     gains = jnp.exp(ordered(at_h, gain_own, over_h(gain_own), 0)) / 8.0
     gain_row = jnp.repeat(gains, 64)[None, :]
+
+    info = full(jnp.stack([codes, place, live, weight], 1))
+    info_other, vq_other = over_c(info), over_c(vq_in)
+    at = jnp.stack([full(at_c == at_h).astype(jnp.int32), at_c, at_l])
+    arranged, olds, qkv_pieces, feed_far = window(
+        arrange(at, tie(info, mod_first), info_other, vq_in, vq_other, lead_pad),
+        old_stats(*tie((qkv_w, proj_w, fc1_w, fc2_w, head_w, ada_w, tables, head_scale[None]), mod_first)),
+        [qkv_piece] + [over_g(qkv_piece, k) for k in range(1, 4)] if g_count == 4 else [],
+        over_h(feed_near),
+    )
+    feats, hot, cols, rows = (arranged[k::4] for k in range(4))
+    head_near = near_rows(tie(head_w, olds))
+    feats_first = tie(feats[0], gain_row)
     inputs_one, qkv_rows, mixed_rows, lse_rows, top, bottom, stream_zero = ([None] * 2 for _ in range(7))
     if g_count == 4:
         inputs_one[0], qkv_rows[0], stream_zero[0], qkv_full, proj_full = enter_first(
-            lax.axis_index("g"), feats[0], lead_table, hot[0], mod_rows[0], qkv_pieces
+            lax.axis_index("g"), feats_first, lead_table, hot[0], mod_rows[0], qkv_pieces
         )
     else:
         wide_piece = lax.all_gather(qkv_piece, "g", axis=0)
         wide_piece = jnp.transpose(wide_piece, (0, 3, 2, 1, 4)).reshape(width, -1)
         qkv_full, proj_full = wide_piece[:, :768], wide_piece[:, 768:]
-        inputs_one[0], qkv_rows[0], stream_zero[0] = enter(feats[0], lead_table, hot[0], mod_rows[0], qkv_full)
-    feed_full = gathered_weight(tie(feed_near, qkv_rows[0]))
-    head_full = gathered_weight(tie(head_near, qkv_rows[0]))
-    held = [head_full]
+        inputs_one[0], qkv_rows[0], stream_zero[0] = enter(feats_first, lead_table, hot[0], mod_rows[0], qkv_full)
+    feed_full = gathered_weight(ordered(at_h, feed_near[None], feed_far[None], 0))
 
     moved, across = [None] * 2, [None] * 2
 
     def attention(r, given):
         mixed_rows[r], lse_rows[r], top[r], bottom[r] = attend(
-            given, gain_row, place_r[r], base_r[r], key_r[r], proj_full
+            given, gain_row, cols[r], rows[r], proj_full
         )
         return top[r], bottom[r]
 
-    attention(0, qkv_rows[0])
+    (top[0], bottom[0]), head_far = window(attention(0, qkv_rows[0]), over_h(head_near))
+    held = [gathered_weight(ordered(at_h, head_near[None], head_far[None], 0))]
     moved[0] = over_c(bottom[0])
     (inputs_one[1], qkv_rows[1], stream_zero[1]), moved[0] = window(
         enter(tie(feats[1], bottom[0]), lead_table, hot[1], mod_rows[1], qkv_full), moved[0]
@@ -1186,11 +1324,7 @@
         inputs_two[r], acts[r], slopes[r], top[r], bottom[r] = feed(pieces, feed_full)
         return top[r], bottom[r]
 
-    pieces_two, (top[0], bottom[0]), olds, _ = turn(
-        norm_two,
-        forward,
-        lambda: old_stats(qkv_w, proj_w, fc1_w, fc2_w, head_w, ada_w, tables, head_scale[None]),
-    )
+    pieces_two, (top[0], bottom[0]), _, _ = turn(norm_two, forward)
     pieces_two[1].append(over_c(pieces_two[1][1]))
     sent = launch()
     (top[1], bottom[1]), across[0] = window(
@@ -1201,8 +1335,7 @@
     half_codes = block_codes // 2
     column = jnp.arange(2 * half_codes, dtype=jnp.int32)
     block_here = (column // half_codes) * 2 + at_l
-    column_code = (block_here * block_codes + at_c * half_codes + column % half_codes)[None, :]
-    code_column = [code_r[r][:, None] for r in range(2)]
+    column_code = full(block_here * block_codes + at_c * half_codes + column % half_codes)[None, :]
     branch_two, stream_two, logits, stats, d_logits, losses, others, inputs_out = ([None] * 2 for _ in range(8))
 
     def norm_out(r, parts):
@@ -1210,18 +1343,20 @@
         return given
 
     def score(r, pieces):
-        inputs_out[r], logits[r], stats[r] = head(pieces, held[0], code_column[r], column_code)
+        inputs_out[r], logits[r], stats[r] = head(pieces, held[0], cols[r], column_code)
         return stats[r]
 
     def compare(r):
         return [over_c(stats[r]), over_l(stats[r]), over_cl(stats[r])]
 
     def score_back(r):
-        lines, losses[r] = merge(weight_sum, stats[r], *others[r], full(weight_r[r])[None, :])
-        d_logits[r], top[r], bottom[r] = head_back(logits[r], held[0], code_column[r], column_code, lines)
+        lines, losses[r] = merge(weight_sum, stats[r], *others[r], rows[r])
+        d_logits[r], top[r], bottom[r] = head_back(logits[r], held[0], cols[r], column_code, lines)
         return top[r], bottom[r]
 
-    pieces_out, stats[0], _, _ = turn(norm_out, score, await_head)
+    pieces_out, stats[0], _, _ = turn(
+        norm_out, score, lambda: held[0], keep=lambda done: held.__setitem__(0, done)
+    )
     pieces_out[1].append(over_c(pieces_out[1][1]))
     stats[1], others[0] = window(score(1, pieces_out[1]), compare(0))
     (top[0], bottom[0]), others[1] = window(score_back(0), compare(1))
@@ -1275,7 +1410,7 @@
 
     def attention_back(r, pieces):
         d_branch_one[r], d_qkv[r], scale_rows[r], top[r], bottom[r] = attend_back(
-            qkv_rows[r], gain_row, place_r[r], base_r[r], key_r[r], lse_rows[r], pieces, proj_full, qkv_full
+            qkv_rows[r], gain_row, cols[r], rows[r], lse_rows[r], pieces, proj_full, qkv_full
         )
         return top[r], bottom[r]
 
@@ -1322,7 +1457,9 @@
     left, right = d_items[:, :mod_half], d_items[:, mod_half:]
     d_items = jnp.where(at_c == 0, left, right) + over_c(jnp.where(at_c == 0, right, left))
     d_items = low(d_items + over_l(d_items))
-    d_items = gather_g(ordered(at_h, d_items, over_h(d_items), 0))
+    d_items, first_sum = window(ordered(at_h, d_items, over_h(d_items), 0), first_sum)
+    leaving = theirs(first_sum)
+    d_items = gather_g(tie(d_items, leaving))
     d_items = ordered(at_c, d_items, over_c(d_items), 1)
     ada_grad = dot_tn(activated, d_items)
     d_act_vec = dot_nt(d_items, ada_low)
@@ -1339,7 +1476,8 @@
     n = kept.shape[1] // 2
     fc1_grad = ordered(at_c, kept[:, :n], moved_half[:, :n], 1)
     fc2_grad = ordered(at_c, kept[:, n:], moved_half[:, n:], 1)
-    kept, moved_half = settle(first_sum, over_h(theirs(first_sum)))
+    ada_grad, tables_grad, first_other = window(ada_grad, tables_grad, over_h(leaving))
+    kept, moved_half = settle(first_sum, first_other)
     first_halves = jnp.stack([kept, moved_half])
     first_halves = jnp.where(at_c == 0, first_halves, first_halves[::-1])
     first_halves = jnp.transpose(first_halves.reshape(2, slice_width, 4, -1), (2, 1, 0, 3))
@@ -1348,7 +1486,6 @@
 
     decay = 1.0 - STEP ** (-0.8)
     grads = [qkv_grad, proj_grad, fc1_grad, fc2_grad, head_grad, ada_grad]
-    masters = [qkv_w, proj_w.T, fc1_w, fc2_w.T, head_w, ada_w]
     wide = [g.size // slice_width * (mp_count if k < 5 else 1) for k, g in enumerate(grads)]
     sizes = [g.size // slice_width for g in grads]
     starts = [sum(sizes[:k]) for k in range(7)]
@@ -1381,39 +1518,38 @@
     col_old = jnp.concatenate(
         [qkv_stat.reshape(-1), proj_stat, fc1_stat, fc2_stat, head_stat, ada_stat]
     )[None, :]
-    col_line, sum_line = finish(flat, col_old, decay, width, starts)
+    heads = head_scale.shape[0]
+    scale_line = jnp.pad(scale_v, (11, 128 - 11 - heads), constant_values=1.0)[None, :]
+    col_line, part_line, own_line, second_line, scale_step = finish(
+        flat, col_old, scale_line, decay, width, starts
+    )
     col_new = [col_line[0, starts[k] : starts[k + 1]] for k in range(6)]
     line = flat[:1, starts[6] :]
-    scale_grad = line[0, 11:15]
+    scale_grad = line[0, 11 : 11 + heads]
     loss_sum = line[0, 22]
-    scale_v_new = decay * scale_v + (1.0 - decay) * (scale_grad * scale_grad + eps_one)
-    scale_step = scale_grad * lax.rsqrt(scale_v_new)
-    scale_spot = jnp.where(spots == 7, jnp.sum(scale_step * scale_step), 0.0)
-    split = over_mp(jnp.where(spots == 5, 0.0, sum_line) + scale_spot)
-    step_line = split + jnp.where(spots == 5, sum_line, 0.0)
-    step_line = step_line + jnp.where(spots == 6, line[0, 10], 0.0)
-    weight_line = jnp.zeros((1, 128), full_type)
-    for k, value in enumerate([line[0, 16 + j] for j in range(5)] + [line[0, 8], line[0, 9], early_line[0, 21]]):
-        weight_line = jnp.where(spots == k, value, weight_line)
-    entries = [width * wide[k] for k in range(6)] + [table_rows * width, head_scale.shape[0] * mp_count]
-    entry_line = jnp.array(entries + [1] * 120, full_type)[None, :]
-    ratio = jnp.sqrt(step_line / entry_line) / clip_rms
-    spread = jnp.maximum(eps_two, jnp.sqrt(weight_line / entry_line))
-    factor = (rate_step * spread / jnp.maximum(1.0, ratio))[0]
-    row_mean = line[0, :6] / width
-    sides = [col_new[0].reshape(3, 1, -1)] + [c[None, :] for c in col_new[1:]]
-    raw_steps = [
-        grads[k] * lax.rsqrt(d_stats_new[k][:, None] * sides[k] / row_mean[k]) for k in range(6)
-    ] + [tables_step, scale_step]
-    parameters = masters + [tables, head_scale]
-    news = [parameters[k] - factor[k] * raw_steps[k] for k in range(8)]
+    scale_v_new = second_line[0, 11 : 11 + heads]
+    entries = [width * wide[k] for k in range(6)] + [table_rows * width, heads * mp_count]
+    news = renew(
+        (line, over_mp(part_line), own_line, early_line),
+        d_stats_new,
+        col_line,
+        grads,
+        (tables_step, scale_step),
+        (
+            qkv_w, proj_w, fc1_w, fc2_w, head_w, ada_w, tables,
+            jnp.pad(head_scale, (11, 128 - 11 - heads))[None, :],
+        ),
+        width,
+        entries,
+        starts,
+    )
     return (
         loss_sum,
         weight_sum,
         qkv_grad,
-        proj_grad.T,
+        news[8],
         fc1_grad,
-        fc2_grad.T,
+        news[9],
         head_grad,
         ada_grad,
         tables_grad,
@@ -1428,13 +1564,13 @@
         tables_v_new,
         scale_v_new,
         news[0],
-        news[1].T,
+        news[1],
         news[2],
-        news[3].T,
+        news[3],
         news[4],
         news[5],
         news[6],
-        news[7],
+        news[7][0, 11 : 11 + heads],
     )
 
 

time: 646 us -> 576 us (0.89)
  other arithmetic: 65.5 us -> 22.8 us
  waiting for transfers between devices: 169 us -> 131 us
  Pallas kernels: 179 us -> 191 us
    ppermute x25, waiting for transfers between devices: 60.3 us -> 36.7 us  [over_l(): return lax.ppermute(a, 'l', swap_pairs)]
    sub x6 -> x0, other arithmetic: 18.2 us -> none  [body(): news = [parameters[k] - factor[k] * raw_steps[k] for k in range(8)]]
    ppermute x11, waiting for transfers between devices: 39.5 us -> 23.5 us  [over_g(): return lax.ppermute(a, 'g', [(i, i ^ k) for i in range(lax.axis_size('g'))])]
    pallas_call x0 -> x2, Pallas kernels: none -> 13.8 us  [the longest x1 10.4 us: renew(): call(functools.partial(renew_kernel, width=width, entries=entries, starts...]
    ppermute x25, starting transfers between devices: 20 us -> 29.5 us  [over_l(): return lax.ppermute(a, 'l', swap_pairs)]
    all_to_all x1, waiting for transfers between devices: 0.69 us -> 7.26 us  [body(): lax.all_to_all(lead_part, DP, 0, 0, tiled=True)]
    unnamed x566 -> x468, local copies, waits for them, and re-layouts: 89.4 us -> 85.9 us
    ppermute x11 -> x13, waiting for transfers between devices: 18.6 us -> 15.1 us  [over_h(): return lax.ppermute(a, 'h', swap_pairs)]
  transfers between devices with their start and end apart: 97 -> 99, of which waited for: 39 -> 34; matrix products, arithmetic and copies ran while one was open for 10% -> 9% of each run, Pallas kernels for 26% -> 31%
where the time goes in v2:
time: 576 us; the launch traced here: 567 us
  Pallas kernels  191 us (33%)
  waiting for transfers between devices  131 us (23%)
  local copies, waits for them, and re-layouts  107 us (19%)
  starting transfers between devices  75.6 us (13%)
  other arithmetic  22.8 us (4%)
  between operations  20.7 us (4%)
  matrix products  10 us (2%)
  blocking collectives  9.24 us (2%)
    unnamed x468, local copies, waits for them, and re-layouts  85.9 us
    pallas_call x2, Pallas kernels, attend_back(): call(functools.partial(attend_back_kernel, tile=256), (pairs,), [part(len...  40.5 us
    ppermute x25, waiting for transfers between devices, over_l(): return lax.ppermute(a, 'l', swap_pairs)  36.7 us
    ppermute x25, starting transfers between devices, over_l(): return lax.ppermute(a, 'l', swap_pairs)  29.5 us
    reduce_scatter x3, waiting for transfers between devices, reduced(): lax.psum_scatter(a.reshape(-1, shape[2]), 'g', scatter_dimension=0, tiled...  25.7 us
    ppermute x11, waiting for transfers between devices, over_g(): return lax.ppermute(a, 'g', [(i, i ^ k) for i in range(lax.axis_size('g'))])  23.5 us
    pallas_call x2, Pallas kernels, attend(): call(attend_kernel, (pairs,), [block, pl.BlockSpec((length, 128), lambda...  18.2 us
    ppermute x13, starting transfers between devices, over_h(): return lax.ppermute(a, 'h', swap_pairs)  17.9 us
  transfers between devices with their start and end apart: 99, of which 34 were waited for; matrix products, arithmetic and copies ran while one was open for 9% of the time, Pallas kernels for 31%

profile of v2, /device:TPU:0, one launch (start us, length us, event | category | flops | bytes accessed | tf_op | source)
XLA Modules:
  0.0 567.3 jit_solution(4314835327199060920)
XLA Ops:
  21.2 9.2 %all-gather = bf16[384,128]{1,0:T(8,128)(2,1)S(1)} all-gather(bf16[48,128]{1,0:T(8,128)(2,1)S(1)} %pad_maximum_fusion.2), channel_id=2, replica_groups=mesh['g'=4,'c'=2,'h'=2,'l'=2] {'g','c'}, dimensions={0}, use_global_device_ids=true | all-gather | bytes 110592 | tf_op jit(solution)/shard_map/all_gather | solution.py:1200
  65.6 8.5 %collective-permute-done.6.c_ref = bf16[2,4,256,128]{3,2,1,0:T(8,128)(2,1)S(1)} collective-permute-done((bf16[2,4,256,128]{3,2,1,0:T(8,128)(2,1)S(1)}, bf16[2,4,256,128]{3,2,1,0:T(8,128)(2,1)S(1)}, u32[]{:S(2)}, u32[]{:S(2)}) %collective-permute-start.6) | collective-permute-done | bytes 524320 | tf_op jit(solution)/shard_map/ppermute | solution.py:78
  85.9 5.7 %enter_first.1 = (bf16[768,1024]{1,0:T(8,128)(2,1)S(1)}, f32[768,768]{1,0:T(8,128)}, f32[192,1024]{1,0:T(8,128)S(1)}, bf16[1024,768]{1,0:T(8,128)(2,1)}, bf16[1024,256]{1,0:T(8,128)(2,1)S(1)}) custom-call(s32[1]{0:T(128)} %bitcast.1.at_ref, bf16[768,48]{1,0:T(8,128)(2,1)S(1)} %copy-done.159, bf16[48,1024]{1,0:T(8,128)(2,1)S(1)} %bitcast.172, ...), custom_call_target="tpu_custom_call" | custom-call | flops 6000000000 | bytes 6000000 | tf_op jit(solution)/shard_map/enter_first/pallas_call | solution.py:334
  94.9 9.0 %attend.2 = (bf16[768,256]{1,0:T(8,128)(2,1)S(1)}, f32[2,2,768]{2,1,0:T(2,128)S(1)}, bf16[384,1024]{1,0:T(8,128)(2,1)S(1)}, bf16[384,1024]{1,0:T(8,128)(2,1)S(1)}) custom-call(f32[768,768]{1,0:T(8,128)S(1)} %copy-done.90, f32[768,768]{1,0:T(8,128)S(1)} %copy-done.90, f32[768,768]{1,0:T(8,128)S(1)} %copy-done.90, ...), custom_call_target="tpu_custom_call" | custom-call | flops 11000000512 | bytes 11000000 | tf_op jit(solution)/shard_map/attend/pallas_call | solution.py:1006
  106.0 5.4 enter.1
  112.8 4.1 collective-permute-start.19
  118.5 9.2 %attend.3 = (bf16[768,256]{1,0:T(8,128)(2,1)S(1)}, f32[2,2,768]{2,1,0:T(2,128)S(1)}, bf16[384,1024]{1,0:T(8,128)(2,1)S(1)}, bf16[384,1024]{1,0:T(8,128)(2,1)S(1)}) custom-call(f32[768,768]{1,0:T(8,128)S(1)} %copy-done.83, f32[768,768]{1,0:T(8,128)S(1)} %copy-done.83, f32[768,768]{1,0:T(8,128)S(1)} %copy-done.83, ...), custom_call_target="tpu_custom_call" | custom-call | flops 11000000512 | bytes 11000000 | tf_op jit(solution)/shard_map/attend/pallas_call | solution.py:1006
  133.6 9.9 %collective-permute-done.21.c_ref = bf16[192,1024]{1,0:T(8,128)(2,1)S(1)} collective-permute-done((bf16[192,1024]{1,0:T(8,128)(2,1)S(1)}, bf16[192,1024]{1,0:T(8,128)(2,1)S(1)}, u32[]{:S(2)}, u32[]{:S(2)}) %collective-permute-start.21) | collective-permute-done | bytes 393248 | tf_op jit(solution)/shard_map/ppermute | solution.py:66
  146.3 4.8 collective-permute-done.23.b_ref
  156.6 8.3 %feed.2 = (bf16[768,1024]{1,0:T(8,128)(2,1)S(1)}, bf16[768,1024]{1,0:T(8,128)(2,1)}, f32[768,1024]{1,0:T(8,128)}, bf16[384,1024]{1,0:T(8,128)(2,1)S(1)}, bf16[384,1024]{1,0:T(8,128)(2,1)S(1)}) custom-call(bf16[192,1024]{1,0:T(8,128)(2,1)S(1)} %get-tuple-element.337.a_ref, bf16[192,1024]{1,0:T(8,128)(2,1)S(1)} %copy-done.63, ...), custom_call_target="tpu_custom_call" | custom-call | flops 8999999488 | bytes 9000000 | tf_op jit(solution)/shard_map/feed/pallas_call | solution.py:492
  171.6 9.0 %feed.3 = (bf16[768,1024]{1,0:T(8,128)(2,1)S(1)}, bf16[768,1024]{1,0:T(8,128)(2,1)}, f32[768,1024]{1,0:T(8,128)}, bf16[384,1024]{1,0:T(8,128)(2,1)S(1)}, bf16[384,1024]{1,0:T(8,128)(2,1)S(1)}) custom-call(bf16[192,1024]{1,0:T(8,128)(2,1)S(1)} %get-tuple-element.352.a_ref, bf16[192,1024]{1,0:T(8,128)(2,1)S(1)} %collective-permute-done.25.b_ref, ...), custom_call_target="tpu_custom_call" | custom-call | flops 8999999488 | bytes 9000000 | tf_op jit(solution)/shard_map/feed/pallas_call | solution.py:492
  186.8 14.8 %all-gather.6.cloned.1.call-done = bf16[2048,512]{1,0:T(8,128)(2,1)} async-done(((bf16[512,512]{1,0:T(8,128)(2,1)}), bf16[2048,512]{1,0:T(8,128)(2,1)}) %all-gather.6.cloned.1.call-update) | async-done | bytes 2097168 | tf_op jit(solution)/shard_map/all_gather | solution.py:1239
  216.1 4.8 head.2
  226.7 4.8 head.3
  250.6 4.1 head_back.3
  262.5 6.0 %head_grad.1 = bf16[4,2,256,512]{3,2,1,0:T(8,128)(2,1)} custom-call(bf16[768,1024]{1,0:T(8,128)(2,1)S(1)} %copy-done.85, bf16[768,1024]{1,0:T(8,128)(2,1)S(1)} %copy-done.87, bf16[768,1024]{1,0:T(8,128)(2,1)S(1)} %copy-done.78, bf16[768,1024]{1,0:T(8,128)(2,1)} %copy-done.79), custom_call_target="tpu_custom_call" | custom-call | flops 6000000000 | bytes 6000000 | tf_op jit(solution)/shard_map/head_grad/pallas_call | solution.py:658
  268.5 4.6 collective-permute-done.47.refs_2_
  280.4 4.4 collective-permute-done.49.b_ref
  286.5 7.6 %feed_back.2 = (bf16[768,1024]{1,0:T(8,128)(2,1)S(1)}, bf16[768,1024]{1,0:T(8,128)(2,1)}, bf16[384,1024]{1,0:T(8,128)(2,1)S(1)}, bf16[384,1024]{1,0:T(8,128)(2,1)S(1)}) custom-call(bf16[192,1024]{1,0:T(8,128)(2,1)S(1)} %copy-done.51, bf16[192,1024]{1,0:T(8,128)(2,1)S(1)} %collective-permute-done.49.b_ref, ...), custom_call_target="tpu_custom_call" | custom-call | flops 7000000000 | bytes 7000000 | tf_op jit(solution)/shard_map/feed_back/pallas_call | solution.py:521
  299.5 7.5 %feed_back.3 = (bf16[768,1024]{1,0:T(8,128)(2,1)S(1)}, bf16[768,1024]{1,0:T(8,128)(2,1)}, bf16[384,1024]{1,0:T(8,128)(2,1)S(1)}, bf16[384,1024]{1,0:T(8,128)(2,1)S(1)}) custom-call(bf16[192,1024]{1,0:T(8,128)(2,1)S(1)} %get-tuple-element.421.a_ref, bf16[192,1024]{1,0:T(8,128)(2,1)S(1)} %collective-permute-done.51.b_ref, ...), custom_call_target="tpu_custom_call" | custom-call | flops 7000000000 | bytes 7000000 | tf_op jit(solution)/shard_map/feed_back/pallas_call | solution.py:521
  320.4 11.2 %feed_grad.1 = bf16[4,2,256,1024]{3,2,1,0:T(8,128)(2,1)} custom-call(bf16[768,1024]{1,0:T(8,128)(2,1)S(1)} %copy-done.127, bf16[768,1024]{1,0:T(8,128)(2,1)S(1)} %copy-done.129, bf16[768,1024]{1,0:T(8,128)(2,1)S(1)} %copy-done.81, bf16[768,1024]{1,0:T(8,128)(2,1)} %get-tuple-element.439.d_ref, bf16[768,1024]{1,0:T(8,128)(2,1)} %copy-done.80, ...), custom_call_target="tpu_custom_call" | custom-call | flops 12000000000 | bytes 12000000 | tf_op jit(solution)/shard_map/feed_grad/pallas_call | solution.py:684
  340.5 4.2 collective-permute-done.59.pb_ref
  349.5 20.1 %attend_back.2 = (bf16[768,1024]{1,0:T(8,128)(2,1)}, bf16[768,768]{1,0:T(8,128)(2,1)S(1)}, f32[2,1,128]{2,1,0:T(1,128)S(1)}, bf16[384,1024]{1,0:T(8,128)(2,1)S(1)}, bf16[384,1024]{1,0:T(8,128)(2,1)S(1)}) custom-call(f32[768,768]{1,0:T(8,128)} %get-tuple-element.308.q_ref.k_ref.v_ref, f32[768,768]{1,0:T(8,128)} %get-tuple-element.308.q_ref.k_ref.v_ref, ...), custom_call_target="tpu_custom_call" | custom-call | flops 16000000000 | bytes 16000000 | tf_op jit(solution)/shard_map/attend_back/pallas_call | solution.py:1122
  374.8 10.3 %reduce-scatter.6.cloned.1.call-done = bf16[512,1024]{1,0:T(8,128)(2,1)} async-done(((bf16[2048,1024]{1,0:T(8,128)(2,1)}), bf16[512,1024]{1,0:T(8,128)(2,1)}) %reduce-scatter.6.cloned.1.call-update) | async-done | bytes 1048592 | tf_op jit(solution)/shard_map/reduce_scatter | solution.py:1369
  392.0 20.4 %attend_back.3 = (bf16[768,1024]{1,0:T(8,128)(2,1)}, bf16[768,768]{1,0:T(8,128)(2,1)S(1)}, f32[2,1,128]{2,1,0:T(1,128)S(1)}, bf16[384,1024]{1,0:T(8,128)(2,1)S(1)}, bf16[384,1024]{1,0:T(8,128)(2,1)S(1)}) custom-call(f32[768,768]{1,0:T(8,128)} %get-tuple-element.328.q_ref.k_ref.v_ref, f32[768,768]{1,0:T(8,128)} %get-tuple-element.328.q_ref.k_ref.v_ref, ...), custom_call_target="tpu_custom_call" | custom-call | flops 16000000000 | bytes 16000000 | tf_op jit(solution)/shard_map/attend_back/pallas_call | solution.py:1122
  420.1 8.9 %first_grad.1 = bf16[4,2,256,512]{3,2,1,0:T(8,128)(2,1)} custom-call(bf16[768,1024]{1,0:T(8,128)(2,1)S(1)} %copy-done.73, bf16[768,1024]{1,0:T(8,128)(2,1)} %copy-done.74, bf16[768,768]{1,0:T(8,128)(2,1)S(1)} %copy-done.76, bf16[768,768]{1,0:T(8,128)(2,1)S(1)} %get-tuple-element.476.d_ref, bf16[768,1024]{1,0:T(8,128)(2,1)} %get-tuple-element.477.e_ref, ...), custom_call_target="tpu_custom_call" | custom-call | flops 6000000000 | bytes 6000000 | tf_op jit(solution)/shard_map/first_grad/pallas_call | solution.py:710
  443.2 7.3 %all-to-all-done = f32[8,48,128]{2,1,0:T(8,128)S(1)} async-done(((f32[8,48,128]{2,1,0:T(8,128)}), f32[8,48,128]{2,1,0:T(8,128)S(1)}, u32[]{:S(2)}, u32[]{:S(2)}) %all-to-all-start) | async-done | bytes 196640 | tf_op jit(solution)/shard_map/all_to_all | solution.py:1468
  451.1 15.4 %reduce-scatter.8.cloned.1.call-done = bf16[512,512]{1,0:T(8,128)(2,1)} async-done(((bf16[2048,512]{1,0:T(8,128)(2,1)}), bf16[512,512]{1,0:T(8,128)(2,1)}) %reduce-scatter.8.cloned.1.call-update) | async-done | bytes 524304 | tf_op jit(solution)/shard_map/reduce_scatter | solution.py:1369
  491.3 4.7 collective-permute-done.79
  511.5 4.6 column_stats.1
  523.2 4.0 collective-permute-done.90
  548.4 10.4 %renew.1 = (f32[3,128,256]{2,1,0:T(8,128)}, f32[256,128]{1,0:T(8,128)}, f32[128,1024]{1,0:T(8,128)}, f32[1024,128]{1,0:T(8,128)}, f32[128,1024]{1,0:T(8,128)}, /...) custom-call(f32[1,128]{1,0:T(1,128)S(1)} %slice.476.line_ref, ...), custom_call_target="tpu_custom_call" | custom-call | flops 8000000000 | bytes 8000000 | tf_op jit(solution)/shard_map/renew/pallas_call | solution.py:921
  (810 shorter events, 283.3 us)
Async XLA Ops:
  7.2 146.4 %all-gather.4.cloned.1.call-start = ((), (), s32[]{:S(2)}) async-start(), calls=%async_computation.4 | async-start | bytes 5242880 | tf_op jit(solution)/shard_map/all_gather | solution.py:1239
  13.6 39.0 %collective-permute-start.3 = (f32[2,4,768]{2,1,0:T(4,128)S(1)}, f32[2,4,768]{2,1,0:T(4,128)S(1)}, u32[]{:S(2)}, u32[]{:S(2)}) collective-permute-start(f32[2,4,768]{2,1,0:T(4,128)S(1)} %add_convert_fusion.11.mine_ref), channel_id=1, source_target_pairs={{0,4},{4,0},{1,5},{5,1},{2,6},{6,2},{3,7},{7,3},{8,12},{12,8},{9,1... | collective-permute-start | bytes 73736 | tf_op jit(solution)/shard_map/ppermute | solution.py:62
  13.9 41.7 %collective-permute-start.4 = (bf16[2,768,32]{2,1,0:T(8,128)(2,1)S(1)}, bf16[2,768,32]{2,1,0:T(8,128)(2,1)}, u32[]{:S(2)}, u32[]{:S(2)}) collective-permute-start(bf16[2,768,32]{2,1,0:T(8,128)(2,1)S(1)} %copy.71.vq_ref), channel_id=1, source_target_pairs={{0,4},{4,0},{1,5},{5,1},{2,6},{6,2},{3,7},{7,3},{8,12},{12,8},{9,1... | collective-permute-start | bytes 294920 | tf_op jit(solution)/shard_map/ppermute | solution.py:62
  17.4 16.2 %collective-permute-start.1 = (bf16[4,256,128]{2,1,0:T(8,128)(2,1)S(1)}, bf16[4,256,128]{2,1,0:T(8,128)(2,1)S(1)}, u32[]{:S(2)}, u32[]{:S(2)}) collective-permute-start(bf16[4,256,128]{2,1,0:T(8,128)(2,1)S(1)} %maximum_select_fusion.7), channel_id=1, source_target_pairs={{0,2},{2,0},{1,3},{3,1},{4,6},{6,4},{5,7},{7,5},{8,10},{10,8},{9,1... | collective-permute-start | bytes 786440 | tf_op jit(solution)/shard_map/ppermute | solution.py:70
  45.5 18.6 %collective-permute-start.5 = (bf16[2,4,256,128]{3,2,1,0:T(8,128)(2,1)S(1)}, bf16[2,4,256,128]{3,2,1,0:T(8,128)(2,1)S(1)}, u32[]{:S(2)}, u32[]{:S(2)}) collective-permute-start(bf16[2,4,256,128]{3,2,1,0:T(8,128)(2,1)S(1)} %maximum_select_fusion.2.a_ref), channel_id=1, source_target_pairs={{0,8},{8,0},{16,24},{24,16},{1,9},{9,1},{17,25},{25,17},{2,10},{10... | collective-permute-start | bytes 1572872 | tf_op jit(solution)/shard_map/ppermute | solution.py:78
  48.1 26.1 %collective-permute-start.6 = (bf16[2,4,256,128]{3,2,1,0:T(8,128)(2,1)S(1)}, bf16[2,4,256,128]{3,2,1,0:T(8,128)(2,1)S(1)}, u32[]{:S(2)}, u32[]{:S(2)}) collective-permute-start(bf16[2,4,256,128]{3,2,1,0:T(8,128)(2,1)S(1)} %maximum_select_fusion.2.a_ref), channel_id=1, source_target_pairs={{0,16},{8,24},{16,0},{24,8},{1,17},{9,25},{17,1},{25,9},{2,18},{10... | collective-permute-start | bytes 1572872 | tf_op jit(solution)/shard_map/ppermute | solution.py:78
  50.9 25.5 %collective-permute-start.7 = (bf16[2,4,256,128]{3,2,1,0:T(8,128)(2,1)S(1)}, bf16[2,4,256,128]{3,2,1,0:T(8,128)(2,1)S(1)}, u32[]{:S(2)}, u32[]{:S(2)}) collective-permute-start(bf16[2,4,256,128]{3,2,1,0:T(8,128)(2,1)S(1)} %maximum_select_fusion.2.a_ref), channel_id=1, source_target_pairs={{0,24},{8,16},{16,8},{24,0},{1,25},{9,17},{17,9},{25,1},{2,26},{10... | collective-permute-start | bytes 1572872 | tf_op jit(solution)/shard_map/ppermute | solution.py:78
  52.6 25.8 %collective-permute-start.10 = (bf16[256,1024]{1,0:T(8,128)(2,1)S(1)}, bf16[256,1024]{1,0:T(8,128)(2,1)S(1)}, u32[]{:S(2)}, u32[]{:S(2)}) collective-permute-start(bf16[256,1024]{1,0:T(8,128)(2,1)S(1)} %get-tuple-element.539), channel_id=1, source_target_pairs={{0,2},{2,0},{1,3},{3,1},{4,6},{6,4},{5,7},{7,5},{8,10},{10,8},{9,1... | collective-permute-start | bytes 1572872 | tf_op jit(solution)/shard_map/ppermute | solution.py:70
  55.6 23.5 %collective-permute-start.12 = (f32[8,4096]{1,0:T(8,128)S(1)}, f32[8,4096]{1,0:T(8,128)S(1)}, u32[]{:S(2)}, u32[]{:S(2)}) collective-permute-start(f32[8,4096]{1,0:T(8,128)S(1)} %get-tuple-element.540), channel_id=1, source_target_pairs={{0,8},{8,0},{16,24},{24,16},{1,9},{9,1},{17,25},{25,17},{2,10},{10... | collective-permute-start | bytes 393224 | tf_op jit(solution)/shard_map/ppermute | solution.py:78
  64.1 15.0 %collective-permute-start.13 = (f32[8,4096]{1,0:T(8,128)S(1)}, f32[8,4096]{1,0:T(8,128)S(1)}, u32[]{:S(2)}, u32[]{:S(2)}) collective-permute-start(f32[8,4096]{1,0:T(8,128)S(1)} %get-tuple-element.542), channel_id=1, source_target_pairs={{0,16},{8,24},{16,0},{24,8},{1,17},{9,25},{17,1},{25,9},{2,18},{10... | collective-permute-start | bytes 393224 | tf_op jit(solution)/shard_map/ppermute | solution.py:78
  82.1 119.5 %all-gather.6.cloned.1.call-start = ((), (), s32[]{:S(2)}) async-start(), calls=%async_computation.5 | async-start | bytes 2621440 | tf_op jit(solution)/shard_map/all_gather | solution.py:1239
  82.4 22.8 %collective-permute-start.17 = (bf16[256,512]{1,0:T(8,128)(2,1)S(1)}, bf16[256,512]{1,0:T(8,128)(2,1)S(1)}, u32[]{:S(2)}, u32[]{:S(2)}) collective-permute-start(bf16[256,512]{1,0:T(8,128)(2,1)S(1)} %maximum_select_fusion.12), channel_id=1, source_target_pairs={{0,2},{2,0},{1,3},{3,1},{4,6},{6,4},{5,7},{7,5},{8,10},{10,8},{9,1... | collective-permute-start | bytes 786440 | tf_op jit(solution)/shard_map/ppermute | solution.py:70
  112.8 16.3 %collective-permute-start.19 = (bf16[192,1024]{1,0:T(8,128)(2,1)S(1)}, bf16[192,1024]{1,0:T(8,128)(2,1)S(1)}, u32[]{:S(2)}, u32[]{:S(2)}) collective-permute-start(bf16[192,1024]{1,0:T(8,128)(2,1)S(1)} %add_convert_fusion.9), channel_id=1, source_target_pairs={{0,1},{1,0},{2,3},{3,2},{4,5},{5,4},{6,7},{7,6},{8,9},{9,8},{10,11... | collective-permute-start | bytes 1179656 | tf_op jit(solution)/shard_map/ppermute | solution.py:66
  131.8 19.4 %collective-permute-start.23 = (bf16[192,1024]{1,0:T(8,128)(2,1)S(1)}, bf16[192,1024]{1,0:T(8,128)(2,1)S(1)}, u32[]{:S(2)}, u32[]{:S(2)}) collective-permute-start(bf16[192,1024]{1,0:T(8,128)(2,1)S(1)} %get-tuple-element.337.a_ref), channel_id=1, source_target_pairs={{0,1},{1,0},{2,3},{3,2},{4,5},{5,4},{6,7},{7,6},{8,9},{9,8},{10,11... | collective-permute-start | bytes 1179656 | tf_op jit(solution)/shard_map/ppermute | solution.py:66
  151.9 14.2 %collective-permute-start.25 = (bf16[192,1024]{1,0:T(8,128)(2,1)S(1)}, bf16[192,1024]{1,0:T(8,128)(2,1)S(1)}, u32[]{:S(2)}, u32[]{:S(2)}) collective-permute-start(bf16[192,1024]{1,0:T(8,128)(2,1)S(1)} %get-tuple-element.352.a_ref), channel_id=1, source_target_pairs={{0,1},{1,0},{2,3},{3,2},{4,5},{5,4},{6,7},{7,6},{8,9},{9,8},{10,11... | collective-permute-start | bytes 1179656 | tf_op jit(solution)/shard_map/ppermute | solution.py:66
  168.0 142.8 %reduce-scatter.4.cloned.1.call-start = ((), (), s32[]{:S(2)}) async-start(), calls=%async_computation.6 | async-start | bytes 2621440 | tf_op jit(solution)/shard_map/reduce_scatter | solution.py:1369
  184.5 17.1 %collective-permute-start.31 = (bf16[192,1024]{1,0:T(8,128)(2,1)S(1)}, bf16[192,1024]{1,0:T(8,128)(2,1)S(1)}, u32[]{:S(2)}, u32[]{:S(2)}) collective-permute-start(bf16[192,1024]{1,0:T(8,128)(2,1)S(1)} %add_convert_fusion.6), channel_id=1, source_target_pairs={{0,1},{1,0},{2,3},{3,2},{4,5},{5,4},{6,7},{7,6},{8,9},{9,8},{10,11... | collective-permute-start | bytes 1179656 | tf_op jit(solution)/shard_map/ppermute | solution.py:66
  185.2 16.4 %collective-permute-start.32 = (bf16[192,1024]{1,0:T(8,128)(2,1)}, bf16[192,1024]{1,0:T(8,128)(2,1)S(1)}, u32[]{:S(2)}, u32[]{:S(2)}) collective-permute-start(bf16[192,1024]{1,0:T(8,128)(2,1)} %get-tuple-element.361.a_ref), channel_id=1, source_target_pairs={{0,4},{4,0},{1,5},{5,1},{2,6},{6,2},{3,7},{7,3},{8,12},{12,8},{9,1... | collective-permute-start | bytes 1179656 | tf_op jit(solution)/shard_map/ppermute | solution.py:62
  185.7 21.5 %collective-permute-start.33 = (bf16[192,1024]{1,0:T(8,128)(2,1)}, bf16[192,1024]{1,0:T(8,128)(2,1)S(1)}, u32[]{:S(2)}, u32[]{:S(2)}) collective-permute-start(bf16[192,1024]{1,0:T(8,128)(2,1)} %get-tuple-element.361.a_ref), channel_id=1, source_target_pairs={{0,1},{1,0},{2,3},{3,2},{4,5},{5,4},{6,7},{7,6},{8,9},{9,8},{10,11... | collective-permute-start | bytes 1179656 | tf_op jit(solution)/shard_map/ppermute | solution.py:66
  208.0 14.1 %collective-permute-start.35 = (bf16[192,1024]{1,0:T(8,128)(2,1)}, bf16[192,1024]{1,0:T(8,128)(2,1)S(1)}, u32[]{:S(2)}, u32[]{:S(2)}) collective-permute-start(bf16[192,1024]{1,0:T(8,128)(2,1)} %get-tuple-element.375.a_ref), channel_id=1, source_target_pairs={{0,1},{1,0},{2,3},{3,2},{4,5},{5,4},{6,7},{7,6},{8,9},{9,8},{10,11... | collective-permute-start | bytes 1179656 | tf_op jit(solution)/shard_map/ppermute | solution.py:66
  273.1 112.1 %reduce-scatter.6.cloned.1.call-start = ((), (), s32[]{:S(2)}) async-start(), calls=%async_computation.7 | async-start | bytes 5242880 | tf_op jit(solution)/shard_map/reduce_scatter | solution.py:1369
  332.4 134.0 %reduce-scatter.8.cloned.1.call-start = ((), (), s32[]{:S(2)}) async-start(), calls=%async_computation.8 | async-start | bytes 2621440 | tf_op jit(solution)/shard_map/reduce_scatter | solution.py:1369
  345.5 25.1 %collective-permute-start.63 = (bf16[256,512]{1,0:T(8,128)(2,1)S(1)}, bf16[256,512]{1,0:T(8,128)(2,1)S(1)}, u32[]{:S(2)}, u32[]{:S(2)}) collective-permute-start(bf16[256,512]{1,0:T(8,128)(2,1)S(1)} %select_bitcast_fusion.2), channel_id=1, source_target_pairs={{0,2},{2,0},{1,3},{3,1},{4,6},{6,4},{5,7},{7,5},{8,10},{10,8},{9,1... | collective-permute-start | bytes 786440 | tf_op jit(solution)/shard_map/ppermute | solution.py:70
  348.0 22.6 %collective-permute-start.61 = (bf16[192,1024]{1,0:T(8,128)(2,1)S(1)}, bf16[192,1024]{1,0:T(8,128)(2,1)}, u32[]{:S(2)}, u32[]{:S(2)}) collective-permute-start(bf16[192,1024]{1,0:T(8,128)(2,1)S(1)} %get-tuple-element.459.pa_ref), channel_id=1, source_target_pairs={{0,1},{1,0},{2,3},{3,2},{4,5},{5,4},{6,7},{7,6},{8,9},{9,8},{10,11... | collective-permute-start | bytes 1179656 | tf_op jit(solution)/shard_map/ppermute | solution.py:66
  349.3 21.3 %collective-permute-start.62 = (bf16[192,1024]{1,0:T(8,128)(2,1)S(1)}, bf16[192,1024]{1,0:T(8,128)(2,1)S(1)}, u32[]{:S(2)}, u32[]{:S(2)}) collective-permute-start(bf16[192,1024]{1,0:T(8,128)(2,1)S(1)} %get-tuple-element.459.pa_ref), channel_id=1, source_target_pairs={{0,4},{4,0},{1,5},{5,1},{2,6},{6,2},{3,7},{7,3},{8,12},{12,8},{9,1... | collective-permute-start | bytes 1179656 | tf_op jit(solution)/shard_map/ppermute | solution.py:62
  373.4 15.5 %collective-permute-start.65 = (bf16[192,1024]{1,0:T(8,128)(2,1)}, bf16[192,1024]{1,0:T(8,128)(2,1)}, u32[]{:S(2)}, u32[]{:S(2)}) collective-permute-start(bf16[192,1024]{1,0:T(8,128)(2,1)} %collective-permute-done.61.pb_ref), channel_id=1, source_target_pairs={{0,4},{4,0},{1,5},{5,1},{2,6},{6,2},{3,7},{7,3},{8,12},{12,8},{9,1... | collective-permute-start | bytes 1179656 | tf_op jit(solution)/shard_map/ppermute | solution.py:62
  374.4 38.4 %collective-permute-start.66 = (bf16[192,1024]{1,0:T(8,128)(2,1)}, bf16[192,1024]{1,0:T(8,128)(2,1)S(1)}, u32[]{:S(2)}, u32[]{:S(2)}) collective-permute-start(bf16[192,1024]{1,0:T(8,128)(2,1)} %add_convert_fusion.1), channel_id=1, source_target_pairs={{0,1},{1,0},{2,3},{3,2},{4,5},{5,4},{6,7},{7,6},{8,9},{9,8},{10,11... | collective-permute-start | bytes 1179656 | tf_op jit(solution)/shard_map/ppermute | solution.py:66
  386.4 27.2 %collective-permute-start.67 = (bf16[256,1024]{1,0:T(8,128)(2,1)S(1)}, bf16[256,1024]{1,0:T(8,128)(2,1)S(1)}, u32[]{:S(2)}, u32[]{:S(2)}) collective-permute-start(bf16[256,1024]{1,0:T(8,128)(2,1)S(1)} %broadcast_select_fusion), channel_id=1, source_target_pairs={{0,2},{2,0},{1,3},{3,1},{4,6},{6,4},{5,7},{7,5},{8,10},{10,8},{9,1... | collective-permute-start | bytes 1572872 | tf_op jit(solution)/shard_map/ppermute | solution.py:70
  450.4 27.0 %collective-permute-start.77 = (f32[48,128]{1,0:T(8,128)S(1)}, f32[48,128]{1,0:T(8,128)S(1)}, u32[]{:S(2)}, u32[]{:S(2)}) collective-permute-start(f32[48,128]{1,0:T(8,128)S(1)} %reduce_sum.28), channel_id=1, source_target_pairs={{0,1},{1,0},{2,3},{3,2},{4,5},{5,4},{6,7},{7,6},{8,9},{9,8},{10,11... | collective-permute-start | bytes 73736 | tf_op jit(solution)/shard_map/ppermute | solution.py:66
  476.9 19.3 %collective-permute-start.82 = (f32[128,512]{1,0:T(8,128)S(1)}, f32[128,512]{1,0:T(8,128)S(1)}, u32[]{:S(2)}, u32[]{:S(2)}) collective-permute-start(f32[128,512]{1,0:T(8,128)S(1)} %get-tuple-element.531), channel_id=1, source_target_pairs={{0,4},{4,0},{1,5},{5,1},{2,6},{6,2},{3,7},{7,3},{8,12},{12,8},{9,1... | collective-permute-start | bytes 786440 | tf_op jit(solution)/shard_map/ppermute | solution.py:62
  480.0 16.4 %collective-permute-start.87 = (f32[1,128]{1,0:T(1,128)S(1)}, f32[1,128]{1,0:T(1,128)S(1)}, u32[]{:S(2)}, u32[]{:S(2)}) collective-permute-start(f32[1,128]{1,0:T(1,128)S(1)} %fusion.26), channel_id=1, source_target_pairs={{0,2},{2,0},{1,3},{3,1},{4,6},{6,4},{5,7},{7,5},{8,10},{10,8},{9,1... | collective-permute-start | bytes 1544 | tf_op jit(solution)/shard_map/ppermute | solution.py:70
  480.5 15.8 %collective-permute-start.85 = (f32[1,128]{1,0:T(1,128)S(1)}, f32[1,128]{1,0:T(1,128)S(1)}, u32[]{:S(2)}, u32[]{:S(2)}) collective-permute-start(f32[1,128]{1,0:T(1,128)S(1)} %copy-done.217), channel_id=1, source_target_pairs={{0,1},{1,0},{2,3},{3,2},{4,5},{5,4},{6,7},{7,6},{8,9},{9,8},{10,11... | collective-permute-start | bytes 1544 | tf_op jit(solution)/shard_map/ppermute | solution.py:66
  (296 other events, 2116.9 us)
Sparse Core Ops, SparseCore 0:
  82.2 53.0 all-gather.3
  168.1 33.4 all-gather.5
  273.2 34.3 reduce-scatter.3
  332.6 52.5 reduce-scatter.5
  430.4 35.9 reduce-scatter.7

commit v3 on v2

--- a/solution.py
+++ b/solution.py
@@ -21,7 +21,7 @@
 highest = lax.Precision.HIGHEST
 swap_pairs = ((0, 1), (1, 0))
 busy_us = {
-    "row_layout": 2, "enter": 5, "enter_first": 6, "attend": 11, "onward": 4, "feed": 9, "head": 6, "merge": 2,
+    "row_layout": 2, "enter": 5, "enter_first": 6, "attend": 11, "onward": 2, "feed": 5, "head": 6, "merge": 2,
     "head_back": 5, "back": 5, "feed_back": 7, "attend_back": 16, "old_stats": 4, "row_stats": 3,
     "column_stats": 5, "finish": 2, "head_grad": 6, "feed_grad": 12, "first_grad": 6,
     "renew": 8, "arrange": 4,
@@ -170,7 +170,7 @@
         out_specs=out_specs,
         out_shape=[jax.ShapeDtypeStruct(shape, dtype) for shape, dtype in out_shape],
         scratch_shapes=scratch,
-        compiler_params=pltpu.CompilerParams(vmem_limit_bytes=48 * 2**20),
+        compiler_params=pltpu.CompilerParams(vmem_limit_bytes=62 * 2**20),
         cost_estimate=cost(name),
         name=name,
     )
@@ -207,6 +207,7 @@
             jax.ShapeDtypeStruct(shape, jnp.int32),
             jax.ShapeDtypeStruct((1, 1), jnp.int32),
         ],
+        compiler_params=pltpu.CompilerParams(vmem_limit_bytes=62 * 2**20),
         cost_estimate=cost("row_layout"),
         name="row_layout",
     )(level_weight, segment, live)
@@ -259,7 +260,7 @@
         in_specs=[pl.BlockSpec(memory_space=pltpu.SMEM)] + [pl.BlockSpec(memory_space=pltpu.VMEM)] * 4,
         out_shape=[jax.ShapeDtypeStruct(shape, dtype) for shape, dtype in shapes],
         scratch_shapes=[pltpu.VMEM((n, 128), full_type), pltpu.VMEM((n, code_dim), full_type)],
-        compiler_params=pltpu.CompilerParams(vmem_limit_bytes=48 * 2**20),
+        compiler_params=pltpu.CompilerParams(vmem_limit_bytes=62 * 2**20),
         cost_estimate=cost("arrange"),
         name="arrange",
     )(at, mine, other, vq, vq_other)
@@ -586,6 +587,7 @@
         merge_kernel,
         in_specs=[pl.BlockSpec(memory_space=pltpu.SMEM)] + [pl.BlockSpec(memory_space=pltpu.VMEM)] * 5,
         out_shape=[jax.ShapeDtypeStruct((n, 128), full_type), jax.ShapeDtypeStruct((1, 128), full_type)],
+        compiler_params=pltpu.CompilerParams(vmem_limit_bytes=62 * 2**20),
         cost_estimate=cost("merge"),
         name="merge",
     )(weight_sum[None], here, over_core, over_line, over_both, weights)
@@ -635,7 +637,7 @@
     return pl.pallas_call(
         old_stats_kernel,
         out_shape=jax.ShapeDtypeStruct((2, 128), full_type),
-        compiler_params=pltpu.CompilerParams(vmem_limit_bytes=48 * 2**20),
+        compiler_params=pltpu.CompilerParams(vmem_limit_bytes=62 * 2**20),
         cost_estimate=cost("old_stats"),
         name="old_stats",
     )(*olds)
@@ -738,7 +740,7 @@
     return pl.pallas_call(
         row_stats_kernel,
         out_shape=jax.ShapeDtypeStruct((8, n), full_type),
-        compiler_params=pltpu.CompilerParams(vmem_limit_bytes=48 * 2**20),
+        compiler_params=pltpu.CompilerParams(vmem_limit_bytes=62 * 2**20),
         cost_estimate=cost("row_stats"),
         name="row_stats",
     )(*gradients)
@@ -802,7 +804,7 @@
         ],
         in_specs=[pl.BlockSpec(memory_space=pltpu.SMEM)]
         + [pl.BlockSpec(memory_space=pltpu.VMEM)] * (5 + len(gradients)),
-        compiler_params=pltpu.CompilerParams(vmem_limit_bytes=48 * 2**20),
+        compiler_params=pltpu.CompilerParams(vmem_limit_bytes=62 * 2**20),
         cost_estimate=cost("column_stats"),
         name="column_stats",
     )(at_c[None], row_new, old, tail, tables_sum, scales, *gradients)
@@ -843,6 +845,7 @@
         functools.partial(finish_kernel, decay=decay, width=width, starts=starts),
         out_shape=[jax.ShapeDtypeStruct(col_old.shape, full_type)]
         + [jax.ShapeDtypeStruct((1, 128), full_type)] * 4,
+        compiler_params=pltpu.CompilerParams(vmem_limit_bytes=62 * 2**20),
         cost_estimate=cost("finish"),
         name="finish",
     )(flat, col_old, scale_line)
@@ -1027,7 +1030,7 @@
 def attend_back_kernel(
     q_ref, k_ref, v_ref, gain_ref, col_ref, line_ref, lse_ref, pa_ref, pb_ref, pc_ref, pd_ref,
     proj_ref, wq_ref, wk_ref, wv_ref, row_ref, d_ref, ds_ref, top_ref, bottom_ref,
-    q_s, k_s, v_s, dm_ref, dqa, dka, dva, sum_s, *, tile
+    q_s, k_s, v_s, dm_ref, dqa, dka, dva, bias_s, sum_s
 ):
     length = q_ref.shape[0]
     first = head_lanes((length, 128))
@@ -1050,36 +1053,43 @@
         for k, ref in enumerate((pa_ref, pb_ref, pc_ref, pd_ref)):
             row_ref[k * quarter : (k + 1) * quarter, :] = ref[...]
 
-    dka[...] = jnp.zeros_like(dka)
-    dva[...] = jnp.zeros_like(dva)
+    tile = length // 2
     first_t = head_lanes((tile, 128))
-    ck = col_ref[:, 2:3]
-
-    def step(i, carry):
-        rows = pl.ds(pl.multiple_of(i * tile, tile), tile)
+
+    @pl.when(pl.program_id(0) == 0)
+    def _():
+        ck = col_ref[:, 2:3]
+        for i in range(2):
+            rows = slice(i * tile, (i + 1) * tile)
+            shape = (length, tile)
+            here = lax.broadcasted_iota(jnp.int32, shape, 0) - lax.broadcasted_iota(jnp.int32, shape, 1)
+            keep = ((ck <= line_ref[0:1, rows]) & (ck >= line_ref[1:2, rows])) | (here == i * tile)
+            bias_s[:, rows] = jnp.where(keep, 0.0, -1e30)
+
+    d_keys, d_values = None, None
+    for i in range(2):
+        rows = slice(i * tile, (i + 1) * tile)
         query_t = q_s[rows, :]
         dmix_t = dm_ref[rows, :]
-        shape = (length, tile)
-        here = lax.broadcasted_iota(jnp.int32, shape, 0) - lax.broadcasted_iota(jnp.int32, shape, 1)
-        keep = ((ck <= line_ref[0:1, rows]) & (ck >= line_ref[1:2, rows])) | (here == i * tile)
         d_query = []
         for head in range(2):
             chosen = first_t if head == 0 else ~first_t
             zero = jnp.zeros_like(query_t)
             query_h = jnp.where(chosen, query_t, zero)
             dmix_h = jnp.where(chosen, dmix_t, zero)
-            scores = dot_nt(k_s[...], query_h)
-            attention = jnp.where(keep, jnp.exp(scores - lse_ref[0, head : head + 1, rows]), 0.0)
-            dva[...] += dot_nn(low(attention), dmix_h)
+            scores = dot_nt(k_s[...], query_h) + bias_s[:, rows]
+            attention = jnp.exp(scores - lse_ref[0, head : head + 1, rows])
+            part = dot_nn(low(attention), dmix_h)
+            d_values = part if d_values is None else d_values + part
             d_att = dot_nt(v_s[...], dmix_h)
             inner = jnp.sum(attention * d_att, 0, keepdims=True)
             d_scores = low(attention * (d_att - inner))
-            dka[...] += dot_nn(d_scores, query_h)
+            part = dot_nn(d_scores, query_h)
+            d_keys = part if d_keys is None else d_keys + part
             d_query.append(dot_tn(d_scores, k_s[...]))
         dqa[rows, :] = jnp.where(first_t, d_query[0], d_query[1])
-        return carry
-
-    lax.fori_loop(0, length // tile, step, 0)
+    dka[...] = d_keys
+    dva[...] = d_values
     q_hat = query * q_n
     k_hat = key * k_n
     d_query = dqa[...]
@@ -1120,7 +1130,7 @@
         return pl.BlockSpec((rows, 128), lambda p: (0, number * pairs + p))
 
     return call(
-        functools.partial(attend_back_kernel, tile=256),
+        attend_back_kernel,
         (pairs,),
         [
             part(length, 0),
@@ -1149,7 +1159,7 @@
         ],
         [pltpu.VMEM((length, 128), low_type)] * 4
         + [pltpu.VMEM((length, 128), full_type)] * 3
-        + [pltpu.VMEM((length, width), full_type)],
+        + [pltpu.VMEM((length, length), full_type), pltpu.VMEM((length, width), full_type)],
         "attend_back",
     )(qkv, qkv, qkv, gain, cols, rows, lse, *pieces, proj, w, w, w)
 

time: 576 us -> 573 us (level)
  local copies, waits for them, and re-layouts: 107 us -> 42.8 us
  Pallas kernels: 191 us -> 246 us
  other arithmetic: 22.8 us -> 37.9 us
  waiting for transfers between devices: 131 us -> 121 us
    unnamed x468 -> x224, local copies, waits for them, and re-layouts: 85.9 us -> 18.2 us
    pallas_call x6, Pallas kernels: 11.5 us -> 26.2 us  [back(): call(functools.partial(back_kernel, gated=gated, carried=has, picks=picks...]
    ppermute x25, waiting for transfers between devices: 36.7 us -> 50.7 us  [over_l(): return lax.ppermute(a, 'l', swap_pairs)]
    all_gather x2, waiting for transfers between devices: 14.8 us -> 1.12 us  [gathered_weight(): wide = lax.all_gather(a.reshape(-1, a.shape[2]), 'g', axis=0, tiled=True)]
    pallas_call x4, Pallas kernels: 5.1 us -> 12.7 us  [onward(): call(functools.partial(onward_kernel, picks=picks), (n // tile,), [tiled(...]
    convert_element_type x12, other arithmetic: 2.11 us -> 9.22 us  [low(): return a.astype(low_type)]
  transfers between devices with their start and end apart: 99 -> 99, of which waited for: 34 -> 39; matrix products, arithmetic and copies ran while one was open for 9% -> 12% of each run, Pallas kernels for 31% -> 40%
where the time goes in v3:
time: 573 us; the launch traced here: 564 us
  Pallas kernels  246 us (43%)
  waiting for transfers between devices  121 us (21%)
  starting transfers between devices  77.8 us (14%)
  local copies, waits for them, and re-layouts  42.8 us (7%)
  other arithmetic  37.9 us (7%)
  between operations  20 us (3%)
  matrix products  10 us (2%)
  blocking collectives  9.24 us (2%)
    ppermute x25, waiting for transfers between devices, over_l(): return lax.ppermute(a, 'l', swap_pairs)  50.7 us
    pallas_call x2, Pallas kernels, attend_back(): call(attend_back_kernel, (pairs,), [part(length, 0), part(length, 1), par...  41.3 us
    ppermute x25, starting transfers between devices, over_l(): return lax.ppermute(a, 'l', swap_pairs)  29.7 us
    pallas_call x6, Pallas kernels, back(): call(functools.partial(back_kernel, gated=gated, carried=has, picks=picks...  26.2 us
    pallas_call x2, Pallas kernels, attend(): call(attend_kernel, (pairs,), [block, pl.BlockSpec((length, 128), lambda...  23.6 us
    reduce_scatter x3, waiting for transfers between devices, reduced(): lax.psum_scatter(a.reshape(-1, shape[2]), 'g', scatter_dimension=0, tiled...  22.7 us
    ppermute x13, starting transfers between devices, over_h(): return lax.ppermute(a, 'h', swap_pairs)  22 us
    ppermute x11, waiting for transfers between devices, over_g(): return lax.ppermute(a, 'g', [(i, i ^ k) for i in range(lax.axis_size('g'))])  21.4 us
  transfers between devices with their start and end apart: 99, of which 39 were waited for; matrix products, arithmetic and copies ran while one was open for 12% of the time, Pallas kernels for 40%

profile of v3, /device:TPU:0, one launch (start us, length us, event | category | flops | bytes accessed | tf_op | source)
XLA Modules:
  0.0 564.5 jit_solution(11320157396348865255)
XLA Ops:
  22.4 9.2 %all-gather = bf16[384,128]{1,0:T(8,128)(2,1)S(1)} all-gather(bf16[48,128]{1,0:T(8,128)(2,1)S(1)} %pad_maximum_fusion.2), channel_id=2, replica_groups=mesh['g'=4,'c'=2,'h'=2,'l'=2] {'g','c'}, dimensions={0}, use_global_device_ids=true | all-gather | bytes 110592 | tf_op jit(solution)/shard_map/all_gather | solution.py:1210
  59.0 4.5 arrange.1
  65.1 8.2 %collective-permute-done.6.c_ref = bf16[2,4,256,128]{3,2,1,0:T(8,128)(2,1)} collective-permute-done((bf16[2,4,256,128]{3,2,1,0:T(8,128)(2,1)}, bf16[2,4,256,128]{3,2,1,0:T(8,128)(2,1)}, u32[]{:S(2)}, u32[]{:S(2)}) %collective-permute-start.6) | collective-permute-done | bytes 524320 | tf_op jit(solution)/shard_map/ppermute | solution.py:78
  84.9 7.7 %enter_first.1 = (bf16[768,1024]{1,0:T(8,128)(2,1)}, f32[768,768]{1,0:T(8,128)}, f32[192,1024]{1,0:T(8,128)}, bf16[1024,768]{1,0:T(8,128)(2,1)}, bf16[1024,256]{1,0:T(8,128)(2,1)}) custom-call(s32[1]{0:T(128)} %bitcast.1.at_ref, bf16[768,48]{1,0:T(8,128)(2,1)} %get-tuple-element.302.feat_ref.refs_7_, bf16[48,1024]{1,0:T(8,128)(2,1)} %bitcast.204, ...), custom_call_target="tpu_custom_call" | custom-call | flops 6000000000 | bytes 6000000 | tf_op jit(solution)/shard_map/enter_first/pallas_call | solution.py:335
  92.6 11.7 %attend.2 = (bf16[768,256]{1,0:T(8,128)(2,1)}, f32[2,2,768]{2,1,0:T(2,128)}, bf16[384,1024]{1,0:T(8,128)(2,1)}, bf16[384,1024]{1,0:T(8,128)(2,1)}) custom-call(f32[768,768]{1,0:T(8,128)} %get-tuple-element.308.q_ref.k_ref.v_ref, f32[768,768]{1,0:T(8,128)} %get-tuple-element.308.q_ref.k_ref.v_ref, f32[768,768]{1,0:T(8,128)} %get-tuple-element.308.q_ref.k_ref.v_ref, ...), custom_call_target="tpu_custom_call" | custom-call | flops 11000000512 | bytes 11000000 | tf_op jit(solution)/shard_map/attend/pallas_call | solution.py:1009
  104.6 7.1 %enter.1 = (bf16[768,1024]{1,0:T(8,128)(2,1)}, f32[768,768]{1,0:T(8,128)}, f32[192,1024]{1,0:T(8,128)}) custom-call(bf16[768,48]{1,0:T(8,128)(2,1)} %get-tuple-element.320.feat_ref.refs_7_, bf16[48,1024]{1,0:T(8,128)(2,1)} %bitcast.205, bf16[768,16]{1,0:T(8,128)(2,1)} %get-tuple-element.321.hot_ref.refs_4_, ...), custom_call_target="tpu_custom_call" | custom-call | flops 5000000000 | bytes 5000000 | tf_op jit(solution)/shard_map/enter/pallas_call | solution.py:300
  115.1 11.9 %attend.3 = (bf16[768,256]{1,0:T(8,128)(2,1)}, f32[2,2,768]{2,1,0:T(2,128)}, bf16[384,1024]{1,0:T(8,128)(2,1)}, bf16[384,1024]{1,0:T(8,128)(2,1)}) custom-call(f32[768,768]{1,0:T(8,128)} %get-tuple-element.328.q_ref.k_ref.v_ref, f32[768,768]{1,0:T(8,128)} %get-tuple-element.328.q_ref.k_ref.v_ref, f32[768,768]{1,0:T(8,128)} %get-tuple-element.328.q_ref.k_ref.v_ref, ...), custom_call_target="tpu_custom_call" | custom-call | flops 11000000512 | bytes 11000000 | tf_op jit(solution)/shard_map/attend/pallas_call | solution.py:1009
  134.2 9.9 %collective-permute-done.21.c_ref = bf16[192,1024]{1,0:T(8,128)(2,1)S(1)} collective-permute-done((bf16[192,1024]{1,0:T(8,128)(2,1)S(1)}, bf16[192,1024]{1,0:T(8,128)(2,1)S(1)}, u32[]{:S(2)}, u32[]{:S(2)}) %collective-permute-start.21) | collective-permute-done | bytes 393248 | tf_op jit(solution)/shard_map/ppermute | solution.py:66
  154.1 10.0 %feed.2 = (bf16[768,1024]{1,0:T(8,128)(2,1)}, bf16[768,1024]{1,0:T(8,128)(2,1)}, f32[768,1024]{1,0:T(8,128)}, bf16[384,1024]{1,0:T(8,128)(2,1)}, bf16[384,1024]{1,0:T(8,128)(2,1)}) custom-call(bf16[192,1024]{1,0:T(8,128)(2,1)} %get-tuple-element.337.a_ref, bf16[192,1024]{1,0:T(8,128)(2,1)} %copy-done.71, bf16[192,1024]{1,0:T(8,128)(2,1)} %copy-done.70, ...), custom_call_target="tpu_custom_call" | custom-call | flops 5000000000 | bytes 5000000 | tf_op jit(solution)/shard_map/feed/pallas_call | solution.py:493
  170.5 9.4 %feed.3 = (bf16[768,1024]{1,0:T(8,128)(2,1)}, bf16[768,1024]{1,0:T(8,128)(2,1)}, f32[768,1024]{1,0:T(8,128)}, bf16[384,1024]{1,0:T(8,128)(2,1)}, bf16[384,1024]{1,0:T(8,128)(2,1)}) custom-call(bf16[192,1024]{1,0:T(8,128)(2,1)} %get-tuple-element.352.a_ref, bf16[192,1024]{1,0:T(8,128)(2,1)} %copy-done.73, bf16[192,1024]{1,0:T(8,128)(2,1)} %copy-done.74, ...), custom_call_target="tpu_custom_call" | custom-call | flops 5000000000 | bytes 5000000 | tf_op jit(solution)/shard_map/feed/pallas_call | solution.py:493
  187.3 8.8 %collective-permute-done.31.c_ref = bf16[192,1024]{1,0:T(8,128)(2,1)S(1)} collective-permute-done((bf16[192,1024]{1,0:T(8,128)(2,1)S(1)}, bf16[192,1024]{1,0:T(8,128)(2,1)S(1)}, u32[]{:S(2)}, u32[]{:S(2)}) %collective-permute-start.31) | collective-permute-done | bytes 393248 | tf_op jit(solution)/shard_map/ppermute | solution.py:66
  206.1 5.9 %head.2 = (bf16[768,1024]{1,0:T(8,128)(2,1)}, f32[768,1024]{1,0:T(8,128)}, f32[8,768]{1,0:T(8,128)}) custom-call(bf16[192,1024]{1,0:T(8,128)(2,1)} %get-tuple-element.361.a_ref, bf16[192,1024]{1,0:T(8,128)(2,1)} %copy-done.80, bf16[192,1024]{1,0:T(8,128)(2,1)} %copy-done.77, bf16[192,1024]{1,0:T(8,128)(2,1)} %copy-done.91, ...), custom_call_target="tpu_custom_call" | custom-call | flops 6000000000 | bytes 6000000 | tf_op jit(solution)/shard_map/head/pallas_call | solution.py:549
  220.1 5.9 %head.3 = (bf16[768,1024]{1,0:T(8,128)(2,1)}, f32[768,1024]{1,0:T(8,128)}, f32[8,768]{1,0:T(8,128)}) custom-call(bf16[192,1024]{1,0:T(8,128)(2,1)} %get-tuple-element.375.a_ref, bf16[192,1024]{1,0:T(8,128)(2,1)} %copy-done.78, bf16[192,1024]{1,0:T(8,128)(2,1)} %copy-done.81, bf16[192,1024]{1,0:T(8,128)(2,1)} %copy-done.88, ...), custom_call_target="tpu_custom_call" | custom-call | flops 6000000000 | bytes 6000000 | tf_op jit(solution)/shard_map/head/pallas_call | solution.py:549
  230.2 6.3 %head_back.2 = (bf16[768,1024]{1,0:T(8,128)(2,1)}, bf16[384,1024]{1,0:T(8,128)(2,1)}, bf16[384,1024]{1,0:T(8,128)(2,1)}) custom-call(f32[768,1024]{1,0:T(8,128)} %get-tuple-element.371.logit_ref, bf16[4,2,256,512]{3,2,1,0:T(8,128)(2,1)} %bitcast.223, f32[768,128]{1,0:T(8,128)} %get-tuple-element.309.col_ref.code_ref, f32[1,1024]{1,0:T(1,128)} %fusion.15.column_ref, ...), custom_call_target="tpu_custom_call" | custom-call | flops 5000000000 | bytes 5000000 | tf_op jit(solution)/shard_map/head_back/pallas_call | solution.py:610
  240.6 6.2 %head_back.3 = (bf16[768,1024]{1,0:T(8,128)(2,1)}, bf16[384,1024]{1,0:T(8,128)(2,1)}, bf16[384,1024]{1,0:T(8,128)(2,1)}) custom-call(f32[768,1024]{1,0:T(8,128)} %get-tuple-element.389.logit_ref, bf16[4,2,256,512]{3,2,1,0:T(8,128)(2,1)} %bitcast.224, f32[768,128]{1,0:T(8,128)} %get-tuple-element.329.col_ref.code_ref, f32[1,1024]{1,0:T(1,128)} %fusion.15.column_ref, ...), custom_call_target="tpu_custom_call" | custom-call | flops 5000000000 | bytes 5000000 | tf_op jit(solution)/shard_map/head_back/pallas_call | solution.py:610
  257.3 7.0 %head_grad.1 = bf16[4,2,256,512]{3,2,1,0:T(8,128)(2,1)} custom-call(bf16[768,1024]{1,0:T(8,128)(2,1)} %get-tuple-element.404.a_ref, bf16[768,1024]{1,0:T(8,128)(2,1)} %get-tuple-element.405.b_ref, bf16[768,1024]{1,0:T(8,128)(2,1)} %get-tuple-element.406.c_ref, bf16[768,1024]{1,0:T(8,128)(2,1)} %get-tuple-element.407.d_ref), custom_call_target="tpu_custom_call" | custom-call | flops 6000000000 | bytes 6000000 | tf_op jit(solution)/shard_map/head_grad/pallas_call | solution.py:660
  272.5 4.9 collective-permute-done.49.b_ref
  279.9 9.0 %feed_back.2 = (bf16[768,1024]{1,0:T(8,128)(2,1)}, bf16[768,1024]{1,0:T(8,128)(2,1)}, bf16[384,1024]{1,0:T(8,128)(2,1)}, bf16[384,1024]{1,0:T(8,128)(2,1)}) custom-call(bf16[192,1024]{1,0:T(8,128)(2,1)} %get-tuple-element.401.a_ref, bf16[192,1024]{1,0:T(8,128)(2,1)} %copy-done.84, bf16[192,1024]{1,0:T(8,128)(2,1)} %copy-done.69, ...), custom_call_target="tpu_custom_call" | custom-call | flops 7000000000 | bytes 7000000 | tf_op jit(solution)/shard_map/feed_back/pallas_call | solution.py:522
  295.1 8.7 %feed_back.3 = (bf16[768,1024]{1,0:T(8,128)(2,1)}, bf16[768,1024]{1,0:T(8,128)(2,1)}, bf16[384,1024]{1,0:T(8,128)(2,1)}, bf16[384,1024]{1,0:T(8,128)(2,1)}) custom-call(bf16[192,1024]{1,0:T(8,128)(2,1)} %get-tuple-element.421.a_ref, bf16[192,1024]{1,0:T(8,128)(2,1)} %copy-done.75, bf16[192,1024]{1,0:T(8,128)(2,1)} %copy-done.79, ...), custom_call_target="tpu_custom_call" | custom-call | flops 7000000000 | bytes 7000000 | tf_op jit(solution)/shard_map/feed_back/pallas_call | solution.py:522
  305.4 4.5 back.8
  312.0 12.6 %feed_grad.1 = bf16[4,2,256,1024]{3,2,1,0:T(8,128)(2,1)} custom-call(bf16[768,1024]{1,0:T(8,128)(2,1)} %get-tuple-element.436.a_ref, bf16[768,1024]{1,0:T(8,128)(2,1)} %get-tuple-element.437.b_ref, bf16[768,1024]{1,0:T(8,128)(2,1)} %get-tuple-element.438.c_ref, bf16[768,1024]{1,0:T(8,128)(2,1)} %get-tuple-element.439.d_ref, ...), custom_call_target="tpu_custom_call" | custom-call | flops 12000000000 | bytes 12000000 | tf_op jit(solution)/shard_map/feed_grad/pallas_call | solution.py:686
  327.1 4.7 back.9
  331.7 5.7 %collective-permute-done.59.pb_ref = bf16[192,1024]{1,0:T(8,128)(2,1)S(1)} collective-permute-done((bf16[192,1024]{1,0:T(8,128)(2,1)S(1)}, bf16[192,1024]{1,0:T(8,128)(2,1)S(1)}, u32[]{:S(2)}, u32[]{:S(2)}) %collective-permute-start.59) | collective-permute-done | bytes 393248 | tf_op jit(solution)/shard_map/ppermute | solution.py:66
  342.7 20.6 %attend_back.2 = (bf16[768,1024]{1,0:T(8,128)(2,1)}, bf16[768,768]{1,0:T(8,128)(2,1)}, f32[2,1,128]{2,1,0:T(1,128)}, bf16[384,1024]{1,0:T(8,128)(2,1)}, bf16[384,1024]{1,0:T(8,128)(2,1)}) custom-call(f32[768,768]{1,0:T(8,128)} %get-tuple-element.308.q_ref.k_ref.v_ref, f32[768,768]{1,0:T(8,128)} %get-tuple-element.308.q_ref.k_ref.v_ref, ...), custom_call_target="tpu_custom_call" | custom-call | flops 16000000000 | bytes 16000000 | tf_op jit(solution)/shard_map/attend_back/pallas_call | solution.py:1132
  369.7 7.7 %reduce-scatter.6.cloned.1.call-done = bf16[512,1024]{1,0:T(8,128)(2,1)} async-done(((bf16[2048,1024]{1,0:T(8,128)(2,1)}), bf16[512,1024]{1,0:T(8,128)(2,1)}) %reduce-scatter.6.cloned.1.call-update) | async-done | bytes 1048592 | tf_op jit(solution)/shard_map/reduce_scatter | solution.py:1379
  382.6 20.6 %attend_back.3 = (bf16[768,1024]{1,0:T(8,128)(2,1)}, bf16[768,768]{1,0:T(8,128)(2,1)}, f32[2,1,128]{2,1,0:T(1,128)}, bf16[384,1024]{1,0:T(8,128)(2,1)}, bf16[384,1024]{1,0:T(8,128)(2,1)}) custom-call(f32[768,768]{1,0:T(8,128)} %get-tuple-element.328.q_ref.k_ref.v_ref, f32[768,768]{1,0:T(8,128)} %get-tuple-element.328.q_ref.k_ref.v_ref, ...), custom_call_target="tpu_custom_call" | custom-call | flops 16000000000 | bytes 16000000 | tf_op jit(solution)/shard_map/attend_back/pallas_call | solution.py:1132
  414.6 10.2 %first_grad.1 = bf16[4,2,256,512]{3,2,1,0:T(8,128)(2,1)} custom-call(bf16[768,1024]{1,0:T(8,128)(2,1)} %get-tuple-element.471.a_ref, bf16[768,1024]{1,0:T(8,128)(2,1)} %get-tuple-element.472.b_ref, bf16[768,768]{1,0:T(8,128)(2,1)} %get-tuple-element.475.c_ref, bf16[768,768]{1,0:T(8,128)(2,1)} %get-tuple-element.476.d_ref, ...), custom_call_target="tpu_custom_call" | custom-call | flops 6000000000 | bytes 6000000 | tf_op jit(solution)/shard_map/first_grad/pallas_call | solution.py:712
  442.4 4.7 all-to-all-done
  447.8 15.0 %reduce-scatter.8.cloned.1.call-done = bf16[512,512]{1,0:T(8,128)(2,1)} async-done(((bf16[2048,512]{1,0:T(8,128)(2,1)}), bf16[512,512]{1,0:T(8,128)(2,1)}) %reduce-scatter.8.cloned.1.call-update) | async-done | bytes 524304 | tf_op jit(solution)/shard_map/reduce_scatter | solution.py:1379
  487.7 4.6 collective-permute-done.79
  510.4 5.9 %column_stats.1 = (f32[2,12416]{1,0:T(2,128)}, f32[8,128]{1,0:T(8,128)}) custom-call(s32[1]{0:T(128)} %bitcast.at_ref, f32[5,128]{1,0:T(8,128)} %fusion.20.row_ref, f32[1,128]{1,0:T(1,128)} %slice.422.old_ref, f32[1,128]{1,0:T(1,128)} %get-tuple-element.526.tail_ref, f32[1,1]{1,0:T(1,128)} %bitcast.74.tables_ref, f32[1,128]{1,0:T(1,128)} %fusion.25.scale_ref, ...), custom_call_target="tpu_custom_call" | custom-call | flops 5000000000 | bytes 5000000 | tf_op jit(solution)/shard_map/column_stats/pallas_call | solution.py:799
  543.2 12.3 %renew.1 = (f32[3,128,256]{2,1,0:T(8,128)}, f32[256,128]{1,0:T(8,128)}, f32[128,1024]{1,0:T(8,128)}, f32[1024,128]{1,0:T(8,128)}, f32[128,1024]{1,0:T(8,128)}, /...) custom-call(f32[1,128]{1,0:T(1,128)} %slice.476.line_ref, ...), custom_call_target="tpu_custom_call" | custom-call | flops 8000000000 | bytes 8000000 | tf_op jit(solution)/shard_map/renew/pallas_call | solution.py:924
  (566 shorter events, 262.8 us)
Async XLA Ops:
  7.2 146.9 %all-gather.4.cloned.1.call-start = ((), (), s32[]{:S(2)}) async-start(), calls=%async_computation.4 | async-start | bytes 5242880 | tf_op jit(solution)/shard_map/all_gather | solution.py:1249
  13.6 37.7 %collective-permute-start.3 = (f32[2,4,768]{2,1,0:T(4,128)S(1)}, f32[2,4,768]{2,1,0:T(4,128)S(1)}, u32[]{:S(2)}, u32[]{:S(2)}) collective-permute-start(f32[2,4,768]{2,1,0:T(4,128)S(1)} %add_convert_fusion.11.mine_ref), channel_id=1, source_target_pairs={{0,4},{4,0},{1,5},{5,1},{2,6},{6,2},{3,7},{7,3},{8,12},{12,8},{9,1... | collective-permute-start | bytes 73736 | tf_op jit(solution)/shard_map/ppermute | solution.py:62
  14.6 42.8 %collective-permute-start.4 = (bf16[2,768,32]{2,1,0:T(8,128)(2,1)}, bf16[2,768,32]{2,1,0:T(8,128)(2,1)}, u32[]{:S(2)}, u32[]{:S(2)}) collective-permute-start(bf16[2,768,32]{2,1,0:T(8,128)(2,1)} %copy.71.vq_ref), channel_id=1, source_target_pairs={{0,4},{4,0},{1,5},{5,1},{2,6},{6,2},{3,7},{7,3},{8,12},{12,8},{9,1... | collective-permute-start | bytes 294920 | tf_op jit(solution)/shard_map/ppermute | solution.py:62
  18.0 16.2 %collective-permute-start.1 = (bf16[4,256,128]{2,1,0:T(8,128)(2,1)S(1)}, bf16[4,256,128]{2,1,0:T(8,128)(2,1)S(1)}, u32[]{:S(2)}, u32[]{:S(2)}) collective-permute-start(bf16[4,256,128]{2,1,0:T(8,128)(2,1)S(1)} %maximum_select_fusion.7), channel_id=1, source_target_pairs={{0,2},{2,0},{1,3},{3,1},{4,6},{6,4},{5,7},{7,5},{8,10},{10,8},{9,1... | collective-permute-start | bytes 786440 | tf_op jit(solution)/shard_map/ppermute | solution.py:70
  45.8 17.7 %collective-permute-start.5 = (bf16[2,4,256,128]{3,2,1,0:T(8,128)(2,1)}, bf16[2,4,256,128]{3,2,1,0:T(8,128)(2,1)}, u32[]{:S(2)}, u32[]{:S(2)}) collective-permute-start(bf16[2,4,256,128]{3,2,1,0:T(8,128)(2,1)} %maximum_select_fusion.2.a_ref), channel_id=1, source_target_pairs={{0,8},{8,0},{16,24},{24,16},{1,9},{9,1},{17,25},{25,17},{2,10},{10... | collective-permute-start | bytes 1572872 | tf_op jit(solution)/shard_map/ppermute | solution.py:78
  47.4 25.9 %collective-permute-start.6 = (bf16[2,4,256,128]{3,2,1,0:T(8,128)(2,1)}, bf16[2,4,256,128]{3,2,1,0:T(8,128)(2,1)}, u32[]{:S(2)}, u32[]{:S(2)}) collective-permute-start(bf16[2,4,256,128]{3,2,1,0:T(8,128)(2,1)} %maximum_select_fusion.2.a_ref), channel_id=1, source_target_pairs={{0,16},{8,24},{16,0},{24,8},{1,17},{9,25},{17,1},{25,9},{2,18},{10... | collective-permute-start | bytes 1572872 | tf_op jit(solution)/shard_map/ppermute | solution.py:78
  50.0 24.9 %collective-permute-start.7 = (bf16[2,4,256,128]{3,2,1,0:T(8,128)(2,1)}, bf16[2,4,256,128]{3,2,1,0:T(8,128)(2,1)}, u32[]{:S(2)}, u32[]{:S(2)}) collective-permute-start(bf16[2,4,256,128]{3,2,1,0:T(8,128)(2,1)} %maximum_select_fusion.2.a_ref), channel_id=1, source_target_pairs={{0,24},{8,16},{16,8},{24,0},{1,25},{9,17},{17,9},{25,1},{2,26},{10... | collective-permute-start | bytes 1572872 | tf_op jit(solution)/shard_map/ppermute | solution.py:78
  51.3 25.8 %collective-permute-start.10 = (bf16[256,1024]{1,0:T(8,128)(2,1)}, bf16[256,1024]{1,0:T(8,128)(2,1)S(1)}, u32[]{:S(2)}, u32[]{:S(2)}) collective-permute-start(bf16[256,1024]{1,0:T(8,128)(2,1)} %get-tuple-element.539), channel_id=1, source_target_pairs={{0,2},{2,0},{1,3},{3,1},{4,6},{6,4},{5,7},{7,5},{8,10},{10,8},{9,1... | collective-permute-start | bytes 1572872 | tf_op jit(solution)/shard_map/ppermute | solution.py:70
  57.4 20.9 %collective-permute-start.12 = (f32[8,4096]{1,0:T(8,128)}, f32[8,4096]{1,0:T(8,128)}, u32[]{:S(2)}, u32[]{:S(2)}) collective-permute-start(f32[8,4096]{1,0:T(8,128)} %get-tuple-element.540), channel_id=1, source_target_pairs={{0,8},{8,0},{16,24},{24,16},{1,9},{9,1},{17,25},{25,17},{2,10},{10... | collective-permute-start | bytes 393224 | tf_op jit(solution)/shard_map/ppermute | solution.py:78
  63.5 14.8 %collective-permute-start.13 = (f32[8,4096]{1,0:T(8,128)}, f32[8,4096]{1,0:T(8,128)S(1)}, u32[]{:S(2)}, u32[]{:S(2)}) collective-permute-start(f32[8,4096]{1,0:T(8,128)} %get-tuple-element.542), channel_id=1, source_target_pairs={{0,16},{8,24},{16,0},{24,8},{1,17},{9,25},{17,1},{25,9},{2,18},{10... | collective-permute-start | bytes 393224 | tf_op jit(solution)/shard_map/ppermute | solution.py:78
  81.6 105.8 %all-gather.6.cloned.1.call-start = ((), (), s32[]{:S(2)}) async-start(), calls=%async_computation.5 | async-start | bytes 2621440 | tf_op jit(solution)/shard_map/all_gather | solution.py:1249
  81.8 22.5 %collective-permute-start.17 = (bf16[256,512]{1,0:T(8,128)(2,1)S(1)}, bf16[256,512]{1,0:T(8,128)(2,1)S(1)}, u32[]{:S(2)}, u32[]{:S(2)}) collective-permute-start(bf16[256,512]{1,0:T(8,128)(2,1)S(1)} %maximum_select_fusion.12), channel_id=1, source_target_pairs={{0,2},{2,0},{1,3},{3,1},{4,6},{6,4},{5,7},{7,5},{8,10},{10,8},{9,1... | collective-permute-start | bytes 786440 | tf_op jit(solution)/shard_map/ppermute | solution.py:70
  112.9 14.1 %collective-permute-start.19 = (bf16[192,1024]{1,0:T(8,128)(2,1)S(1)}, bf16[192,1024]{1,0:T(8,128)(2,1)S(1)}, u32[]{:S(2)}, u32[]{:S(2)}) collective-permute-start(bf16[192,1024]{1,0:T(8,128)(2,1)S(1)} %add_convert_fusion.9), channel_id=1, source_target_pairs={{0,1},{1,0},{2,3},{3,2},{4,5},{5,4},{6,7},{7,6},{8,9},{9,8},{10,11... | collective-permute-start | bytes 1179656 | tf_op jit(solution)/shard_map/ppermute | solution.py:66
  132.3 19.4 %collective-permute-start.23 = (bf16[192,1024]{1,0:T(8,128)(2,1)}, bf16[192,1024]{1,0:T(8,128)(2,1)S(1)}, u32[]{:S(2)}, u32[]{:S(2)}) collective-permute-start(bf16[192,1024]{1,0:T(8,128)(2,1)} %get-tuple-element.337.a_ref), channel_id=1, source_target_pairs={{0,1},{1,0},{2,3},{3,2},{4,5},{5,4},{6,7},{7,6},{8,9},{9,8},{10,11... | collective-permute-start | bytes 1179656 | tf_op jit(solution)/shard_map/ppermute | solution.py:66
  152.6 152.1 %reduce-scatter.4.cloned.1.call-start = ((), (), s32[]{:S(2)}) async-start(), calls=%async_computation.6 | async-start | bytes 2621440 | tf_op jit(solution)/shard_map/reduce_scatter | solution.py:1379
  184.1 12.0 %collective-permute-start.31 = (bf16[192,1024]{1,0:T(8,128)(2,1)S(1)}, bf16[192,1024]{1,0:T(8,128)(2,1)S(1)}, u32[]{:S(2)}, u32[]{:S(2)}) collective-permute-start(bf16[192,1024]{1,0:T(8,128)(2,1)S(1)} %add_convert_fusion.6), channel_id=1, source_target_pairs={{0,1},{1,0},{2,3},{3,2},{4,5},{5,4},{6,7},{7,6},{8,9},{9,8},{10,11... | collective-permute-start | bytes 1179656 | tf_op jit(solution)/shard_map/ppermute | solution.py:66
  185.2 18.4 %collective-permute-start.33 = (bf16[192,1024]{1,0:T(8,128)(2,1)}, bf16[192,1024]{1,0:T(8,128)(2,1)S(1)}, u32[]{:S(2)}, u32[]{:S(2)}) collective-permute-start(bf16[192,1024]{1,0:T(8,128)(2,1)} %get-tuple-element.361.a_ref), channel_id=1, source_target_pairs={{0,1},{1,0},{2,3},{3,2},{4,5},{5,4},{6,7},{7,6},{8,9},{9,8},{10,11... | collective-permute-start | bytes 1179656 | tf_op jit(solution)/shard_map/ppermute | solution.py:66
  267.4 110.0 %reduce-scatter.6.cloned.1.call-start = ((), (), s32[]{:S(2)}) async-start(), calls=%async_computation.7 | async-start | bytes 5242880 | tf_op jit(solution)/shard_map/reduce_scatter | solution.py:1379
  311.1 13.5 %collective-permute-start.57 = (bf16[192,1024]{1,0:T(8,128)(2,1)S(1)}, bf16[192,1024]{1,0:T(8,128)(2,1)S(1)}, u32[]{:S(2)}, u32[]{:S(2)}) collective-permute-start(bf16[192,1024]{1,0:T(8,128)(2,1)S(1)} %add_convert_fusion.2), channel_id=1, source_target_pairs={{0,1},{1,0},{2,3},{3,2},{4,5},{5,4},{6,7},{7,6},{8,9},{9,8},{10,11... | collective-permute-start | bytes 1179656 | tf_op jit(solution)/shard_map/ppermute | solution.py:66
  312.0 12.6 %collective-permute-start.58 = (bf16[192,1024]{1,0:T(8,128)(2,1)}, bf16[192,1024]{1,0:T(8,128)(2,1)S(1)}, u32[]{:S(2)}, u32[]{:S(2)}) collective-permute-start(bf16[192,1024]{1,0:T(8,128)(2,1)} %get-tuple-element.433.pa_ref), channel_id=1, source_target_pairs={{0,4},{4,0},{1,5},{5,1},{2,6},{6,2},{3,7},{7,3},{8,12},{12,8},{9,1... | collective-permute-start | bytes 1179656 | tf_op jit(solution)/shard_map/ppermute | solution.py:62
  325.5 137.3 %reduce-scatter.8.cloned.1.call-start = ((), (), s32[]{:S(2)}) async-start(), calls=%async_computation.8 | async-start | bytes 2621440 | tf_op jit(solution)/shard_map/reduce_scatter | solution.py:1379
  338.7 24.6 %collective-permute-start.63 = (bf16[256,512]{1,0:T(8,128)(2,1)S(1)}, bf16[256,512]{1,0:T(8,128)(2,1)S(1)}, u32[]{:S(2)}, u32[]{:S(2)}) collective-permute-start(bf16[256,512]{1,0:T(8,128)(2,1)S(1)} %select_bitcast_fusion.2), channel_id=1, source_target_pairs={{0,2},{2,0},{1,3},{3,1},{4,6},{6,4},{5,7},{7,5},{8,10},{10,8},{9,1... | collective-permute-start | bytes 786440 | tf_op jit(solution)/shard_map/ppermute | solution.py:70
  340.7 22.6 %collective-permute-start.61 = (bf16[192,1024]{1,0:T(8,128)(2,1)}, bf16[192,1024]{1,0:T(8,128)(2,1)S(1)}, u32[]{:S(2)}, u32[]{:S(2)}) collective-permute-start(bf16[192,1024]{1,0:T(8,128)(2,1)} %get-tuple-element.459.pa_ref), channel_id=1, source_target_pairs={{0,1},{1,0},{2,3},{3,2},{4,5},{5,4},{6,7},{7,6},{8,9},{9,8},{10,11... | collective-permute-start | bytes 1179656 | tf_op jit(solution)/shard_map/ppermute | solution.py:66
  341.9 21.5 %collective-permute-start.62 = (bf16[192,1024]{1,0:T(8,128)(2,1)}, bf16[192,1024]{1,0:T(8,128)(2,1)}, u32[]{:S(2)}, u32[]{:S(2)}) collective-permute-start(bf16[192,1024]{1,0:T(8,128)(2,1)} %get-tuple-element.459.pa_ref), channel_id=1, source_target_pairs={{0,4},{4,0},{1,5},{5,1},{2,6},{6,2},{3,7},{7,3},{8,12},{12,8},{9,1... | collective-permute-start | bytes 1179656 | tf_op jit(solution)/shard_map/ppermute | solution.py:62
  367.1 14.7 %collective-permute-start.65 = (bf16[192,1024]{1,0:T(8,128)(2,1)}, bf16[192,1024]{1,0:T(8,128)(2,1)S(1)}, u32[]{:S(2)}, u32[]{:S(2)}) collective-permute-start(bf16[192,1024]{1,0:T(8,128)(2,1)} %copy-done.65), channel_id=1, source_target_pairs={{0,4},{4,0},{1,5},{5,1},{2,6},{6,2},{3,7},{7,3},{8,12},{12,8},{9,1... | collective-permute-start | bytes 1179656 | tf_op jit(solution)/shard_map/ppermute | solution.py:62
  368.7 35.8 %collective-permute-start.66 = (bf16[192,1024]{1,0:T(8,128)(2,1)S(1)}, bf16[192,1024]{1,0:T(8,128)(2,1)}, u32[]{:S(2)}, u32[]{:S(2)}) collective-permute-start(bf16[192,1024]{1,0:T(8,128)(2,1)S(1)} %add_convert_fusion.1), channel_id=1, source_target_pairs={{0,1},{1,0},{2,3},{3,2},{4,5},{5,4},{6,7},{7,6},{8,9},{9,8},{10,11... | collective-permute-start | bytes 1179656 | tf_op jit(solution)/shard_map/ppermute | solution.py:66
  379.4 26.1 %collective-permute-start.67 = (bf16[256,1024]{1,0:T(8,128)(2,1)}, bf16[256,1024]{1,0:T(8,128)(2,1)}, u32[]{:S(2)}, u32[]{:S(2)}) collective-permute-start(bf16[256,1024]{1,0:T(8,128)(2,1)} %broadcast_select_fusion), channel_id=1, source_target_pairs={{0,2},{2,0},{1,3},{3,1},{4,6},{6,4},{5,7},{7,5},{8,10},{10,8},{9,1... | collective-permute-start | bytes 1572872 | tf_op jit(solution)/shard_map/ppermute | solution.py:70
  447.2 26.6 %collective-permute-start.77 = (f32[48,128]{1,0:T(8,128)S(1)}, f32[48,128]{1,0:T(8,128)S(1)}, u32[]{:S(2)}, u32[]{:S(2)}) collective-permute-start(f32[48,128]{1,0:T(8,128)S(1)} %reduce_sum.28), channel_id=1, source_target_pairs={{0,1},{1,0},{2,3},{3,2},{4,5},{5,4},{6,7},{7,6},{8,9},{9,8},{10,11... | collective-permute-start | bytes 73736 | tf_op jit(solution)/shard_map/ppermute | solution.py:66
  473.2 19.3 %collective-permute-start.82 = (f32[128,512]{1,0:T(8,128)S(1)}, f32[128,512]{1,0:T(8,128)S(1)}, u32[]{:S(2)}, u32[]{:S(2)}) collective-permute-start(f32[128,512]{1,0:T(8,128)S(1)} %get-tuple-element.531), channel_id=1, source_target_pairs={{0,4},{4,0},{1,5},{5,1},{2,6},{6,2},{3,7},{7,3},{8,12},{12,8},{9,1... | collective-permute-start | bytes 786440 | tf_op jit(solution)/shard_map/ppermute | solution.py:62
  476.3 17.1 %collective-permute-start.87 = (f32[1,128]{1,0:T(1,128)S(1)}, f32[1,128]{1,0:T(1,128)S(1)}, u32[]{:S(2)}, u32[]{:S(2)}) collective-permute-start(f32[1,128]{1,0:T(1,128)S(1)} %fusion.26), channel_id=1, source_target_pairs={{0,2},{2,0},{1,3},{3,1},{4,6},{6,4},{5,7},{7,5},{8,10},{10,8},{9,1... | collective-permute-start | bytes 1544 | tf_op jit(solution)/shard_map/ppermute | solution.py:70
  476.8 16.6 %collective-permute-start.85 = (f32[1,128]{1,0:T(1,128)S(1)}, f32[1,128]{1,0:T(1,128)S(1)}, u32[]{:S(2)}, u32[]{:S(2)}) collective-permute-start(f32[1,128]{1,0:T(1,128)S(1)} %copy-done.61), channel_id=1, source_target_pairs={{0,1},{1,0},{2,3},{3,2},{4,5},{5,4},{6,7},{7,6},{8,9},{9,8},{10,11... | collective-permute-start | bytes 1544 | tf_op jit(solution)/shard_map/ppermute | solution.py:66
  478.8 13.4 %collective-permute-start.79 = (bf16[256,512]{1,0:T(8,128)(2,1)S(1)}, bf16[256,512]{1,0:T(8,128)(2,1)S(1)}, u32[]{:S(2)}, u32[]{:S(2)}) collective-permute-start(bf16[256,512]{1,0:T(8,128)(2,1)S(1)} %select_bitcast_fusion.1), channel_id=1, source_target_pairs={{0,2},{2,0},{1,3},{3,1},{4,6},{6,4},{5,7},{7,5},{8,10},{10,8},{9,1... | collective-permute-start | bytes 786440 | tf_op jit(solution)/shard_map/ppermute | solution.py:70
  (174 other events, 1193.7 us)
Sparse Core Ops, SparseCore 0:
  81.7 53.5 all-gather.3
  152.7 34.5 all-gather.5
  267.5 34.6 reduce-scatter.3
  324.8 52.5 reduce-scatter.5
  425.4 37.2 reduce-scatter.7

commit v4 on v3

--- a/solution.py
+++ b/solution.py
@@ -363,7 +363,7 @@
 
 def onward(parts, stream, hot, mods, picks):
     n, width = parts[2].shape
-    tile = n // 2
+    tile = n
     return call(
         functools.partial(onward_kernel, picks=picks),
         (n // tile,),
@@ -416,7 +416,7 @@
 
 def back(parts, stream, hot, mods, picks, carried, branch, feats):
     n, width = parts[2].shape
-    tile = n // 2
+    tile = n
     gated, has = branch is not None, carried is not None
     extra = ([carried] if has else []) + ([branch] if gated else [feats])
     specs = [tiled(tile, width)] * 4 + [tiled(tile, 16), whole(mods.shape)]
@@ -983,11 +983,10 @@
         for head in range(2):
             chosen = first_t if head == 0 else ~first_t
             scores = dot_nt(jnp.where(chosen, query_t, jnp.zeros_like(query_t)), k_s[...]) + bias_s[rows, :]
-            peak = jnp.max(scores, -1, keepdims=True)
-            exponent = jnp.exp(scores - peak)
+            exponent = jnp.exp(scores)
             total = jnp.sum(exponent, -1, keepdims=True)
             mixed.append(dot_nn(low(exponent * (1.0 / total)), v_s[...]))
-            logs.append(peak + jnp.log(total))
+            logs.append(jnp.log(total))
         mixed = low(jnp.where(first_t, mixed[0], mixed[1]))
         mix_ref[rows, :] = mixed
         turned = jnp.where(first_t, logs[0], logs[1]).T
@@ -1277,20 +1276,21 @@
         across[0] = over_l(sent)
         return sent
 
-    head_gain = tie(head_scale, gathered)
+    head_gain = tie(head_scale, mod_first)
     gain_own = jnp.where(at_c == 0, head_gain[:2], head_gain[2:])
-    gains = jnp.exp(ordered(at_h, gain_own, over_h(gain_own), 0)) / 8.0
-    gain_row = jnp.repeat(gains, 64)[None, :]
 
     info = full(jnp.stack([codes, place, live, weight], 1))
     info_other, vq_other = over_c(info), over_c(vq_in)
     at = jnp.stack([full(at_c == at_h).astype(jnp.int32), at_c, at_l])
-    arranged, olds, qkv_pieces, feed_far = window(
+    arranged, olds, qkv_pieces, feed_far, gain_far = window(
         arrange(at, tie(info, mod_first), info_other, vq_in, vq_other, lead_pad),
         old_stats(*tie((qkv_w, proj_w, fc1_w, fc2_w, head_w, ada_w, tables, head_scale[None]), mod_first)),
         [qkv_piece] + [over_g(qkv_piece, k) for k in range(1, 4)] if g_count == 4 else [],
         over_h(feed_near),
-    )
+        over_h(gain_own),
+    )
+    gains = jnp.exp(ordered(at_h, gain_own, gain_far, 0)) / 8.0
+    gain_row = jnp.repeat(gains, 64)[None, :]
     feats, hot, cols, rows = (arranged[k::4] for k in range(4))
     head_near = near_rows(tie(head_w, olds))
     feats_first = tie(feats[0], gain_row)

time: 573 us -> 572 us (level)
  Pallas kernels: 246 us -> 253 us
    pallas_call x2, Pallas kernels: 12.5 us -> 23.3 us  [head_back(): call(head_back_kernel, (2,), [tiled(tile, units), whole(w.shape), tiled(t...]
    unnamed x224 -> x222, local copies, waits for them, and re-layouts: 18.2 us -> 16.7 us
  transfers between devices with their start and end apart: 99 -> 99, of which waited for: 39 -> 36; matrix products, arithmetic and copies ran while one was open for 12% -> 11% of each run, Pallas kernels for 40% -> 41%
where the time goes in v4:
time: 572 us; the launch traced here: 567 us
  Pallas kernels  253 us (44%)
  waiting for transfers between devices  121 us (21%)
  starting transfers between devices  76.5 us (13%)
  local copies, waits for them, and re-layouts  40.6 us (7%)
  other arithmetic  37.1 us (6%)
  between operations  20 us (3%)
  matrix products  10 us (2%)
  blocking collectives  9.24 us (2%)
    ppermute x25, waiting for transfers between devices, over_l(): return lax.ppermute(a, 'l', swap_pairs)  46.9 us
    pallas_call x2, Pallas kernels, attend_back(): call(attend_back_kernel, (pairs,), [part(length, 0), part(length, 1), par...  41.4 us
    ppermute x25, starting transfers between devices, over_l(): return lax.ppermute(a, 'l', swap_pairs)  30.7 us
    pallas_call x6, Pallas kernels, back(): call(functools.partial(back_kernel, gated=gated, carried=has, picks=picks...  24 us
    pallas_call x2, Pallas kernels, head_back(): call(head_back_kernel, (2,), [tiled(tile, units), whole(w.shape), tiled(t...  23.3 us
    reduce_scatter x3, waiting for transfers between devices, reduced(): lax.psum_scatter(a.reshape(-1, shape[2]), 'g', scatter_dimension=0, tiled...  23.2 us
    pallas_call x2, Pallas kernels, attend(): call(attend_kernel, (pairs,), [block, pl.BlockSpec((length, 128), lambda...  21.9 us
    ppermute x11, waiting for transfers between devices, over_g(): return lax.ppermute(a, 'g', [(i, i ^ k) for i in range(lax.axis_size('g'))])  21.1 us
  transfers between devices with their start and end apart: 99, of which 36 were waited for; matrix products, arithmetic and copies ran while one was open for 11% of the time, Pallas kernels for 41%

profile of v4, /device:TPU:0, one launch (start us, length us, event | category | flops | bytes accessed | tf_op | source)
XLA Modules:
  0.0 567.4 jit_solution(2805853115421075424)
XLA Ops:
  22.4 9.2 %all-gather = bf16[384,128]{1,0:T(8,128)(2,1)S(1)} all-gather(bf16[48,128]{1,0:T(8,128)(2,1)S(1)} %pad_maximum_fusion.2), channel_id=2, replica_groups=mesh['g'=4,'c'=2,'h'=2,'l'=2] {'g','c'}, dimensions={0}, use_global_device_ids=true | all-gather | bytes 110592 | tf_op jit(solution)/shard_map/all_gather | solution.py:1209
  54.3 4.5 arrange.1
  60.5 9.1 %collective-permute-done.6.c_ref = bf16[2,4,256,128]{3,2,1,0:T(8,128)(2,1)} collective-permute-done((bf16[2,4,256,128]{3,2,1,0:T(8,128)(2,1)}, bf16[2,4,256,128]{3,2,1,0:T(8,128)(2,1)}, u32[]{:S(2)}, u32[]{:S(2)}) %collective-permute-start.6) | collective-permute-done | bytes 524320 | tf_op jit(solution)/shard_map/ppermute | solution.py:78
  71.4 5.9 %collective-permute-done.11 = f32[2]{0:T(128)S(1)} collective-permute-done((f32[2]{0:T(128)S(1)}, f32[2]{0:T(128)S(1)}, u32[]{:S(2)}, u32[]{:S(2)}) %collective-permute-start.11) | collective-permute-done | bytes 40 | tf_op jit(solution)/shard_map/ppermute | solution.py:70
  82.5 7.7 %enter_first.1 = (bf16[768,1024]{1,0:T(8,128)(2,1)}, f32[768,768]{1,0:T(8,128)}, f32[192,1024]{1,0:T(8,128)}, bf16[1024,768]{1,0:T(8,128)(2,1)}, bf16[1024,256]{1,0:T(8,128)(2,1)}) custom-call(s32[1]{0:T(128)} %bitcast.1.at_ref, bf16[768,48]{1,0:T(8,128)(2,1)} %get-tuple-element.304.feat_ref.refs_7_, bf16[48,1024]{1,0:T(8,128)(2,1)} %bitcast.204, ...), custom_call_target="tpu_custom_call" | custom-call | flops 6000000000 | bytes 6000000 | tf_op jit(solution)/shard_map/enter_first/pallas_call | solution.py:335
  90.2 10.8 %attend.2 = (bf16[768,256]{1,0:T(8,128)(2,1)}, f32[2,2,768]{2,1,0:T(2,128)}, bf16[384,1024]{1,0:T(8,128)(2,1)}, bf16[384,1024]{1,0:T(8,128)(2,1)}) custom-call(f32[768,768]{1,0:T(8,128)} %get-tuple-element.310.q_ref.k_ref.v_ref, f32[768,768]{1,0:T(8,128)} %get-tuple-element.310.q_ref.k_ref.v_ref, f32[768,768]{1,0:T(8,128)} %get-tuple-element.310.q_ref.k_ref.v_ref, ...), custom_call_target="tpu_custom_call" | custom-call | flops 11000000512 | bytes 11000000 | tf_op jit(solution)/shard_map/attend/pallas_call | solution.py:1008
  101.2 7.1 %enter.1 = (bf16[768,1024]{1,0:T(8,128)(2,1)}, f32[768,768]{1,0:T(8,128)}, f32[192,1024]{1,0:T(8,128)}) custom-call(bf16[768,48]{1,0:T(8,128)(2,1)} %get-tuple-element.322.feat_ref.refs_7_, bf16[48,1024]{1,0:T(8,128)(2,1)} %bitcast.205, bf16[768,16]{1,0:T(8,128)(2,1)} %get-tuple-element.323.hot_ref.refs_4_, ...), custom_call_target="tpu_custom_call" | custom-call | flops 5000000000 | bytes 5000000 | tf_op jit(solution)/shard_map/enter/pallas_call | solution.py:300
  112.0 11.0 %attend.3 = (bf16[768,256]{1,0:T(8,128)(2,1)}, f32[2,2,768]{2,1,0:T(2,128)}, bf16[384,1024]{1,0:T(8,128)(2,1)}, bf16[384,1024]{1,0:T(8,128)(2,1)}) custom-call(f32[768,768]{1,0:T(8,128)} %get-tuple-element.330.q_ref.k_ref.v_ref, f32[768,768]{1,0:T(8,128)} %get-tuple-element.330.q_ref.k_ref.v_ref, f32[768,768]{1,0:T(8,128)} %get-tuple-element.330.q_ref.k_ref.v_ref, ...), custom_call_target="tpu_custom_call" | custom-call | flops 11000000512 | bytes 11000000 | tf_op jit(solution)/shard_map/attend/pallas_call | solution.py:1008
  130.2 10.0 %collective-permute-done.21.c_ref = bf16[192,1024]{1,0:T(8,128)(2,1)S(1)} collective-permute-done((bf16[192,1024]{1,0:T(8,128)(2,1)S(1)}, bf16[192,1024]{1,0:T(8,128)(2,1)S(1)}, u32[]{:S(2)}, u32[]{:S(2)}) %collective-permute-start.21) | collective-permute-done | bytes 393248 | tf_op jit(solution)/shard_map/ppermute | solution.py:66
  150.1 9.9 %feed.2 = (bf16[768,1024]{1,0:T(8,128)(2,1)}, bf16[768,1024]{1,0:T(8,128)(2,1)}, f32[768,1024]{1,0:T(8,128)}, bf16[384,1024]{1,0:T(8,128)(2,1)}, bf16[384,1024]{1,0:T(8,128)(2,1)}) custom-call(bf16[192,1024]{1,0:T(8,128)(2,1)} %get-tuple-element.339.a_ref, bf16[192,1024]{1,0:T(8,128)(2,1)} %copy-done.70, bf16[192,1024]{1,0:T(8,128)(2,1)} %copy-done.69, ...), custom_call_target="tpu_custom_call" | custom-call | flops 5000000000 | bytes 5000000 | tf_op jit(solution)/shard_map/feed/pallas_call | solution.py:493
  166.5 9.4 %feed.3 = (bf16[768,1024]{1,0:T(8,128)(2,1)}, bf16[768,1024]{1,0:T(8,128)(2,1)}, f32[768,1024]{1,0:T(8,128)}, bf16[384,1024]{1,0:T(8,128)(2,1)}, bf16[384,1024]{1,0:T(8,128)(2,1)}) custom-call(bf16[192,1024]{1,0:T(8,128)(2,1)} %get-tuple-element.354.a_ref, bf16[192,1024]{1,0:T(8,128)(2,1)} %copy-done.72, bf16[192,1024]{1,0:T(8,128)(2,1)} %copy-done.73, ...), custom_call_target="tpu_custom_call" | custom-call | flops 5000000000 | bytes 5000000 | tf_op jit(solution)/shard_map/feed/pallas_call | solution.py:493
  184.0 8.0 %collective-permute-done.31.c_ref = bf16[192,1024]{1,0:T(8,128)(2,1)S(1)} collective-permute-done((bf16[192,1024]{1,0:T(8,128)(2,1)S(1)}, bf16[192,1024]{1,0:T(8,128)(2,1)S(1)}, u32[]{:S(2)}, u32[]{:S(2)}) %collective-permute-start.31) | collective-permute-done | bytes 393248 | tf_op jit(solution)/shard_map/ppermute | solution.py:66
  202.7 6.0 %head.2 = (bf16[768,1024]{1,0:T(8,128)(2,1)}, f32[768,1024]{1,0:T(8,128)}, f32[8,768]{1,0:T(8,128)}) custom-call(bf16[192,1024]{1,0:T(8,128)(2,1)} %get-tuple-element.363.a_ref, bf16[192,1024]{1,0:T(8,128)(2,1)} %copy-done.79, bf16[192,1024]{1,0:T(8,128)(2,1)} %copy-done.76, bf16[192,1024]{1,0:T(8,128)(2,1)} %copy-done.90, ...), custom_call_target="tpu_custom_call" | custom-call | flops 6000000000 | bytes 6000000 | tf_op jit(solution)/shard_map/head/pallas_call | solution.py:549
  216.6 5.9 %head.3 = (bf16[768,1024]{1,0:T(8,128)(2,1)}, f32[768,1024]{1,0:T(8,128)}, f32[8,768]{1,0:T(8,128)}) custom-call(bf16[192,1024]{1,0:T(8,128)(2,1)} %get-tuple-element.377.a_ref, bf16[192,1024]{1,0:T(8,128)(2,1)} %copy-done.77, bf16[192,1024]{1,0:T(8,128)(2,1)} %copy-done.80, bf16[192,1024]{1,0:T(8,128)(2,1)} %copy-done.87, ...), custom_call_target="tpu_custom_call" | custom-call | flops 6000000000 | bytes 6000000 | tf_op jit(solution)/shard_map/head/pallas_call | solution.py:549
  226.7 6.3 %head_back.2 = (bf16[768,1024]{1,0:T(8,128)(2,1)}, bf16[384,1024]{1,0:T(8,128)(2,1)}, bf16[384,1024]{1,0:T(8,128)(2,1)}) custom-call(f32[768,1024]{1,0:T(8,128)} %get-tuple-element.373.logit_ref, bf16[4,2,256,512]{3,2,1,0:T(8,128)(2,1)} %bitcast.223, f32[768,128]{1,0:T(8,128)} %get-tuple-element.311.col_ref.code_ref, f32[1,1024]{1,0:T(1,128)} %fusion.15.column_ref, ...), custom_call_target="tpu_custom_call" | custom-call | flops 5000000000 | bytes 5000000 | tf_op jit(solution)/shard_map/head_back/pallas_call | solution.py:610
  237.2 17.1 %head_back.3 = (bf16[768,1024]{1,0:T(8,128)(2,1)}, bf16[384,1024]{1,0:T(8,128)(2,1)}, bf16[384,1024]{1,0:T(8,128)(2,1)}) custom-call(f32[768,1024]{1,0:T(8,128)} %get-tuple-element.391.logit_ref, bf16[4,2,256,512]{3,2,1,0:T(8,128)(2,1)} %bitcast.224, f32[768,128]{1,0:T(8,128)} %get-tuple-element.331.col_ref.code_ref, f32[1,1024]{1,0:T(1,128)} %fusion.15.column_ref, ...), custom_call_target="tpu_custom_call" | custom-call | flops 5000000000 | bytes 5000000 | tf_op jit(solution)/shard_map/head_back/pallas_call | solution.py:610
  260.2 7.0 %head_grad.1 = bf16[4,2,256,512]{3,2,1,0:T(8,128)(2,1)} custom-call(bf16[768,1024]{1,0:T(8,128)(2,1)} %get-tuple-element.406.a_ref, bf16[768,1024]{1,0:T(8,128)(2,1)} %get-tuple-element.407.b_ref, bf16[768,1024]{1,0:T(8,128)(2,1)} %get-tuple-element.408.c_ref, bf16[768,1024]{1,0:T(8,128)(2,1)} %get-tuple-element.409.d_ref), custom_call_target="tpu_custom_call" | custom-call | flops 6000000000 | bytes 6000000 | tf_op jit(solution)/shard_map/head_grad/pallas_call | solution.py:660
  275.5 5.4 collective-permute-done.49.b_ref
  283.3 9.1 %feed_back.2 = (bf16[768,1024]{1,0:T(8,128)(2,1)}, bf16[768,1024]{1,0:T(8,128)(2,1)}, bf16[384,1024]{1,0:T(8,128)(2,1)}, bf16[384,1024]{1,0:T(8,128)(2,1)}) custom-call(bf16[192,1024]{1,0:T(8,128)(2,1)} %get-tuple-element.403.a_ref, bf16[192,1024]{1,0:T(8,128)(2,1)} %copy-done.83, bf16[192,1024]{1,0:T(8,128)(2,1)} %copy-done.68, ...), custom_call_target="tpu_custom_call" | custom-call | flops 7000000000 | bytes 7000000 | tf_op jit(solution)/shard_map/feed_back/pallas_call | solution.py:522
  298.7 8.7 %feed_back.3 = (bf16[768,1024]{1,0:T(8,128)(2,1)}, bf16[768,1024]{1,0:T(8,128)(2,1)}, bf16[384,1024]{1,0:T(8,128)(2,1)}, bf16[384,1024]{1,0:T(8,128)(2,1)}) custom-call(bf16[192,1024]{1,0:T(8,128)(2,1)} %get-tuple-element.423.a_ref, bf16[192,1024]{1,0:T(8,128)(2,1)} %copy-done.74, bf16[192,1024]{1,0:T(8,128)(2,1)} %copy-done.78, ...), custom_call_target="tpu_custom_call" | custom-call | flops 7000000000 | bytes 7000000 | tf_op jit(solution)/shard_map/feed_back/pallas_call | solution.py:522
  308.9 4.3 back.8
  315.3 12.6 %feed_grad.1 = bf16[4,2,256,1024]{3,2,1,0:T(8,128)(2,1)} custom-call(bf16[768,1024]{1,0:T(8,128)(2,1)} %get-tuple-element.438.a_ref, bf16[768,1024]{1,0:T(8,128)(2,1)} %get-tuple-element.439.b_ref, bf16[768,1024]{1,0:T(8,128)(2,1)} %get-tuple-element.440.c_ref, bf16[768,1024]{1,0:T(8,128)(2,1)} %get-tuple-element.441.d_ref, ...), custom_call_target="tpu_custom_call" | custom-call | flops 12000000000 | bytes 12000000 | tf_op jit(solution)/shard_map/feed_grad/pallas_call | solution.py:686
  334.5 6.2 %collective-permute-done.59.pb_ref = bf16[192,1024]{1,0:T(8,128)(2,1)S(1)} collective-permute-done((bf16[192,1024]{1,0:T(8,128)(2,1)S(1)}, bf16[192,1024]{1,0:T(8,128)(2,1)S(1)}, u32[]{:S(2)}, u32[]{:S(2)}) %collective-permute-start.59) | collective-permute-done | bytes 393248 | tf_op jit(solution)/shard_map/ppermute | solution.py:66
  345.5 20.8 %attend_back.2 = (bf16[768,1024]{1,0:T(8,128)(2,1)}, bf16[768,768]{1,0:T(8,128)(2,1)}, f32[2,1,128]{2,1,0:T(1,128)}, bf16[384,1024]{1,0:T(8,128)(2,1)}, bf16[384,1024]{1,0:T(8,128)(2,1)}) custom-call(f32[768,768]{1,0:T(8,128)} %get-tuple-element.310.q_ref.k_ref.v_ref, f32[768,768]{1,0:T(8,128)} %get-tuple-element.310.q_ref.k_ref.v_ref, ...), custom_call_target="tpu_custom_call" | custom-call | flops 16000000000 | bytes 16000000 | tf_op jit(solution)/shard_map/attend_back/pallas_call | solution.py:1131
  372.8 7.9 %reduce-scatter.6.cloned.1.call-done = bf16[512,1024]{1,0:T(8,128)(2,1)} async-done(((bf16[2048,1024]{1,0:T(8,128)(2,1)}), bf16[512,1024]{1,0:T(8,128)(2,1)}) %reduce-scatter.6.cloned.1.call-update) | async-done | bytes 1048592 | tf_op jit(solution)/shard_map/reduce_scatter | solution.py:1379
  385.9 20.6 %attend_back.3 = (bf16[768,1024]{1,0:T(8,128)(2,1)}, bf16[768,768]{1,0:T(8,128)(2,1)}, f32[2,1,128]{2,1,0:T(1,128)}, bf16[384,1024]{1,0:T(8,128)(2,1)}, bf16[384,1024]{1,0:T(8,128)(2,1)}) custom-call(f32[768,768]{1,0:T(8,128)} %get-tuple-element.330.q_ref.k_ref.v_ref, f32[768,768]{1,0:T(8,128)} %get-tuple-element.330.q_ref.k_ref.v_ref, ...), custom_call_target="tpu_custom_call" | custom-call | flops 16000000000 | bytes 16000000 | tf_op jit(solution)/shard_map/attend_back/pallas_call | solution.py:1131
  417.5 10.3 %first_grad.1 = bf16[4,2,256,512]{3,2,1,0:T(8,128)(2,1)} custom-call(bf16[768,1024]{1,0:T(8,128)(2,1)} %get-tuple-element.473.a_ref, bf16[768,1024]{1,0:T(8,128)(2,1)} %get-tuple-element.474.b_ref, bf16[768,768]{1,0:T(8,128)(2,1)} %get-tuple-element.477.c_ref, bf16[768,768]{1,0:T(8,128)(2,1)} %get-tuple-element.478.d_ref, ...), custom_call_target="tpu_custom_call" | custom-call | flops 6000000000 | bytes 6000000 | tf_op jit(solution)/shard_map/first_grad/pallas_call | solution.py:712
  444.9 4.8 all-to-all-done
  450.3 15.4 %reduce-scatter.8.cloned.1.call-done = bf16[512,512]{1,0:T(8,128)(2,1)} async-done(((bf16[2048,512]{1,0:T(8,128)(2,1)}), bf16[512,512]{1,0:T(8,128)(2,1)}) %reduce-scatter.8.cloned.1.call-update) | async-done | bytes 524304 | tf_op jit(solution)/shard_map/reduce_scatter | solution.py:1379
  490.5 4.7 collective-permute-done.79
  513.3 5.9 %column_stats.1 = (f32[2,12416]{1,0:T(2,128)}, f32[8,128]{1,0:T(8,128)}) custom-call(s32[1]{0:T(128)} %bitcast.at_ref, f32[5,128]{1,0:T(8,128)} %fusion.20.row_ref, f32[1,128]{1,0:T(1,128)} %slice.422.old_ref, f32[1,128]{1,0:T(1,128)} %get-tuple-element.528.tail_ref, f32[1,1]{1,0:T(1,128)} %bitcast.74.tables_ref, f32[1,128]{1,0:T(1,128)} %fusion.25.scale_ref, ...), custom_call_target="tpu_custom_call" | custom-call | flops 5000000000 | bytes 5000000 | tf_op jit(solution)/shard_map/column_stats/pallas_call | solution.py:799
  546.1 12.3 %renew.1 = (f32[3,128,256]{2,1,0:T(8,128)}, f32[256,128]{1,0:T(8,128)}, f32[128,1024]{1,0:T(8,128)}, f32[1024,128]{1,0:T(8,128)}, f32[128,1024]{1,0:T(8,128)}, /...) custom-call(f32[1,128]{1,0:T(1,128)} %slice.476.line_ref, ...), custom_call_target="tpu_custom_call" | custom-call | flops 8000000000 | bytes 8000000 | tf_op jit(solution)/shard_map/renew/pallas_call | solution.py:924
  (564 shorter events, 253.8 us)
Async XLA Ops:
  7.2 142.9 %all-gather.4.cloned.1.call-start = ((), (), s32[]{:S(2)}) async-start(), calls=%async_computation.4 | async-start | bytes 5242880 | tf_op jit(solution)/shard_map/all_gather | solution.py:1248
  13.6 37.8 %collective-permute-start.3 = (f32[2,4,768]{2,1,0:T(4,128)S(1)}, f32[2,4,768]{2,1,0:T(4,128)S(1)}, u32[]{:S(2)}, u32[]{:S(2)}) collective-permute-start(f32[2,4,768]{2,1,0:T(4,128)S(1)} %add_convert_fusion.11.mine_ref), channel_id=1, source_target_pairs={{0,4},{4,0},{1,5},{5,1},{2,6},{6,2},{3,7},{7,3},{8,12},{12,8},{9,1... | collective-permute-start | bytes 73736 | tf_op jit(solution)/shard_map/ppermute | solution.py:62
  14.6 36.8 %collective-permute-start.4 = (bf16[2,768,32]{2,1,0:T(8,128)(2,1)}, bf16[2,768,32]{2,1,0:T(8,128)(2,1)}, u32[]{:S(2)}, u32[]{:S(2)}) collective-permute-start(bf16[2,768,32]{2,1,0:T(8,128)(2,1)} %copy.71.vq_ref), channel_id=1, source_target_pairs={{0,4},{4,0},{1,5},{5,1},{2,6},{6,2},{3,7},{7,3},{8,12},{12,8},{9,1... | collective-permute-start | bytes 294920 | tf_op jit(solution)/shard_map/ppermute | solution.py:62
  18.0 16.2 %collective-permute-start.1 = (bf16[4,256,128]{2,1,0:T(8,128)(2,1)S(1)}, bf16[4,256,128]{2,1,0:T(8,128)(2,1)S(1)}, u32[]{:S(2)}, u32[]{:S(2)}) collective-permute-start(bf16[4,256,128]{2,1,0:T(8,128)(2,1)S(1)} %maximum_select_fusion.7), channel_id=1, source_target_pairs={{0,2},{2,0},{1,3},{3,1},{4,6},{6,4},{5,7},{7,5},{8,10},{10,8},{9,1... | collective-permute-start | bytes 786440 | tf_op jit(solution)/shard_map/ppermute | solution.py:70
  42.4 16.5 %collective-permute-start.5 = (bf16[2,4,256,128]{3,2,1,0:T(8,128)(2,1)}, bf16[2,4,256,128]{3,2,1,0:T(8,128)(2,1)}, u32[]{:S(2)}, u32[]{:S(2)}) collective-permute-start(bf16[2,4,256,128]{3,2,1,0:T(8,128)(2,1)} %maximum_select_fusion.2.a_ref), channel_id=1, source_target_pairs={{0,8},{8,0},{16,24},{24,16},{1,9},{9,1},{17,25},{25,17},{2,10},{10... | collective-permute-start | bytes 1572872 | tf_op jit(solution)/shard_map/ppermute | solution.py:78
  44.0 25.6 %collective-permute-start.6 = (bf16[2,4,256,128]{3,2,1,0:T(8,128)(2,1)}, bf16[2,4,256,128]{3,2,1,0:T(8,128)(2,1)}, u32[]{:S(2)}, u32[]{:S(2)}) collective-permute-start(bf16[2,4,256,128]{3,2,1,0:T(8,128)(2,1)} %maximum_select_fusion.2.a_ref), channel_id=1, source_target_pairs={{0,16},{8,24},{16,0},{24,8},{1,17},{9,25},{17,1},{25,9},{2,18},{10... | collective-permute-start | bytes 1572872 | tf_op jit(solution)/shard_map/ppermute | solution.py:78
  46.6 24.6 %collective-permute-start.7 = (bf16[2,4,256,128]{3,2,1,0:T(8,128)(2,1)}, bf16[2,4,256,128]{3,2,1,0:T(8,128)(2,1)}, u32[]{:S(2)}, u32[]{:S(2)}) collective-permute-start(bf16[2,4,256,128]{3,2,1,0:T(8,128)(2,1)} %maximum_select_fusion.2.a_ref), channel_id=1, source_target_pairs={{0,24},{8,16},{16,8},{24,0},{1,25},{9,17},{17,9},{25,1},{2,26},{10... | collective-permute-start | bytes 1572872 | tf_op jit(solution)/shard_map/ppermute | solution.py:78
  51.4 25.9 %collective-permute-start.10 = (bf16[256,1024]{1,0:T(8,128)(2,1)}, bf16[256,1024]{1,0:T(8,128)(2,1)S(1)}, u32[]{:S(2)}, u32[]{:S(2)}) collective-permute-start(bf16[256,1024]{1,0:T(8,128)(2,1)} %get-tuple-element.541), channel_id=1, source_target_pairs={{0,2},{2,0},{1,3},{3,1},{4,6},{6,4},{5,7},{7,5},{8,10},{10,8},{9,1... | collective-permute-start | bytes 1572872 | tf_op jit(solution)/shard_map/ppermute | solution.py:70
  51.4 25.9 %collective-permute-start.11 = (f32[2]{0:T(128)S(1)}, f32[2]{0:T(128)S(1)}, u32[]{:S(2)}, u32[]{:S(2)}) collective-permute-start(f32[2]{0:T(128)S(1)} %broadcast_select_fusion.13), channel_id=1, source_target_pairs={{0,2},{2,0},{1,3},{3,1},{4,6},{6,4},{5,7},{7,5},{8,10},{10,8},{9,1... | collective-permute-start | bytes 32 | tf_op jit(solution)/shard_map/ppermute | solution.py:70
  58.9 19.6 %collective-permute-start.12 = (f32[8,4096]{1,0:T(8,128)S(1)}, f32[8,4096]{1,0:T(8,128)S(1)}, u32[]{:S(2)}, u32[]{:S(2)}) collective-permute-start(f32[8,4096]{1,0:T(8,128)S(1)} %get-tuple-element.542), channel_id=1, source_target_pairs={{0,8},{8,0},{16,24},{24,16},{1,9},{9,1},{17,25},{25,17},{2,10},{10... | collective-permute-start | bytes 393224 | tf_op jit(solution)/shard_map/ppermute | solution.py:78
  81.1 102.9 %all-gather.6.cloned.1.call-start = ((), (), s32[]{:S(2)}) async-start(), calls=%async_computation.5 | async-start | bytes 2621440 | tf_op jit(solution)/shard_map/all_gather | solution.py:1248
  81.4 19.7 %collective-permute-start.17 = (bf16[256,512]{1,0:T(8,128)(2,1)S(1)}, bf16[256,512]{1,0:T(8,128)(2,1)S(1)}, u32[]{:S(2)}, u32[]{:S(2)}) collective-permute-start(bf16[256,512]{1,0:T(8,128)(2,1)S(1)} %maximum_select_fusion.12), channel_id=1, source_target_pairs={{0,2},{2,0},{1,3},{3,1},{4,6},{6,4},{5,7},{7,5},{8,10},{10,8},{9,1... | collective-permute-start | bytes 786440 | tf_op jit(solution)/shard_map/ppermute | solution.py:70
  109.5 13.5 %collective-permute-start.19 = (bf16[192,1024]{1,0:T(8,128)(2,1)S(1)}, bf16[192,1024]{1,0:T(8,128)(2,1)S(1)}, u32[]{:S(2)}, u32[]{:S(2)}) collective-permute-start(bf16[192,1024]{1,0:T(8,128)(2,1)S(1)} %add_convert_fusion.9), channel_id=1, source_target_pairs={{0,1},{1,0},{2,3},{3,2},{4,5},{5,4},{6,7},{7,6},{8,9},{9,8},{10,11... | collective-permute-start | bytes 1179656 | tf_op jit(solution)/shard_map/ppermute | solution.py:66
  128.5 19.2 %collective-permute-start.23 = (bf16[192,1024]{1,0:T(8,128)(2,1)}, bf16[192,1024]{1,0:T(8,128)(2,1)S(1)}, u32[]{:S(2)}, u32[]{:S(2)}) collective-permute-start(bf16[192,1024]{1,0:T(8,128)(2,1)} %get-tuple-element.339.a_ref), channel_id=1, source_target_pairs={{0,1},{1,0},{2,3},{3,2},{4,5},{5,4},{6,7},{7,6},{8,9},{9,8},{10,11... | collective-permute-start | bytes 1179656 | tf_op jit(solution)/shard_map/ppermute | solution.py:66
  148.6 159.5 %reduce-scatter.4.cloned.1.call-start = ((), (), s32[]{:S(2)}) async-start(), calls=%async_computation.6 | async-start | bytes 2621440 | tf_op jit(solution)/shard_map/reduce_scatter | solution.py:1379
  181.4 18.7 %collective-permute-start.33 = (bf16[192,1024]{1,0:T(8,128)(2,1)}, bf16[192,1024]{1,0:T(8,128)(2,1)S(1)}, u32[]{:S(2)}, u32[]{:S(2)}) collective-permute-start(bf16[192,1024]{1,0:T(8,128)(2,1)} %get-tuple-element.363.a_ref), channel_id=1, source_target_pairs={{0,1},{1,0},{2,3},{3,2},{4,5},{5,4},{6,7},{7,6},{8,9},{9,8},{10,11... | collective-permute-start | bytes 1179656 | tf_op jit(solution)/shard_map/ppermute | solution.py:66
  236.1 18.2 %collective-permute-start.45 = (bf16[192,1024]{1,0:T(8,128)(2,1)S(1)}, bf16[192,1024]{1,0:T(8,128)(2,1)S(1)}, u32[]{:S(2)}, u32[]{:S(2)}) collective-permute-start(bf16[192,1024]{1,0:T(8,128)(2,1)S(1)} %add_convert_fusion.5), channel_id=1, source_target_pairs={{0,1},{1,0},{2,3},{3,2},{4,5},{5,4},{6,7},{7,6},{8,9},{9,8},{10,11... | collective-permute-start | bytes 1179656 | tf_op jit(solution)/shard_map/ppermute | solution.py:66
  270.5 110.2 %reduce-scatter.6.cloned.1.call-start = ((), (), s32[]{:S(2)}) async-start(), calls=%async_computation.7 | async-start | bytes 5242880 | tf_op jit(solution)/shard_map/reduce_scatter | solution.py:1379
  314.3 13.6 %collective-permute-start.57 = (bf16[192,1024]{1,0:T(8,128)(2,1)S(1)}, bf16[192,1024]{1,0:T(8,128)(2,1)S(1)}, u32[]{:S(2)}, u32[]{:S(2)}) collective-permute-start(bf16[192,1024]{1,0:T(8,128)(2,1)S(1)} %add_convert_fusion.2), channel_id=1, source_target_pairs={{0,1},{1,0},{2,3},{3,2},{4,5},{5,4},{6,7},{7,6},{8,9},{9,8},{10,11... | collective-permute-start | bytes 1179656 | tf_op jit(solution)/shard_map/ppermute | solution.py:66
  315.3 12.6 %collective-permute-start.58 = (bf16[192,1024]{1,0:T(8,128)(2,1)}, bf16[192,1024]{1,0:T(8,128)(2,1)S(1)}, u32[]{:S(2)}, u32[]{:S(2)}) collective-permute-start(bf16[192,1024]{1,0:T(8,128)(2,1)} %get-tuple-element.435.pa_ref), channel_id=1, source_target_pairs={{0,4},{4,0},{1,5},{5,1},{2,6},{6,2},{3,7},{7,3},{8,12},{12,8},{9,1... | collective-permute-start | bytes 1179656 | tf_op jit(solution)/shard_map/ppermute | solution.py:62
  328.7 136.9 %reduce-scatter.8.cloned.1.call-start = ((), (), s32[]{:S(2)}) async-start(), calls=%async_computation.8 | async-start | bytes 2621440 | tf_op jit(solution)/shard_map/reduce_scatter | solution.py:1379
  342.0 24.3 %collective-permute-start.63 = (bf16[256,512]{1,0:T(8,128)(2,1)S(1)}, bf16[256,512]{1,0:T(8,128)(2,1)S(1)}, u32[]{:S(2)}, u32[]{:S(2)}) collective-permute-start(bf16[256,512]{1,0:T(8,128)(2,1)S(1)} %select_bitcast_fusion.2), channel_id=1, source_target_pairs={{0,2},{2,0},{1,3},{3,1},{4,6},{6,4},{5,7},{7,5},{8,10},{10,8},{9,1... | collective-permute-start | bytes 786440 | tf_op jit(solution)/shard_map/ppermute | solution.py:70
  343.8 22.5 %collective-permute-start.61 = (bf16[192,1024]{1,0:T(8,128)(2,1)}, bf16[192,1024]{1,0:T(8,128)(2,1)S(1)}, u32[]{:S(2)}, u32[]{:S(2)}) collective-permute-start(bf16[192,1024]{1,0:T(8,128)(2,1)} %get-tuple-element.461.pa_ref), channel_id=1, source_target_pairs={{0,1},{1,0},{2,3},{3,2},{4,5},{5,4},{6,7},{7,6},{8,9},{9,8},{10,11... | collective-permute-start | bytes 1179656 | tf_op jit(solution)/shard_map/ppermute | solution.py:66
  344.7 21.6 %collective-permute-start.62 = (bf16[192,1024]{1,0:T(8,128)(2,1)}, bf16[192,1024]{1,0:T(8,128)(2,1)}, u32[]{:S(2)}, u32[]{:S(2)}) collective-permute-start(bf16[192,1024]{1,0:T(8,128)(2,1)} %get-tuple-element.461.pa_ref), channel_id=1, source_target_pairs={{0,4},{4,0},{1,5},{5,1},{2,6},{6,2},{3,7},{7,3},{8,12},{12,8},{9,1... | collective-permute-start | bytes 1179656 | tf_op jit(solution)/shard_map/ppermute | solution.py:62
  370.0 15.2 %collective-permute-start.65 = (bf16[192,1024]{1,0:T(8,128)(2,1)}, bf16[192,1024]{1,0:T(8,128)(2,1)S(1)}, u32[]{:S(2)}, u32[]{:S(2)}) collective-permute-start(bf16[192,1024]{1,0:T(8,128)(2,1)} %copy-done.64), channel_id=1, source_target_pairs={{0,4},{4,0},{1,5},{5,1},{2,6},{6,2},{3,7},{7,3},{8,12},{12,8},{9,1... | collective-permute-start | bytes 1179656 | tf_op jit(solution)/shard_map/ppermute | solution.py:62
  371.7 36.1 %collective-permute-start.66 = (bf16[192,1024]{1,0:T(8,128)(2,1)S(1)}, bf16[192,1024]{1,0:T(8,128)(2,1)}, u32[]{:S(2)}, u32[]{:S(2)}) collective-permute-start(bf16[192,1024]{1,0:T(8,128)(2,1)S(1)} %add_convert_fusion.1), channel_id=1, source_target_pairs={{0,1},{1,0},{2,3},{3,2},{4,5},{5,4},{6,7},{7,6},{8,9},{9,8},{10,11... | collective-permute-start | bytes 1179656 | tf_op jit(solution)/shard_map/ppermute | solution.py:66
  382.7 26.1 %collective-permute-start.67 = (bf16[256,1024]{1,0:T(8,128)(2,1)}, bf16[256,1024]{1,0:T(8,128)(2,1)}, u32[]{:S(2)}, u32[]{:S(2)}) collective-permute-start(bf16[256,1024]{1,0:T(8,128)(2,1)} %broadcast_select_fusion), channel_id=1, source_target_pairs={{0,2},{2,0},{1,3},{3,1},{4,6},{6,4},{5,7},{7,5},{8,10},{10,8},{9,1... | collective-permute-start | bytes 1572872 | tf_op jit(solution)/shard_map/ppermute | solution.py:70
  449.7 27.0 %collective-permute-start.77 = (f32[48,128]{1,0:T(8,128)S(1)}, f32[48,128]{1,0:T(8,128)S(1)}, u32[]{:S(2)}, u32[]{:S(2)}) collective-permute-start(f32[48,128]{1,0:T(8,128)S(1)} %reduce_sum.28), channel_id=1, source_target_pairs={{0,1},{1,0},{2,3},{3,2},{4,5},{5,4},{6,7},{7,6},{8,9},{9,8},{10,11... | collective-permute-start | bytes 73736 | tf_op jit(solution)/shard_map/ppermute | solution.py:66
  476.1 19.3 %collective-permute-start.82 = (f32[128,512]{1,0:T(8,128)S(1)}, f32[128,512]{1,0:T(8,128)S(1)}, u32[]{:S(2)}, u32[]{:S(2)}) collective-permute-start(f32[128,512]{1,0:T(8,128)S(1)} %get-tuple-element.533), channel_id=1, source_target_pairs={{0,4},{4,0},{1,5},{5,1},{2,6},{6,2},{3,7},{7,3},{8,12},{12,8},{9,1... | collective-permute-start | bytes 786440 | tf_op jit(solution)/shard_map/ppermute | solution.py:62
  479.2 17.1 %collective-permute-start.87 = (f32[1,128]{1,0:T(1,128)S(1)}, f32[1,128]{1,0:T(1,128)S(1)}, u32[]{:S(2)}, u32[]{:S(2)}) collective-permute-start(f32[1,128]{1,0:T(1,128)S(1)} %fusion.26), channel_id=1, source_target_pairs={{0,2},{2,0},{1,3},{3,1},{4,6},{6,4},{5,7},{7,5},{8,10},{10,8},{9,1... | collective-permute-start | bytes 1544 | tf_op jit(solution)/shard_map/ppermute | solution.py:70
  479.7 16.6 %collective-permute-start.85 = (f32[1,128]{1,0:T(1,128)S(1)}, f32[1,128]{1,0:T(1,128)S(1)}, u32[]{:S(2)}, u32[]{:S(2)}) collective-permute-start(f32[1,128]{1,0:T(1,128)S(1)} %copy-done.60), channel_id=1, source_target_pairs={{0,1},{1,0},{2,3},{3,2},{4,5},{5,4},{6,7},{7,6},{8,9},{9,8},{10,11... | collective-permute-start | bytes 1544 | tf_op jit(solution)/shard_map/ppermute | solution.py:66
  481.7 13.4 %collective-permute-start.79 = (bf16[256,512]{1,0:T(8,128)(2,1)S(1)}, bf16[256,512]{1,0:T(8,128)(2,1)S(1)}, u32[]{:S(2)}, u32[]{:S(2)}) collective-permute-start(bf16[256,512]{1,0:T(8,128)(2,1)S(1)} %select_bitcast_fusion.1), channel_id=1, source_target_pairs={{0,2},{2,0},{1,3},{3,1},{4,6},{6,4},{5,7},{7,5},{8,10},{10,8},{9,1... | collective-permute-start | bytes 786440 | tf_op jit(solution)/shard_map/ppermute | solution.py:70
  (173 other events, 1197.4 us)
Sparse Core Ops, SparseCore 0:
  81.2 51.5 all-gather.3
  148.7 35.1 all-gather.5
  270.6 34.9 reduce-scatter.3
  328.1 52.5 reduce-scatter.5
  428.3 37.2 reduce-scatter.7

commit v5 on v4

--- a/solution.py
+++ b/solution.py
@@ -22,9 +22,9 @@
 swap_pairs = ((0, 1), (1, 0))
 busy_us = {
     "row_layout": 2, "enter": 5, "enter_first": 6, "attend": 11, "onward": 2, "feed": 5, "head": 6, "merge": 2,
-    "head_back": 5, "back": 5, "feed_back": 7, "attend_back": 16, "old_stats": 4, "row_stats": 3,
+    "head_back": 5, "back": 5, "feed_back": 7, "attend_back": 16, "old_stats": 2, "row_stats": 3,
     "column_stats": 5, "finish": 2, "head_grad": 6, "feed_grad": 12, "first_grad": 6,
-    "renew": 8, "arrange": 4,
+    "renew": 8, "arrange": 2,
 }
 DP = ("g", "c")
 MP = ("h", "l")

time: 572 us -> 572 us (level)
  no operation moved by 1% of the time
where the time goes in v5:
time: 572 us; the launch traced here: 567 us
  Pallas kernels  253 us (44%)
  waiting for transfers between devices  121 us (21%)
  starting transfers between devices  76.6 us (13%)
  local copies, waits for them, and re-layouts  40.6 us (7%)
  other arithmetic  37.1 us (6%)
  between operations  20 us (3%)
  matrix products  10 us (2%)
  blocking collectives  9.24 us (2%)
    ppermute x25, waiting for transfers between devices, over_l(): return lax.ppermute(a, 'l', swap_pairs)  46.9 us
    pallas_call x2, Pallas kernels, attend_back(): call(attend_back_kernel, (pairs,), [part(length, 0), part(length, 1), par...  41.4 us
    ppermute x25, starting transfers between devices, over_l(): return lax.ppermute(a, 'l', swap_pairs)  30.7 us
    pallas_call x6, Pallas kernels, back(): call(functools.partial(back_kernel, gated=gated, carried=has, picks=picks...  24 us
    pallas_call x2, Pallas kernels, head_back(): call(head_back_kernel, (2,), [tiled(tile, units), whole(w.shape), tiled(t...  23.3 us
    reduce_scatter x3, waiting for transfers between devices, reduced(): lax.psum_scatter(a.reshape(-1, shape[2]), 'g', scatter_dimension=0, tiled...  23.2 us
    pallas_call x2, Pallas kernels, attend(): call(attend_kernel, (pairs,), [block, pl.BlockSpec((length, 128), lambda...  21.9 us
    ppermute x11, waiting for transfers between devices, over_g(): return lax.ppermute(a, 'g', [(i, i ^ k) for i in range(lax.axis_size('g'))])  21.1 us
  transfers between devices with their start and end apart: 99, of which 36 were waited for; matrix products, arithmetic and copies ran while one was open for 11% of the time, Pallas kernels for 41%

profile of v5, /device:TPU:0, one launch (start us, length us, event | category | flops | bytes accessed | tf_op | source)
XLA Modules:
  0.0 567.5 jit_solution(5576309020192098229)
XLA Ops:
  22.4 9.2 %all-gather = bf16[384,128]{1,0:T(8,128)(2,1)S(1)} all-gather(bf16[48,128]{1,0:T(8,128)(2,1)S(1)} %pad_maximum_fusion.2), channel_id=2, replica_groups=mesh['g'=4,'c'=2,'h'=2,'l'=2] {'g','c'}, dimensions={0}, use_global_device_ids=true | all-gather | bytes 110592 | tf_op jit(solution)/shard_map/all_gather | solution.py:1209
  54.4 4.5 arrange.1
  60.5 9.1 %collective-permute-done.6.c_ref = bf16[2,4,256,128]{3,2,1,0:T(8,128)(2,1)} collective-permute-done((bf16[2,4,256,128]{3,2,1,0:T(8,128)(2,1)}, bf16[2,4,256,128]{3,2,1,0:T(8,128)(2,1)}, u32[]{:S(2)}, u32[]{:S(2)}) %collective-permute-start.6) | collective-permute-done | bytes 524320 | tf_op jit(solution)/shard_map/ppermute | solution.py:78
  71.4 5.9 %collective-permute-done.11 = f32[2]{0:T(128)S(1)} collective-permute-done((f32[2]{0:T(128)S(1)}, f32[2]{0:T(128)S(1)}, u32[]{:S(2)}, u32[]{:S(2)}) %collective-permute-start.11) | collective-permute-done | bytes 40 | tf_op jit(solution)/shard_map/ppermute | solution.py:70
  82.6 7.7 %enter_first.1 = (bf16[768,1024]{1,0:T(8,128)(2,1)}, f32[768,768]{1,0:T(8,128)}, f32[192,1024]{1,0:T(8,128)}, bf16[1024,768]{1,0:T(8,128)(2,1)}, bf16[1024,256]{1,0:T(8,128)(2,1)}) custom-call(s32[1]{0:T(128)} %bitcast.1.at_ref, bf16[768,48]{1,0:T(8,128)(2,1)} %get-tuple-element.304.feat_ref.refs_7_, bf16[48,1024]{1,0:T(8,128)(2,1)} %bitcast.204, ...), custom_call_target="tpu_custom_call" | custom-call | flops 6000000000 | bytes 6000000 | tf_op jit(solution)/shard_map/enter_first/pallas_call | solution.py:335
  90.2 10.8 %attend.2 = (bf16[768,256]{1,0:T(8,128)(2,1)}, f32[2,2,768]{2,1,0:T(2,128)}, bf16[384,1024]{1,0:T(8,128)(2,1)}, bf16[384,1024]{1,0:T(8,128)(2,1)}) custom-call(f32[768,768]{1,0:T(8,128)} %get-tuple-element.310.q_ref.k_ref.v_ref, f32[768,768]{1,0:T(8,128)} %get-tuple-element.310.q_ref.k_ref.v_ref, f32[768,768]{1,0:T(8,128)} %get-tuple-element.310.q_ref.k_ref.v_ref, ...), custom_call_target="tpu_custom_call" | custom-call | flops 11000000512 | bytes 11000000 | tf_op jit(solution)/shard_map/attend/pallas_call | solution.py:1008
  101.2 7.1 %enter.1 = (bf16[768,1024]{1,0:T(8,128)(2,1)}, f32[768,768]{1,0:T(8,128)}, f32[192,1024]{1,0:T(8,128)}) custom-call(bf16[768,48]{1,0:T(8,128)(2,1)} %get-tuple-element.322.feat_ref.refs_7_, bf16[48,1024]{1,0:T(8,128)(2,1)} %bitcast.205, bf16[768,16]{1,0:T(8,128)(2,1)} %get-tuple-element.323.hot_ref.refs_4_, ...), custom_call_target="tpu_custom_call" | custom-call | flops 5000000000 | bytes 5000000 | tf_op jit(solution)/shard_map/enter/pallas_call | solution.py:300
  112.0 11.0 %attend.3 = (bf16[768,256]{1,0:T(8,128)(2,1)}, f32[2,2,768]{2,1,0:T(2,128)}, bf16[384,1024]{1,0:T(8,128)(2,1)}, bf16[384,1024]{1,0:T(8,128)(2,1)}) custom-call(f32[768,768]{1,0:T(8,128)} %get-tuple-element.330.q_ref.k_ref.v_ref, f32[768,768]{1,0:T(8,128)} %get-tuple-element.330.q_ref.k_ref.v_ref, f32[768,768]{1,0:T(8,128)} %get-tuple-element.330.q_ref.k_ref.v_ref, ...), custom_call_target="tpu_custom_call" | custom-call | flops 11000000512 | bytes 11000000 | tf_op jit(solution)/shard_map/attend/pallas_call | solution.py:1008
  130.2 10.0 %collective-permute-done.21.c_ref = bf16[192,1024]{1,0:T(8,128)(2,1)S(1)} collective-permute-done((bf16[192,1024]{1,0:T(8,128)(2,1)S(1)}, bf16[192,1024]{1,0:T(8,128)(2,1)S(1)}, u32[]{:S(2)}, u32[]{:S(2)}) %collective-permute-start.21) | collective-permute-done | bytes 393248 | tf_op jit(solution)/shard_map/ppermute | solution.py:66
  150.1 9.9 %feed.2 = (bf16[768,1024]{1,0:T(8,128)(2,1)}, bf16[768,1024]{1,0:T(8,128)(2,1)}, f32[768,1024]{1,0:T(8,128)}, bf16[384,1024]{1,0:T(8,128)(2,1)}, bf16[384,1024]{1,0:T(8,128)(2,1)}) custom-call(bf16[192,1024]{1,0:T(8,128)(2,1)} %get-tuple-element.339.a_ref, bf16[192,1024]{1,0:T(8,128)(2,1)} %copy-done.70, bf16[192,1024]{1,0:T(8,128)(2,1)} %copy-done.69, ...), custom_call_target="tpu_custom_call" | custom-call | flops 5000000000 | bytes 5000000 | tf_op jit(solution)/shard_map/feed/pallas_call | solution.py:493
  166.5 9.4 %feed.3 = (bf16[768,1024]{1,0:T(8,128)(2,1)}, bf16[768,1024]{1,0:T(8,128)(2,1)}, f32[768,1024]{1,0:T(8,128)}, bf16[384,1024]{1,0:T(8,128)(2,1)}, bf16[384,1024]{1,0:T(8,128)(2,1)}) custom-call(bf16[192,1024]{1,0:T(8,128)(2,1)} %get-tuple-element.354.a_ref, bf16[192,1024]{1,0:T(8,128)(2,1)} %copy-done.72, bf16[192,1024]{1,0:T(8,128)(2,1)} %copy-done.73, ...), custom_call_target="tpu_custom_call" | custom-call | flops 5000000000 | bytes 5000000 | tf_op jit(solution)/shard_map/feed/pallas_call | solution.py:493
  184.0 8.0 %collective-permute-done.31.c_ref = bf16[192,1024]{1,0:T(8,128)(2,1)S(1)} collective-permute-done((bf16[192,1024]{1,0:T(8,128)(2,1)S(1)}, bf16[192,1024]{1,0:T(8,128)(2,1)S(1)}, u32[]{:S(2)}, u32[]{:S(2)}) %collective-permute-start.31) | collective-permute-done | bytes 393248 | tf_op jit(solution)/shard_map/ppermute | solution.py:66
  202.7 6.0 %head.2 = (bf16[768,1024]{1,0:T(8,128)(2,1)}, f32[768,1024]{1,0:T(8,128)}, f32[8,768]{1,0:T(8,128)}) custom-call(bf16[192,1024]{1,0:T(8,128)(2,1)} %get-tuple-element.363.a_ref, bf16[192,1024]{1,0:T(8,128)(2,1)} %copy-done.79, bf16[192,1024]{1,0:T(8,128)(2,1)} %copy-done.76, bf16[192,1024]{1,0:T(8,128)(2,1)} %copy-done.90, ...), custom_call_target="tpu_custom_call" | custom-call | flops 6000000000 | bytes 6000000 | tf_op jit(solution)/shard_map/head/pallas_call | solution.py:549
  216.6 5.9 %head.3 = (bf16[768,1024]{1,0:T(8,128)(2,1)}, f32[768,1024]{1,0:T(8,128)}, f32[8,768]{1,0:T(8,128)}) custom-call(bf16[192,1024]{1,0:T(8,128)(2,1)} %get-tuple-element.377.a_ref, bf16[192,1024]{1,0:T(8,128)(2,1)} %copy-done.77, bf16[192,1024]{1,0:T(8,128)(2,1)} %copy-done.80, bf16[192,1024]{1,0:T(8,128)(2,1)} %copy-done.87, ...), custom_call_target="tpu_custom_call" | custom-call | flops 6000000000 | bytes 6000000 | tf_op jit(solution)/shard_map/head/pallas_call | solution.py:549
  226.7 6.3 %head_back.2 = (bf16[768,1024]{1,0:T(8,128)(2,1)}, bf16[384,1024]{1,0:T(8,128)(2,1)}, bf16[384,1024]{1,0:T(8,128)(2,1)}) custom-call(f32[768,1024]{1,0:T(8,128)} %get-tuple-element.373.logit_ref, bf16[4,2,256,512]{3,2,1,0:T(8,128)(2,1)} %bitcast.223, f32[768,128]{1,0:T(8,128)} %get-tuple-element.311.col_ref.code_ref, f32[1,1024]{1,0:T(1,128)} %fusion.15.column_ref, ...), custom_call_target="tpu_custom_call" | custom-call | flops 5000000000 | bytes 5000000 | tf_op jit(solution)/shard_map/head_back/pallas_call | solution.py:610
  237.2 17.1 %head_back.3 = (bf16[768,1024]{1,0:T(8,128)(2,1)}, bf16[384,1024]{1,0:T(8,128)(2,1)}, bf16[384,1024]{1,0:T(8,128)(2,1)}) custom-call(f32[768,1024]{1,0:T(8,128)} %get-tuple-element.391.logit_ref, bf16[4,2,256,512]{3,2,1,0:T(8,128)(2,1)} %bitcast.224, f32[768,128]{1,0:T(8,128)} %get-tuple-element.331.col_ref.code_ref, f32[1,1024]{1,0:T(1,128)} %fusion.15.column_ref, ...), custom_call_target="tpu_custom_call" | custom-call | flops 5000000000 | bytes 5000000 | tf_op jit(solution)/shard_map/head_back/pallas_call | solution.py:610
  260.2 7.0 %head_grad.1 = bf16[4,2,256,512]{3,2,1,0:T(8,128)(2,1)} custom-call(bf16[768,1024]{1,0:T(8,128)(2,1)} %get-tuple-element.406.a_ref, bf16[768,1024]{1,0:T(8,128)(2,1)} %get-tuple-element.407.b_ref, bf16[768,1024]{1,0:T(8,128)(2,1)} %get-tuple-element.408.c_ref, bf16[768,1024]{1,0:T(8,128)(2,1)} %get-tuple-element.409.d_ref), custom_call_target="tpu_custom_call" | custom-call | flops 6000000000 | bytes 6000000 | tf_op jit(solution)/shard_map/head_grad/pallas_call | solution.py:660
  275.5 5.4 collective-permute-done.49.b_ref
  283.3 9.1 %feed_back.2 = (bf16[768,1024]{1,0:T(8,128)(2,1)}, bf16[768,1024]{1,0:T(8,128)(2,1)}, bf16[384,1024]{1,0:T(8,128)(2,1)}, bf16[384,1024]{1,0:T(8,128)(2,1)}) custom-call(bf16[192,1024]{1,0:T(8,128)(2,1)} %get-tuple-element.403.a_ref, bf16[192,1024]{1,0:T(8,128)(2,1)} %copy-done.83, bf16[192,1024]{1,0:T(8,128)(2,1)} %copy-done.68, ...), custom_call_target="tpu_custom_call" | custom-call | flops 7000000000 | bytes 7000000 | tf_op jit(solution)/shard_map/feed_back/pallas_call | solution.py:522
  298.7 8.8 %feed_back.3 = (bf16[768,1024]{1,0:T(8,128)(2,1)}, bf16[768,1024]{1,0:T(8,128)(2,1)}, bf16[384,1024]{1,0:T(8,128)(2,1)}, bf16[384,1024]{1,0:T(8,128)(2,1)}) custom-call(bf16[192,1024]{1,0:T(8,128)(2,1)} %get-tuple-element.423.a_ref, bf16[192,1024]{1,0:T(8,128)(2,1)} %copy-done.74, bf16[192,1024]{1,0:T(8,128)(2,1)} %copy-done.78, ...), custom_call_target="tpu_custom_call" | custom-call | flops 7000000000 | bytes 7000000 | tf_op jit(solution)/shard_map/feed_back/pallas_call | solution.py:522
  308.9 4.3 back.8
  315.3 12.6 %feed_grad.1 = bf16[4,2,256,1024]{3,2,1,0:T(8,128)(2,1)} custom-call(bf16[768,1024]{1,0:T(8,128)(2,1)} %get-tuple-element.438.a_ref, bf16[768,1024]{1,0:T(8,128)(2,1)} %get-tuple-element.439.b_ref, bf16[768,1024]{1,0:T(8,128)(2,1)} %get-tuple-element.440.c_ref, bf16[768,1024]{1,0:T(8,128)(2,1)} %get-tuple-element.441.d_ref, ...), custom_call_target="tpu_custom_call" | custom-call | flops 12000000000 | bytes 12000000 | tf_op jit(solution)/shard_map/feed_grad/pallas_call | solution.py:686
  334.5 6.2 %collective-permute-done.59.pb_ref = bf16[192,1024]{1,0:T(8,128)(2,1)S(1)} collective-permute-done((bf16[192,1024]{1,0:T(8,128)(2,1)S(1)}, bf16[192,1024]{1,0:T(8,128)(2,1)S(1)}, u32[]{:S(2)}, u32[]{:S(2)}) %collective-permute-start.59) | collective-permute-done | bytes 393248 | tf_op jit(solution)/shard_map/ppermute | solution.py:66
  345.5 20.8 %attend_back.2 = (bf16[768,1024]{1,0:T(8,128)(2,1)}, bf16[768,768]{1,0:T(8,128)(2,1)}, f32[2,1,128]{2,1,0:T(1,128)}, bf16[384,1024]{1,0:T(8,128)(2,1)}, bf16[384,1024]{1,0:T(8,128)(2,1)}) custom-call(f32[768,768]{1,0:T(8,128)} %get-tuple-element.310.q_ref.k_ref.v_ref, f32[768,768]{1,0:T(8,128)} %get-tuple-element.310.q_ref.k_ref.v_ref, ...), custom_call_target="tpu_custom_call" | custom-call | flops 16000000000 | bytes 16000000 | tf_op jit(solution)/shard_map/attend_back/pallas_call | solution.py:1131
  372.9 7.9 %reduce-scatter.6.cloned.1.call-done = bf16[512,1024]{1,0:T(8,128)(2,1)} async-done(((bf16[2048,1024]{1,0:T(8,128)(2,1)}), bf16[512,1024]{1,0:T(8,128)(2,1)}) %reduce-scatter.6.cloned.1.call-update) | async-done | bytes 1048592 | tf_op jit(solution)/shard_map/reduce_scatter | solution.py:1379
  385.9 20.6 %attend_back.3 = (bf16[768,1024]{1,0:T(8,128)(2,1)}, bf16[768,768]{1,0:T(8,128)(2,1)}, f32[2,1,128]{2,1,0:T(1,128)}, bf16[384,1024]{1,0:T(8,128)(2,1)}, bf16[384,1024]{1,0:T(8,128)(2,1)}) custom-call(f32[768,768]{1,0:T(8,128)} %get-tuple-element.330.q_ref.k_ref.v_ref, f32[768,768]{1,0:T(8,128)} %get-tuple-element.330.q_ref.k_ref.v_ref, ...), custom_call_target="tpu_custom_call" | custom-call | flops 16000000000 | bytes 16000000 | tf_op jit(solution)/shard_map/attend_back/pallas_call | solution.py:1131
  417.5 10.3 %first_grad.1 = bf16[4,2,256,512]{3,2,1,0:T(8,128)(2,1)} custom-call(bf16[768,1024]{1,0:T(8,128)(2,1)} %get-tuple-element.473.a_ref, bf16[768,1024]{1,0:T(8,128)(2,1)} %get-tuple-element.474.b_ref, bf16[768,768]{1,0:T(8,128)(2,1)} %get-tuple-element.477.c_ref, bf16[768,768]{1,0:T(8,128)(2,1)} %get-tuple-element.478.d_ref, ...), custom_call_target="tpu_custom_call" | custom-call | flops 6000000000 | bytes 6000000 | tf_op jit(solution)/shard_map/first_grad/pallas_call | solution.py:712
  444.9 4.8 all-to-all-done
  450.3 15.4 %reduce-scatter.8.cloned.1.call-done = bf16[512,512]{1,0:T(8,128)(2,1)} async-done(((bf16[2048,512]{1,0:T(8,128)(2,1)}), bf16[512,512]{1,0:T(8,128)(2,1)}) %reduce-scatter.8.cloned.1.call-update) | async-done | bytes 524304 | tf_op jit(solution)/shard_map/reduce_scatter | solution.py:1379
  490.5 4.7 collective-permute-done.79
  513.3 5.9 %column_stats.1 = (f32[2,12416]{1,0:T(2,128)}, f32[8,128]{1,0:T(8,128)}) custom-call(s32[1]{0:T(128)} %bitcast.at_ref, f32[5,128]{1,0:T(8,128)} %fusion.20.row_ref, f32[1,128]{1,0:T(1,128)} %slice.422.old_ref, f32[1,128]{1,0:T(1,128)} %get-tuple-element.528.tail_ref, f32[1,1]{1,0:T(1,128)} %bitcast.74.tables_ref, f32[1,128]{1,0:T(1,128)} %fusion.25.scale_ref, ...), custom_call_target="tpu_custom_call" | custom-call | flops 5000000000 | bytes 5000000 | tf_op jit(solution)/shard_map/column_stats/pallas_call | solution.py:799
  546.1 12.3 %renew.1 = (f32[3,128,256]{2,1,0:T(8,128)}, f32[256,128]{1,0:T(8,128)}, f32[128,1024]{1,0:T(8,128)}, f32[1024,128]{1,0:T(8,128)}, f32[128,1024]{1,0:T(8,128)}, /...) custom-call(f32[1,128]{1,0:T(1,128)} %slice.476.line_ref, ...), custom_call_target="tpu_custom_call" | custom-call | flops 8000000000 | bytes 8000000 | tf_op jit(solution)/shard_map/renew/pallas_call | solution.py:924
  (564 shorter events, 253.9 us)
Async XLA Ops:
  7.2 142.9 %all-gather.4.cloned.1.call-start = ((), (), s32[]{:S(2)}) async-start(), calls=%async_computation.4 | async-start | bytes 5242880 | tf_op jit(solution)/shard_map/all_gather | solution.py:1248
  13.6 37.8 %collective-permute-start.3 = (f32[2,4,768]{2,1,0:T(4,128)S(1)}, f32[2,4,768]{2,1,0:T(4,128)S(1)}, u32[]{:S(2)}, u32[]{:S(2)}) collective-permute-start(f32[2,4,768]{2,1,0:T(4,128)S(1)} %add_convert_fusion.11.mine_ref), channel_id=1, source_target_pairs={{0,4},{4,0},{1,5},{5,1},{2,6},{6,2},{3,7},{7,3},{8,12},{12,8},{9,1... | collective-permute-start | bytes 73736 | tf_op jit(solution)/shard_map/ppermute | solution.py:62
  14.6 36.8 %collective-permute-start.4 = (bf16[2,768,32]{2,1,0:T(8,128)(2,1)}, bf16[2,768,32]{2,1,0:T(8,128)(2,1)}, u32[]{:S(2)}, u32[]{:S(2)}) collective-permute-start(bf16[2,768,32]{2,1,0:T(8,128)(2,1)} %copy.71.vq_ref), channel_id=1, source_target_pairs={{0,4},{4,0},{1,5},{5,1},{2,6},{6,2},{3,7},{7,3},{8,12},{12,8},{9,1... | collective-permute-start | bytes 294920 | tf_op jit(solution)/shard_map/ppermute | solution.py:62
  18.0 16.2 %collective-permute-start.1 = (bf16[4,256,128]{2,1,0:T(8,128)(2,1)S(1)}, bf16[4,256,128]{2,1,0:T(8,128)(2,1)S(1)}, u32[]{:S(2)}, u32[]{:S(2)}) collective-permute-start(bf16[4,256,128]{2,1,0:T(8,128)(2,1)S(1)} %maximum_select_fusion.7), channel_id=1, source_target_pairs={{0,2},{2,0},{1,3},{3,1},{4,6},{6,4},{5,7},{7,5},{8,10},{10,8},{9,1... | collective-permute-start | bytes 786440 | tf_op jit(solution)/shard_map/ppermute | solution.py:70
  42.4 16.5 %collective-permute-start.5 = (bf16[2,4,256,128]{3,2,1,0:T(8,128)(2,1)}, bf16[2,4,256,128]{3,2,1,0:T(8,128)(2,1)}, u32[]{:S(2)}, u32[]{:S(2)}) collective-permute-start(bf16[2,4,256,128]{3,2,1,0:T(8,128)(2,1)} %maximum_select_fusion.2.a_ref), channel_id=1, source_target_pairs={{0,8},{8,0},{16,24},{24,16},{1,9},{9,1},{17,25},{25,17},{2,10},{10... | collective-permute-start | bytes 1572872 | tf_op jit(solution)/shard_map/ppermute | solution.py:78
  44.0 25.6 %collective-permute-start.6 = (bf16[2,4,256,128]{3,2,1,0:T(8,128)(2,1)}, bf16[2,4,256,128]{3,2,1,0:T(8,128)(2,1)}, u32[]{:S(2)}, u32[]{:S(2)}) collective-permute-start(bf16[2,4,256,128]{3,2,1,0:T(8,128)(2,1)} %maximum_select_fusion.2.a_ref), channel_id=1, source_target_pairs={{0,16},{8,24},{16,0},{24,8},{1,17},{9,25},{17,1},{25,9},{2,18},{10... | collective-permute-start | bytes 1572872 | tf_op jit(solution)/shard_map/ppermute | solution.py:78
  46.6 24.6 %collective-permute-start.7 = (bf16[2,4,256,128]{3,2,1,0:T(8,128)(2,1)}, bf16[2,4,256,128]{3,2,1,0:T(8,128)(2,1)}, u32[]{:S(2)}, u32[]{:S(2)}) collective-permute-start(bf16[2,4,256,128]{3,2,1,0:T(8,128)(2,1)} %maximum_select_fusion.2.a_ref), channel_id=1, source_target_pairs={{0,24},{8,16},{16,8},{24,0},{1,25},{9,17},{17,9},{25,1},{2,26},{10... | collective-permute-start | bytes 1572872 | tf_op jit(solution)/shard_map/ppermute | solution.py:78
  51.4 26.0 %collective-permute-start.10 = (bf16[256,1024]{1,0:T(8,128)(2,1)}, bf16[256,1024]{1,0:T(8,128)(2,1)S(1)}, u32[]{:S(2)}, u32[]{:S(2)}) collective-permute-start(bf16[256,1024]{1,0:T(8,128)(2,1)} %get-tuple-element.541), channel_id=1, source_target_pairs={{0,2},{2,0},{1,3},{3,1},{4,6},{6,4},{5,7},{7,5},{8,10},{10,8},{9,1... | collective-permute-start | bytes 1572872 | tf_op jit(solution)/shard_map/ppermute | solution.py:70
  51.5 25.9 %collective-permute-start.11 = (f32[2]{0:T(128)S(1)}, f32[2]{0:T(128)S(1)}, u32[]{:S(2)}, u32[]{:S(2)}) collective-permute-start(f32[2]{0:T(128)S(1)} %broadcast_select_fusion.13), channel_id=1, source_target_pairs={{0,2},{2,0},{1,3},{3,1},{4,6},{6,4},{5,7},{7,5},{8,10},{10,8},{9,1... | collective-permute-start | bytes 32 | tf_op jit(solution)/shard_map/ppermute | solution.py:70
  58.9 19.6 %collective-permute-start.12 = (f32[8,4096]{1,0:T(8,128)S(1)}, f32[8,4096]{1,0:T(8,128)S(1)}, u32[]{:S(2)}, u32[]{:S(2)}) collective-permute-start(f32[8,4096]{1,0:T(8,128)S(1)} %get-tuple-element.542), channel_id=1, source_target_pairs={{0,8},{8,0},{16,24},{24,16},{1,9},{9,1},{17,25},{25,17},{2,10},{10... | collective-permute-start | bytes 393224 | tf_op jit(solution)/shard_map/ppermute | solution.py:78
  81.1 102.9 %all-gather.6.cloned.1.call-start = ((), (), s32[]{:S(2)}) async-start(), calls=%async_computation.5 | async-start | bytes 2621440 | tf_op jit(solution)/shard_map/all_gather | solution.py:1248
  81.4 19.7 %collective-permute-start.17 = (bf16[256,512]{1,0:T(8,128)(2,1)S(1)}, bf16[256,512]{1,0:T(8,128)(2,1)S(1)}, u32[]{:S(2)}, u32[]{:S(2)}) collective-permute-start(bf16[256,512]{1,0:T(8,128)(2,1)S(1)} %maximum_select_fusion.12), channel_id=1, source_target_pairs={{0,2},{2,0},{1,3},{3,1},{4,6},{6,4},{5,7},{7,5},{8,10},{10,8},{9,1... | collective-permute-start | bytes 786440 | tf_op jit(solution)/shard_map/ppermute | solution.py:70
  109.6 13.5 %collective-permute-start.19 = (bf16[192,1024]{1,0:T(8,128)(2,1)S(1)}, bf16[192,1024]{1,0:T(8,128)(2,1)S(1)}, u32[]{:S(2)}, u32[]{:S(2)}) collective-permute-start(bf16[192,1024]{1,0:T(8,128)(2,1)S(1)} %add_convert_fusion.9), channel_id=1, source_target_pairs={{0,1},{1,0},{2,3},{3,2},{4,5},{5,4},{6,7},{7,6},{8,9},{9,8},{10,11... | collective-permute-start | bytes 1179656 | tf_op jit(solution)/shard_map/ppermute | solution.py:66
  128.5 19.2 %collective-permute-start.23 = (bf16[192,1024]{1,0:T(8,128)(2,1)}, bf16[192,1024]{1,0:T(8,128)(2,1)S(1)}, u32[]{:S(2)}, u32[]{:S(2)}) collective-permute-start(bf16[192,1024]{1,0:T(8,128)(2,1)} %get-tuple-element.339.a_ref), channel_id=1, source_target_pairs={{0,1},{1,0},{2,3},{3,2},{4,5},{5,4},{6,7},{7,6},{8,9},{9,8},{10,11... | collective-permute-start | bytes 1179656 | tf_op jit(solution)/shard_map/ppermute | solution.py:66
  148.6 159.5 %reduce-scatter.4.cloned.1.call-start = ((), (), s32[]{:S(2)}) async-start(), calls=%async_computation.6 | async-start | bytes 2621440 | tf_op jit(solution)/shard_map/reduce_scatter | solution.py:1379
  181.4 18.7 %collective-permute-start.33 = (bf16[192,1024]{1,0:T(8,128)(2,1)}, bf16[192,1024]{1,0:T(8,128)(2,1)S(1)}, u32[]{:S(2)}, u32[]{:S(2)}) collective-permute-start(bf16[192,1024]{1,0:T(8,128)(2,1)} %get-tuple-element.363.a_ref), channel_id=1, source_target_pairs={{0,1},{1,0},{2,3},{3,2},{4,5},{5,4},{6,7},{7,6},{8,9},{9,8},{10,11... | collective-permute-start | bytes 1179656 | tf_op jit(solution)/shard_map/ppermute | solution.py:66
  236.1 18.2 %collective-permute-start.45 = (bf16[192,1024]{1,0:T(8,128)(2,1)S(1)}, bf16[192,1024]{1,0:T(8,128)(2,1)S(1)}, u32[]{:S(2)}, u32[]{:S(2)}) collective-permute-start(bf16[192,1024]{1,0:T(8,128)(2,1)S(1)} %add_convert_fusion.5), channel_id=1, source_target_pairs={{0,1},{1,0},{2,3},{3,2},{4,5},{5,4},{6,7},{7,6},{8,9},{9,8},{10,11... | collective-permute-start | bytes 1179656 | tf_op jit(solution)/shard_map/ppermute | solution.py:66
  270.5 110.2 %reduce-scatter.6.cloned.1.call-start = ((), (), s32[]{:S(2)}) async-start(), calls=%async_computation.7 | async-start | bytes 5242880 | tf_op jit(solution)/shard_map/reduce_scatter | solution.py:1379
  314.3 13.6 %collective-permute-start.57 = (bf16[192,1024]{1,0:T(8,128)(2,1)S(1)}, bf16[192,1024]{1,0:T(8,128)(2,1)S(1)}, u32[]{:S(2)}, u32[]{:S(2)}) collective-permute-start(bf16[192,1024]{1,0:T(8,128)(2,1)S(1)} %add_convert_fusion.2), channel_id=1, source_target_pairs={{0,1},{1,0},{2,3},{3,2},{4,5},{5,4},{6,7},{7,6},{8,9},{9,8},{10,11... | collective-permute-start | bytes 1179656 | tf_op jit(solution)/shard_map/ppermute | solution.py:66
  315.3 12.6 %collective-permute-start.58 = (bf16[192,1024]{1,0:T(8,128)(2,1)}, bf16[192,1024]{1,0:T(8,128)(2,1)S(1)}, u32[]{:S(2)}, u32[]{:S(2)}) collective-permute-start(bf16[192,1024]{1,0:T(8,128)(2,1)} %get-tuple-element.435.pa_ref), channel_id=1, source_target_pairs={{0,4},{4,0},{1,5},{5,1},{2,6},{6,2},{3,7},{7,3},{8,12},{12,8},{9,1... | collective-permute-start | bytes 1179656 | tf_op jit(solution)/shard_map/ppermute | solution.py:62
  328.7 136.9 %reduce-scatter.8.cloned.1.call-start = ((), (), s32[]{:S(2)}) async-start(), calls=%async_computation.8 | async-start | bytes 2621440 | tf_op jit(solution)/shard_map/reduce_scatter | solution.py:1379
  342.0 24.3 %collective-permute-start.63 = (bf16[256,512]{1,0:T(8,128)(2,1)S(1)}, bf16[256,512]{1,0:T(8,128)(2,1)S(1)}, u32[]{:S(2)}, u32[]{:S(2)}) collective-permute-start(bf16[256,512]{1,0:T(8,128)(2,1)S(1)} %select_bitcast_fusion.2), channel_id=1, source_target_pairs={{0,2},{2,0},{1,3},{3,1},{4,6},{6,4},{5,7},{7,5},{8,10},{10,8},{9,1... | collective-permute-start | bytes 786440 | tf_op jit(solution)/shard_map/ppermute | solution.py:70
  343.8 22.5 %collective-permute-start.61 = (bf16[192,1024]{1,0:T(8,128)(2,1)}, bf16[192,1024]{1,0:T(8,128)(2,1)S(1)}, u32[]{:S(2)}, u32[]{:S(2)}) collective-permute-start(bf16[192,1024]{1,0:T(8,128)(2,1)} %get-tuple-element.461.pa_ref), channel_id=1, source_target_pairs={{0,1},{1,0},{2,3},{3,2},{4,5},{5,4},{6,7},{7,6},{8,9},{9,8},{10,11... | collective-permute-start | bytes 1179656 | tf_op jit(solution)/shard_map/ppermute | solution.py:66
  344.7 21.6 %collective-permute-start.62 = (bf16[192,1024]{1,0:T(8,128)(2,1)}, bf16[192,1024]{1,0:T(8,128)(2,1)}, u32[]{:S(2)}, u32[]{:S(2)}) collective-permute-start(bf16[192,1024]{1,0:T(8,128)(2,1)} %get-tuple-element.461.pa_ref), channel_id=1, source_target_pairs={{0,4},{4,0},{1,5},{5,1},{2,6},{6,2},{3,7},{7,3},{8,12},{12,8},{9,1... | collective-permute-start | bytes 1179656 | tf_op jit(solution)/shard_map/ppermute | solution.py:62
  370.0 15.2 %collective-permute-start.65 = (bf16[192,1024]{1,0:T(8,128)(2,1)}, bf16[192,1024]{1,0:T(8,128)(2,1)S(1)}, u32[]{:S(2)}, u32[]{:S(2)}) collective-permute-start(bf16[192,1024]{1,0:T(8,128)(2,1)} %copy-done.64), channel_id=1, source_target_pairs={{0,4},{4,0},{1,5},{5,1},{2,6},{6,2},{3,7},{7,3},{8,12},{12,8},{9,1... | collective-permute-start | bytes 1179656 | tf_op jit(solution)/shard_map/ppermute | solution.py:62
  371.7 36.1 %collective-permute-start.66 = (bf16[192,1024]{1,0:T(8,128)(2,1)S(1)}, bf16[192,1024]{1,0:T(8,128)(2,1)}, u32[]{:S(2)}, u32[]{:S(2)}) collective-permute-start(bf16[192,1024]{1,0:T(8,128)(2,1)S(1)} %add_convert_fusion.1), channel_id=1, source_target_pairs={{0,1},{1,0},{2,3},{3,2},{4,5},{5,4},{6,7},{7,6},{8,9},{9,8},{10,11... | collective-permute-start | bytes 1179656 | tf_op jit(solution)/shard_map/ppermute | solution.py:66
  382.8 26.1 %collective-permute-start.67 = (bf16[256,1024]{1,0:T(8,128)(2,1)}, bf16[256,1024]{1,0:T(8,128)(2,1)}, u32[]{:S(2)}, u32[]{:S(2)}) collective-permute-start(bf16[256,1024]{1,0:T(8,128)(2,1)} %broadcast_select_fusion), channel_id=1, source_target_pairs={{0,2},{2,0},{1,3},{3,1},{4,6},{6,4},{5,7},{7,5},{8,10},{10,8},{9,1... | collective-permute-start | bytes 1572872 | tf_op jit(solution)/shard_map/ppermute | solution.py:70
  449.7 27.0 %collective-permute-start.77 = (f32[48,128]{1,0:T(8,128)S(1)}, f32[48,128]{1,0:T(8,128)S(1)}, u32[]{:S(2)}, u32[]{:S(2)}) collective-permute-start(f32[48,128]{1,0:T(8,128)S(1)} %reduce_sum.28), channel_id=1, source_target_pairs={{0,1},{1,0},{2,3},{3,2},{4,5},{5,4},{6,7},{7,6},{8,9},{9,8},{10,11... | collective-permute-start | bytes 73736 | tf_op jit(solution)/shard_map/ppermute | solution.py:66
  476.1 19.3 %collective-permute-start.82 = (f32[128,512]{1,0:T(8,128)S(1)}, f32[128,512]{1,0:T(8,128)S(1)}, u32[]{:S(2)}, u32[]{:S(2)}) collective-permute-start(f32[128,512]{1,0:T(8,128)S(1)} %get-tuple-element.533), channel_id=1, source_target_pairs={{0,4},{4,0},{1,5},{5,1},{2,6},{6,2},{3,7},{7,3},{8,12},{12,8},{9,1... | collective-permute-start | bytes 786440 | tf_op jit(solution)/shard_map/ppermute | solution.py:62
  479.2 17.1 %collective-permute-start.87 = (f32[1,128]{1,0:T(1,128)S(1)}, f32[1,128]{1,0:T(1,128)S(1)}, u32[]{:S(2)}, u32[]{:S(2)}) collective-permute-start(f32[1,128]{1,0:T(1,128)S(1)} %fusion.26), channel_id=1, source_target_pairs={{0,2},{2,0},{1,3},{3,1},{4,6},{6,4},{5,7},{7,5},{8,10},{10,8},{9,1... | collective-permute-start | bytes 1544 | tf_op jit(solution)/shard_map/ppermute | solution.py:70
  479.7 16.6 %collective-permute-start.85 = (f32[1,128]{1,0:T(1,128)S(1)}, f32[1,128]{1,0:T(1,128)S(1)}, u32[]{:S(2)}, u32[]{:S(2)}) collective-permute-start(f32[1,128]{1,0:T(1,128)S(1)} %copy-done.60), channel_id=1, source_target_pairs={{0,1},{1,0},{2,3},{3,2},{4,5},{5,4},{6,7},{7,6},{8,9},{9,8},{10,11... | collective-permute-start | bytes 1544 | tf_op jit(solution)/shard_map/ppermute | solution.py:66
  481.7 13.4 %collective-permute-start.79 = (bf16[256,512]{1,0:T(8,128)(2,1)S(1)}, bf16[256,512]{1,0:T(8,128)(2,1)S(1)}, u32[]{:S(2)}, u32[]{:S(2)}) collective-permute-start(bf16[256,512]{1,0:T(8,128)(2,1)S(1)} %select_bitcast_fusion.1), channel_id=1, source_target_pairs={{0,2},{2,0},{1,3},{3,1},{4,6},{6,4},{5,7},{7,5},{8,10},{10,8},{9,1... | collective-permute-start | bytes 786440 | tf_op jit(solution)/shard_map/ppermute | solution.py:70
  (173 other events, 1194.9 us)
Sparse Core Ops, SparseCore 0:
  81.2 51.5 all-gather.3
  148.7 35.2 all-gather.5
  270.6 34.9 reduce-scatter.3
  328.1 52.5 reduce-scatter.5
  428.3 37.2 reduce-scatter.7
